TPU v7x, 32 devices: a whole 2x2x4 slice. The times are simulated.
32 devices in a mesh: dp: 8 (over z, x), tensor: 4 (over y, core).
Axes of the slice: x: 2, y: 2, z: 4, core: 2. Of those that a mesh axis runs over, the one named last changes fastest.
Arguments:
- tokens: bfloat16 [16384, 512], P(('dp', 'tensor')), may hold values from -6 to 6
- segment_ids: int32 [16384], P('dp'), may hold values from 0 to 63, never falling along the last dimension, each value on 1 to 8192 neighbouring positions
- query_weight: float32 [512, 512], P('dp', 'tensor'), may hold values from -0.25 to 0.25
- key_weight: float32 [512, 512], P('dp', 'tensor'), may hold values from -0.25 to 0.25
- value_weight: float32 [512, 512], P('dp', 'tensor'), may hold values from -0.25 to 0.25
- output_weight: float32 [512, 512], P('tensor', 'dp'), may hold values from -2.4 to 2.4
- inner_weight: float32 [512, 2048], P('dp', 'tensor'), may hold values from -0.25 to 0.25
- outer_weight: float32 [2048, 512], P('tensor', 'dp'), may hold values from -0.125 to 0.125
- inner_bias: float32 [2048], replicated, may hold values from -3 to 3
- first_gain: float32 [512], replicated, may hold values from 0.1 to 1.9
- first_shift: float32 [512], replicated, may hold values from -3 to 3
- second_gain: float32 [512], replicated, may hold values from 0.1 to 1.9
- second_shift: float32 [512], replicated, may hold values from -3 to 3
- mixer_bias: float32 [512], replicated, may hold values from -3 to 3
- outer_bias: float32 [512], replicated, may hold values from -3 to 3
- grad_out: bfloat16 [16384, 512], P(('dp', 'tensor')), may hold values from -6 to 6
Outputs:
- layer_out: bfloat16 [16384, 512], P(('dp', 'tensor'))
- grad_tokens: bfloat16 [16384, 512], P(('dp', 'tensor'))
- grad_query: float32 [512, 512], P('dp', 'tensor')
- grad_key: float32 [512, 512], P('dp', 'tensor')
- grad_value: float32 [512, 512], P('dp', 'tensor')
- grad_output: float32 [512, 512], P('tensor', 'dp')
- grad_inner: float32 [512, 2048], P('dp', 'tensor')
- grad_outer: float32 [2048, 512], P('tensor', 'dp')
- grad_inner_bias: float32 [2048], replicated
- grad_first_gain: float32 [512], replicated
- grad_first_shift: float32 [512], replicated
- grad_second_gain: float32 [512], replicated
- grad_second_shift: float32 [512], replicated
- grad_mixer_bias: float32 [512], replicated
- grad_outer_bias: float32 [512], replicated
Inputs may be any that keep to these rules, and one draw needn't show every extreme that they name: `segment_ids`: segment ids never fall along the sequence; a document holds 1 to 8192 consecutive tokens, and one holds exactly 8192.
All inputs are finite; a program needn't handle non-finite values.
Results may differ from a plain program's by a relative error of at most 0.015.
Values may be sent and summed in bfloat16 or wider, within the bound.
A program may use at most 128 MiB of HBM per device.

v0:
```python
import jax
import jax.numpy as jnp
from jax import lax
from jax.sharding import PartitionSpec as P

HEAD = 64


EPSILON = 1e-05
HIGHEST = lax.Precision.HIGHEST


def prefix(value, axis, join, neutral, backward):
    count, mine = (lax.axis_size(axis), lax.axis_index(axis))
    pieces = jax.tree.map(lambda part: lax.all_gather(part, axis), value)
    if backward:
        pieces = jax.tree.map(lambda part: part[::-1], pieces)
        mine = count - 1 - mine
    so_far = jax.tree.map(
        lambda part, zero: jnp.full_like(part, 0) + jnp.asarray(zero, part.dtype), value, neutral
    )

    def turn(position, so_far):
        longer = join(so_far, jax.tree.map(lambda part: part[position], pieces))
        return jax.tree.map(lambda new, old: jnp.where(position < mine, new, old), longer, so_far)

    return lax.fori_loop(0, count - 1, turn, so_far)


def layer_norm(values, gain, shift):
    center = values - jnp.mean(values, axis=-1, keepdims=True)
    spread = jnp.mean(center * center, axis=-1, keepdims=True)
    return center * lax.rsqrt(spread + EPSILON) * gain + shift


def feature(values):
    return jax.nn.elu(values) + 1.0


def gelu_exact(values):
    return jax.nn.gelu(values, approximate=False)


def chain_link(earlier, later):
    early_state, early_total, early_key = earlier
    late_state, late_total, late_key = later
    empty = late_key < 0
    joined = early_key == late_key
    merged_state = jnp.where(
        empty[..., None, None],
        early_state,
        late_state + jnp.where(joined[..., None, None], early_state, 0.0),
    )
    merged_total = jnp.where(
        empty[..., None], early_total, late_total + jnp.where(joined[..., None], early_total, 0.0)
    )
    merged_key = jnp.where(empty, early_key, late_key)
    return (merged_state, merged_total, merged_key)


def chain_step(carry, element):
    return (chain_link(carry, element), carry)


def empty_chain(local_heads):
    return (
        jnp.zeros((local_heads, HEAD, HEAD), jnp.float32),
        jnp.zeros((local_heads, HEAD), jnp.float32),
        jnp.full((1,), -1, jnp.int32),
    )


def causal_mask(block_segs):
    block_size = block_segs.shape[0]
    later_row = lax.broadcasted_iota(jnp.int32, (block_size, block_size), 0)
    earlier_col = lax.broadcasted_iota(jnp.int32, (block_size, block_size), 1)
    return (later_row >= earlier_col) & (block_segs[:, None] == block_segs[None, :])


def block_forward(pieces):
    queries, keys_part, values_part, block_segs, enter_state, enter_total, enter_key = pieces
    scores = jnp.einsum("thd,shd->hts", queries, keys_part, preferred_element_type=jnp.float32)
    weights = jnp.where(causal_mask(block_segs)[None], scores, 0.0)
    query_wide = queries.astype(jnp.float32)
    carried = (block_segs == enter_key[0]).astype(jnp.float32)
    numerator = jnp.einsum(
        "hts,she->the", weights, values_part.astype(jnp.float32), precision=HIGHEST
    )
    numerator = numerator + carried[:, None, None] * jnp.einsum(
        "thd,hde->the", query_wide, enter_state, precision=HIGHEST
    )
    denominator = jnp.sum(weights, axis=-1).T + carried[:, None] * jnp.einsum(
        "thd,hd->th", query_wide, enter_total, precision=HIGHEST
    )
    return (numerator, denominator)


def block_backward(pieces):
    (
        queries,
        keys_part,
        values_part,
        block_segs,
        numer_grad,
        denom_grad,
        enter_state,
        enter_total,
        enter_key,
    ) = pieces
    allowed = causal_mask(block_segs)[None]
    scores = jnp.einsum("thd,shd->hts", queries, keys_part, preferred_element_type=jnp.float32)
    weights = jnp.where(allowed, scores, 0.0)
    query_wide = queries.astype(jnp.float32)
    key_wide = keys_part.astype(jnp.float32)
    value_wide = values_part.astype(jnp.float32)
    score_grad = (
        jnp.einsum("the,she->hts", numer_grad, value_wide, precision=HIGHEST)
        + denom_grad.T[:, :, None]
    )
    score_grad = jnp.where(allowed, score_grad, 0.0)
    carried = (block_segs == enter_key[0]).astype(jnp.float32)
    carried_part = (
        jnp.einsum("hde,the->thd", enter_state, numer_grad, precision=HIGHEST)
        + denom_grad[:, :, None] * enter_total[None]
    )
    query_grad = (
        jnp.einsum("hts,shd->thd", score_grad, key_wide, precision=HIGHEST)
        + carried[:, None, None] * carried_part
    )
    key_grad = jnp.einsum("hts,thd->shd", score_grad, query_wide, precision=HIGHEST)
    value_grad = jnp.einsum("hts,the->she", weights, numer_grad, precision=HIGHEST)
    carried_queries = query_wide * carried[:, None, None]
    state_grad = jnp.einsum("thd,the->hde", carried_queries, numer_grad, precision=HIGHEST)
    total_grad = jnp.einsum("thd,th->hd", carried_queries, denom_grad, precision=HIGHEST)
    return (query_grad, key_grad, value_grad, state_grad, total_grad)


def mix_forward(query_raw, key_raw, value_raw, segment_ids, carry_in):
    total_rows, width = query_raw.shape
    local_heads = width // HEAD
    block_rows = min(1024, total_rows)
    block_count = total_rows // block_rows
    block_shape = (block_count, block_rows, local_heads, HEAD)
    queries = feature(query_raw).astype(jnp.bfloat16).reshape(block_shape)
    keys_all = feature(key_raw).astype(jnp.bfloat16).reshape(block_shape)
    values_all = value_raw.astype(jnp.bfloat16).reshape(block_shape)
    block_segs = segment_ids.reshape(block_count, block_rows)
    last_ids = block_segs[:, -1:]
    tail = (block_segs == last_ids).astype(jnp.bfloat16)[:, :, None, None]
    tail_keys = keys_all * tail
    block_state = jnp.einsum(
        "nthd,nthe->nhde", tail_keys, values_all, preferred_element_type=jnp.float32
    )
    block_total = jnp.sum(tail_keys.astype(jnp.float32), axis=1)
    identity = empty_chain(local_heads)
    local_total, local_prefix = lax.scan(chain_step, identity, (block_state, block_total, last_ids))
    incoming = carry_in(local_total, identity)
    entering = chain_link(incoming, local_prefix)
    numerator, denominator = lax.map(
        block_forward, (queries, keys_all, values_all, block_segs) + entering
    )
    mixed = numerator / denominator[..., None]
    return (
        mixed.reshape(total_rows, width),
        denominator,
        entering,
        (queries, keys_all, values_all, block_segs),
    )


def mix_backward(mixed_grad, mixed, denominator, entering, saved, query_raw, key_raw, carry_back):
    queries, keys_all, values_all, block_segs = saved
    local_heads = queries.shape[2]
    total_rows, width = query_raw.shape
    grad_blocks = mixed_grad.reshape(queries.shape)
    mixed_blocks = mixed.reshape(queries.shape)
    numer_grad = grad_blocks / denominator[..., None]
    denom_grad = -jnp.sum(grad_blocks * mixed_blocks, axis=-1) / denominator
    query_part, key_inner, value_inner, state_grads, total_grads = lax.map(
        block_backward,
        (queries, keys_all, values_all, block_segs, numer_grad, denom_grad) + entering,
    )
    first_ids = block_segs[:, :1]
    identity = empty_chain(local_heads)
    local_total, local_suffix = lax.scan(
        chain_step, identity, (state_grads, total_grads, first_ids), reverse=True
    )
    from_right = carry_back(local_total, identity)
    leaving = chain_link(from_right, local_suffix)
    last_ids = block_segs[:, -1:]
    matching = leaving[2] == last_ids
    leave_state = jnp.where(matching[..., None, None], leaving[0], 0.0)
    leave_total = jnp.where(matching[..., None], leaving[1], 0.0)
    tail = (block_segs == last_ids).astype(jnp.float32)[:, :, None, None]
    keys_wide = keys_all.astype(jnp.float32)
    values_wide = values_all.astype(jnp.float32)
    key_part = key_inner + tail * (
        jnp.einsum("nhde,nthe->nthd", leave_state, values_wide, precision=HIGHEST)
        + leave_total[:, None]
    )
    value_part = value_inner + tail * jnp.einsum(
        "nhde,nthd->nthe", leave_state, keys_wide, precision=HIGHEST
    )
    _, query_back = jax.vjp(feature, query_raw)
    (query_grad,) = query_back(query_part.reshape(total_rows, width))
    _, key_back = jax.vjp(feature, key_raw)
    (key_grad,) = key_back(key_part.reshape(total_rows, width))
    return (
        query_grad.astype(jnp.bfloat16),
        key_grad.astype(jnp.bfloat16),
        value_part.reshape(total_rows, width).astype(jnp.bfloat16),
    )


def local(
    tokens,
    segment_ids,
    query_weight,
    key_weight,
    value_weight,
    output_weight,
    inner_weight,
    outer_weight,
    inner_bias,
    first_gain,
    first_shift,
    second_gain,
    second_shift,
    mixer_bias,
    outer_bias,
    grad_out,
):
    w_query, w_key, w_value, w_inner, w_output, w_outer = (
        lax.all_gather(query_weight.astype(jnp.bfloat16), "dp", axis=0, tiled=True),
        lax.all_gather(key_weight.astype(jnp.bfloat16), "dp", axis=0, tiled=True),
        lax.all_gather(value_weight.astype(jnp.bfloat16), "dp", axis=0, tiled=True),
        lax.all_gather(inner_weight.astype(jnp.bfloat16), "dp", axis=0, tiled=True),
        lax.all_gather(output_weight.astype(jnp.bfloat16), "dp", axis=1, tiled=True),
        lax.all_gather(outer_weight.astype(jnp.bfloat16), "dp", axis=1, tiled=True),
    )
    own_input = tokens.astype(jnp.float32)
    first_low = layer_norm(own_input, first_gain, first_shift).astype(jnp.bfloat16)

    def heads_forward(local_total, identity):
        return prefix(local_total, "dp", chain_link, identity, False)

    def heads_backward(local_total, identity):
        return prefix(local_total, "dp", chain_link, identity, True)

    normed = lax.all_gather(first_low, "tensor", axis=0, tiled=True)
    query_raw = jnp.dot(normed, w_query, preferred_element_type=jnp.float32)
    key_raw = jnp.dot(normed, w_key, preferred_element_type=jnp.float32)
    value_raw = jnp.dot(normed, w_value, preferred_element_type=jnp.float32)
    mixed, denominator, entering, saved = mix_forward(
        query_raw, key_raw, value_raw, segment_ids, heads_forward
    )
    mixed_low = mixed.astype(jnp.bfloat16)
    residual = (
        own_input
        + lax.psum_scatter(
            jnp.dot(mixed_low, w_output, preferred_element_type=jnp.float32),
            "tensor",
            scatter_dimension=0,
            tiled=True,
        )
        + mixer_bias
    )
    second_low = layer_norm(residual, second_gain, second_shift).astype(jnp.bfloat16)
    cotangent = grad_out.astype(jnp.float32)
    w_inner_full, w_outer_full = (
        lax.all_gather(w_inner, "tensor", axis=1, tiled=True),
        lax.all_gather(w_outer, "tensor", axis=0, tiled=True),
    )
    hidden = jnp.dot(second_low, w_inner_full, preferred_element_type=jnp.float32) + inner_bias
    activated = gelu_exact(hidden).astype(jnp.bfloat16)
    layer_out = (
        residual + jnp.dot(activated, w_outer_full, preferred_element_type=jnp.float32) + outer_bias
    ).astype(jnp.bfloat16)
    _, gelu_back = jax.vjp(gelu_exact, hidden)
    (hidden_grad,) = gelu_back(
        jnp.einsum("td,fd->tf", grad_out, w_outer_full, preferred_element_type=jnp.float32)
    )
    hidden_low = hidden_grad.astype(jnp.bfloat16)
    inner_full = jnp.einsum("td,tf->df", second_low, hidden_low, preferred_element_type=jnp.float32)
    outer_full = jnp.einsum("tf,td->fd", activated, grad_out, preferred_element_type=jnp.float32)
    inner_w_grad, outer_w_grad = (
        lax.psum_scatter(
            inner_full.astype(jnp.bfloat16), "tensor", scatter_dimension=1, tiled=True
        ).astype(jnp.float32),
        lax.psum_scatter(
            outer_full.astype(jnp.bfloat16), "tensor", scatter_dimension=0, tiled=True
        ).astype(jnp.float32),
    )
    inner_bias_grad = jnp.sum(hidden_low.astype(jnp.float32), axis=0)
    second_grad = jnp.einsum(
        "tf,df->td", hidden_low, w_inner_full, preferred_element_type=jnp.float32
    )
    _, second_back = jax.vjp(layer_norm, residual, second_gain, second_shift)
    residual_norm, second_gain_grad, second_shift_grad = second_back(second_grad)
    residual_grad = cotangent + residual_norm
    branch_low = residual_grad.astype(jnp.bfloat16)
    mixer_bias_grad = jnp.sum(branch_low.astype(jnp.float32), axis=0)
    branch_all = lax.all_gather(branch_low, "tensor", axis=0, tiled=True)
    output_w_grad = jnp.einsum(
        "tk,td->kd", mixed_low, branch_all, preferred_element_type=jnp.float32
    )
    mixed_grad = jnp.einsum("td,kd->tk", branch_all, w_output, preferred_element_type=jnp.float32)
    query_grad, key_grad, value_grad = mix_backward(
        mixed_grad, mixed, denominator, entering, saved, query_raw, key_raw, heads_backward
    )
    query_w_grad = jnp.einsum("td,tk->dk", normed, query_grad, preferred_element_type=jnp.float32)
    key_w_grad = jnp.einsum("td,tk->dk", normed, key_grad, preferred_element_type=jnp.float32)
    value_w_grad = jnp.einsum("td,tk->dk", normed, value_grad, preferred_element_type=jnp.float32)
    summed = jnp.einsum("tk,dk->td", query_grad, w_query, preferred_element_type=jnp.float32)
    summed = summed + jnp.einsum("tk,dk->td", key_grad, w_key, preferred_element_type=jnp.float32)
    first_grad = lax.psum_scatter(
        summed + jnp.einsum("tk,dk->td", value_grad, w_value, preferred_element_type=jnp.float32),
        "tensor",
        scatter_dimension=0,
        tiled=True,
    )
    _, first_back = jax.vjp(layer_norm, own_input, first_gain, first_shift)
    input_norm, first_gain_grad, first_shift_grad = first_back(first_grad)
    grad_tokens = (residual_grad + input_norm).astype(jnp.bfloat16)
    outer_bias_grad = jnp.sum(cotangent, axis=0)
    summed_weights = (
        lax.psum_scatter(
            query_w_grad.astype(jnp.bfloat16), "dp", scatter_dimension=0, tiled=True
        ).astype(jnp.float32),
        lax.psum_scatter(
            key_w_grad.astype(jnp.bfloat16), "dp", scatter_dimension=0, tiled=True
        ).astype(jnp.float32),
        lax.psum_scatter(
            value_w_grad.astype(jnp.bfloat16), "dp", scatter_dimension=0, tiled=True
        ).astype(jnp.float32),
        lax.psum_scatter(
            inner_w_grad.astype(jnp.bfloat16), "dp", scatter_dimension=0, tiled=True
        ).astype(jnp.float32),
        lax.psum_scatter(
            output_w_grad.astype(jnp.bfloat16), "dp", scatter_dimension=1, tiled=True
        ).astype(jnp.float32),
        lax.psum_scatter(
            outer_w_grad.astype(jnp.bfloat16), "dp", scatter_dimension=1, tiled=True
        ).astype(jnp.float32),
    )
    summed_small = lax.psum(
        (
            first_gain_grad,
            first_shift_grad,
            second_gain_grad,
            second_shift_grad,
            mixer_bias_grad,
            outer_bias_grad,
            inner_bias_grad,
        ),
        ("dp", "tensor"),
    )
    return (
        layer_out,
        grad_tokens,
        summed_weights[0],
        summed_weights[1],
        summed_weights[2],
        summed_weights[4],
        summed_weights[3],
        summed_weights[5],
        summed_small[6],
        summed_small[0],
        summed_small[1],
        summed_small[2],
        summed_small[3],
        summed_small[4],
        summed_small[5],
    )


def solution(mesh):
    in_specs = (
        P(("dp", "tensor"), None),
        P("dp"),
        P("dp", "tensor"),
        P("dp", "tensor"),
        P("dp", "tensor"),
        P("tensor", "dp"),
        P("dp", "tensor"),
        P("tensor", "dp"),
        P(),
        P(),
        P(),
        P(),
        P(),
        P(),
        P(),
        P(("dp", "tensor"), None),
    )
    out_specs = (
        P(("dp", "tensor"), None),
        P(("dp", "tensor"), None),
        P("dp", "tensor"),
        P("dp", "tensor"),
        P("dp", "tensor"),
        P("tensor", "dp"),
        P("dp", "tensor"),
        P("tensor", "dp"),
        P(),
        P(),
        P(),
        P(),
        P(),
        P(),
        P(),
    )
    return jax.shard_map(local, mesh=mesh, in_specs=in_specs, out_specs=out_specs, check_vma=False)
```

profile of v0, /device:TPU:0, one launch (start us, length us, event | category | flops | bytes accessed | tf_op | source)
XLA Modules:
  0.0 1093.1 jit_solution(823055790154026586)
XLA Ops:
  18.5 32.3 %all_gather.76 = bf16[128,512]{0,1:T(8,128)(2,1)S(1)} all-gather(bf16[128,64]{0,1:T(8,128)(2,1)S(1)} %convert_element_type.174), channel_id=1, replica_groups=mesh['dp'=8,'tensor'=4] {'dp'}, dimensions={1}, use_global_device_ids=true | all-gather | bytes 147456 | tf_op jit(solution)/shard_map/all_gather | solution.py:238
  50.8 30.5 %all_gather.67 = bf16[512,128]{1,0:T(8,128)(2,1)S(1)} all-gather(bf16[64,128]{1,0:T(8,128)(2,1)S(1)} %convert_element_type.164), channel_id=1, replica_groups=mesh['dp'=8,'tensor'=4] {'dp'}, dimensions={0}, use_global_device_ids=true | all-gather | bytes 147456 | tf_op jit(solution)/shard_map/all_gather | solution.py:236
  81.4 30.5 %all_gather.69 = bf16[512,128]{1,0:T(8,128)(2,1)S(1)} all-gather(bf16[64,128]{1,0:T(8,128)(2,1)S(1)} %convert_element_type.168), channel_id=1, replica_groups=mesh['dp'=8,'tensor'=4] {'dp'}, dimensions={0}, use_global_device_ids=true | all-gather | bytes 147456 | tf_op jit(solution)/shard_map/all_gather | solution.py:235
  111.9 32.3 %all_gather.68 = bf16[512,128]{1,0:T(8,128)(2,1)} all-gather(bf16[64,128]{1,0:T(8,128)(2,1)S(1)} %convert_element_type.166), channel_id=1, replica_groups=mesh['dp'=8,'tensor'=4] {'dp'}, dimensions={0}, use_global_device_ids=true | all-gather | bytes 147456 | tf_op jit(solution)/shard_map/all_gather | solution.py:234
  180.2 19.2 %all-gather.6 = f32[8,2,64]{2,1,0:T(2,128)} all-gather(f32[1,2,64]{2,1,0:T(2,128)S(1)} %bitcast.406), channel_id=4, replica_groups=mesh['dp'=8,'tensor'=4] {'dp'}, dimensions={0}, use_global_device_ids=true | all-gather | bytes 4608 | tf_op jit(solution)/shard_map/all_gather | solution.py:15
  199.4 33.7 %all-gather.1 = f32[16,64,64]{2,1,0:T(8,128)} all-gather(f32[2,64,64]{2,1,0:T(8,128)S(1)} %get-tuple-element.693), channel_id=3, replica_groups=mesh['dp'=8,'tensor'=4] {'dp'}, dimensions={0}, use_global_device_ids=true | all-gather | bytes 294912 | tf_op jit(solution)/shard_map/all_gather | solution.py:15
  233.1 33.3 %while.118 = (s32[]{:T(128)}, f32[2,64,64]{2,1,0:T(8,128)S(1)}, f32[2,64]{1,0:T(2,128)S(1)}, s32[1]{0:T(128)}, s32[]{:T(128)}, /*index=5*/s32[8,1]{0,1:T(1,128)}...) while((s32[]{:T(128)}, f32[2,64,64]{2,1,0:T(8,128)S(1)}, ...), condition=%wide.region_6.7_spmd.clone, body=%wide.region_5.6_spmd.clone.sunk | while | flops 41608 | bytes 100055 | solution.py:27
  274.2 37.9 %while.115 = (s32[]{:T(128)}, f32[2,1024,2,64]{1,0,3,2:T(2,128)}, f32[2,1024,2]{1,0,2:T(2,128)S(1)}, bf16[2,1024,2,64]{1,3,2,0:T(8,128)(2,1)}, s32[2,1024]{1,0:T...) while((s32[]{:T(128)}, f32[2,1024,2,64]{1,0,3,2:T(2,128)}, ...), condition=%wide.region_9.10_spmd, body=%wide.region_7.9_spmd.sunk | while | flops 1990987776 | bytes 27173056 | solution.py:159
  318.7 33.5 %all_gather.77 = bf16[512,512]{1,0:T(8,128)(2,1)} all-gather(bf16[64,512]{1,0:T(8,128)(2,1)S(1)} %convert_element_type.176), channel_id=1, replica_groups=mesh['dp'=8,'tensor'=4] {'dp'}, dimensions={0}, use_global_device_ids=true | all-gather | bytes 589824 | tf_op jit(solution)/shard_map/all_gather | solution.py:237
  352.3 33.2 %all_gather.79 = bf16[512,512]{0,1:T(8,128)(2,1)} all-gather(bf16[512,64]{0,1:T(8,128)(2,1)S(1)} %convert_element_type.178), channel_id=1, replica_groups=mesh['dp'=8,'tensor'=4] {'dp'}, dimensions={1}, use_global_device_ids=true | all-gather | bytes 589824 | tf_op jit(solution)/shard_map/all_gather | solution.py:239
  392.7 16.3 %all-gather.17.cloned.1.call-done = bf16[2048,512]{0,1:T(8,128)(2,1)} async-done(((bf16[512,512]{0,1:T(8,128)(2,1)}), bf16[2048,512]{0,1:T(8,128)(2,1)}) %all-gather.17.cloned.1.call-update) | async-done | bytes 2097168 | tf_op jit(solution)/shard_map/all_gather | solution.py:272
  409.0 14.0 %convert_reduce_fusion = (f32[2048]{0:T(1024)S(1)}, bf16[512,2048]{1,0:T(8,128)(2,1)S(1)}, f32[512,2048]{1,0:T(8,128)}) fusion(f32[512,2048]{1,0:T(8,128)} %fusion.148, f32[2048]{0:T(1024)S(1)} %copy-done.49, bf16[512,512]{1,0:T(8,128)(2,1)S(1)} %copy-done.19, bf16[2048,512]{0,1:T(8,128)(2,1)} %all-gather.17.cloned.1.call-done), kind=kOutput, calls=%fused_computation.141 | convolution fusion | flops 1152382976 | bytes 13123584 | tf_op jit(solution)/shard_map/td,fd->tf/dot_general | solution.py:281
  456.3 54.4 %while.116 = (s32[]{:T(128)}, f32[2,1024,2,64]{1,3,2,0:T(8,128)}, f32[2,1024,2,64]{1,3,2,0:T(8,128)}, f32[2,1024,2,64]{1,3,2,0:T(8,128)}, f32[2,2,64,64]{3,2,1,0...) while((s32[]{:T(128)}, f32[2,1024,2,64]{1,3,2,0:T(8,128)}, ...), condition=%wide.region_17.18_spmd, body=%wide.region_16.17_spmd.sunk | while | flops 6928467968 | bytes 79143800 | solution.py:179
  528.3 17.7 %all-gather.7 = f32[8,2,64]{2,1,0:T(2,128)S(1)} all-gather(f32[1,2,64]{2,1,0:T(2,128)S(1)} %bitcast.405), channel_id=7, replica_groups=mesh['dp'=8,'tensor'=4] {'dp'}, dimensions={0}, use_global_device_ids=true | all-gather | bytes 4608 | tf_op jit(solution)/shard_map/all_gather | solution.py:15
  546.1 31.4 %all-gather.4 = f32[16,64,64]{2,1,0:T(8,128)S(1)} all-gather(f32[2,64,64]{2,1,0:T(8,128)S(1)} %get-tuple-element.708), channel_id=6, replica_groups=mesh['dp'=8,'tensor'=4] {'dp'}, dimensions={0}, use_global_device_ids=true | all-gather | bytes 294912 | tf_op jit(solution)/shard_map/all_gather | solution.py:15
  577.5 18.3 %while.120 = (s32[]{:T(128)}, f32[2,64,64]{2,1,0:T(8,128)S(1)}, f32[2,64]{1,0:T(2,128)S(1)}, s32[1]{0:T(128)}, s32[]{:T(128)}, /*index=5*/s32[8,1]{0,1:T(1,128)S...) while((s32[]{:T(128)}, f32[2,64,64]{2,1,0:T(8,128)S(1)}, ...), condition=%wide.region_21.22_spmd.clone, body=%wide.region_20.21_spmd.clone.sunk | while | flops 41608 | bytes 100055 | solution.py:27
  638.4 36.1 %reduce-scatter.23.cloned.1.call-done = bf16[128,64]{0,1:T(8,128)(2,1)} async-done(((bf16[128,512]{0,1:T(8,128)(2,1)}), bf16[128,64]{0,1:T(8,128)(2,1)}) %reduce-scatter.23.cloned.1.call-update) | async-done | bytes 16400 | tf_op jit(solution)/shard_map/reduce_scatter | solution.py:339
  675.8 62.3 %reduce-scatter.21.cloned.1.call-done = bf16[64,128]{1,0:T(8,128)(2,1)} async-done(((bf16[512,128]{1,0:T(8,128)(2,1)}), bf16[64,128]{1,0:T(8,128)(2,1)}) %reduce-scatter.21.cloned.1.call-update) | async-done | bytes 16400 | tf_op jit(solution)/shard_map/reduce_scatter | solution.py:333
  739.4 62.1 %reduce-scatter.19.cloned.1.call-done = bf16[64,128]{1,0:T(8,128)(2,1)} async-done(((bf16[512,128]{1,0:T(8,128)(2,1)}), bf16[64,128]{1,0:T(8,128)(2,1)}) %reduce-scatter.19.cloned.1.call-update) | async-done | bytes 16400 | tf_op jit(solution)/shard_map/reduce_scatter | solution.py:330
  802.9 62.8 %reduce-scatter.17.cloned.1.call-done = bf16[64,128]{1,0:T(8,128)(2,1)} async-done(((bf16[512,128]{1,0:T(8,128)(2,1)}), bf16[64,128]{1,0:T(8,128)(2,1)}) %reduce-scatter.17.cloned.1.call-update) | async-done | bytes 16400 | tf_op jit(solution)/shard_map/reduce_scatter | solution.py:327
  867.0 63.2 %reduce-scatter.31.cloned.1.call-done = bf16[64,512]{1,0:T(8,128)(2,1)} async-done(((bf16[512,512]{1,0:T(8,128)(2,1)}), bf16[64,512]{1,0:T(8,128)(2,1)}) %reduce-scatter.31.cloned.1.call-update) | async-done | bytes 65552
  932.0 62.5 %reduce-scatter.27.cloned.1.call-done = bf16[64,512]{1,0:T(8,128)(2,1)} async-done(((bf16[512,512]{1,0:T(8,128)(2,1)}), bf16[64,512]{1,0:T(8,128)(2,1)}) %reduce-scatter.27.cloned.1.call-update) | async-done | bytes 65552 | tf_op jit(solution)/shard_map/reduce_scatter | solution.py:336
  995.9 44.7 %reduce-scatter.15.cloned.1.call-done = f32[512,512]{1,0:T(8,128)} async-done(((f32[2048,512]{1,0:T(8,128)}), f32[512,512]{1,0:T(8,128)}) %reduce-scatter.15.cloned.1.call-update) | async-done | bytes 1048592 | tf_op jit(solution)/shard_map/reduce_scatter | solution.py:316
  1046.6 39.8 %all-reduce.2 = (f32[2048]{0:T(1024)}, f32[512]{0:T(512)}, f32[512]{0:T(512)}, f32[512]{0:T(512)}, f32[512]{0:T(512)}, /*index=5*/f32[512]{0:T(512)}, f32[512]{0:T(512)}) all-reduce(f32[2048]{0:T(1024)S(1)} %get-tuple-element.1199, f32[512]{0:T(512)S(1)} %get-tuple-element.1058, ...), channel_id=1, replica_groups=mesh['dp'=8,'tensor'=4] {'dp','tensor'}, use_global_device_ids=true, to_apply=%region_34.35 | all-reduce | flops 5120 | bytes 40960 | tf_op jit(solution)/shard_map/psum | solution.py:346
  (405 shorter events, 296.4 us)
Async XLA Ops:
  7.2 137.0 %all-gather.13.cloned.1.call-start = ((), (), s32[]{:S(2)}) async-start(), calls=%async_computation.10 | async-start | bytes 2621440 | tf_op jit(solution)/shard_map/all_gather | solution.py:250
  8.4 135.8 %copy-start.37 = (f32[512]{0:T(512)}, f32[512]{0:T(512)S(1)}, u32[]{:S(2)}) copy-start(f32[512]{0:T(512)S(1)} %broadcast_multiply_fusion.2) | copy-start | bytes 6148
  9.8 134.4 %copy-start.43 = (f32[512]{0:T(512)}, f32[512]{0:T(512)S(1)}, u32[]{:S(2)}) copy-start(f32[512]{0:T(512)S(1)} %fusion.120) | copy-start | bytes 6148
  9.8 134.4 %copy-start.41 = (f32[512]{0:T(512)}, f32[512]{0:T(512)S(1)}, u32[]{:S(2)}) copy-start(f32[512]{0:T(512)S(1)} %fusion.142) | copy-start | bytes 6148
  11.9 373.8 %reduce-scatter.13.cloned.1.call-start = ((), (), s32[]{:S(2)}) async-start(), calls=%async_computation.11 | async-start | bytes 5242880 | tf_op jit(solution)/shard_map/reduce_scatter | solution.py:260
  318.6 68.9 %all-gather.15.cloned.1.call-start = ((), (), s32[]{:S(2)}) async-start(), calls=%async_computation.12 | async-start | bytes 2621440 | tf_op jit(solution)/shard_map/all_gather | solution.py:271
  352.2 56.7 %all-gather.17.cloned.1.call-start = ((), (), s32[]{:S(2)}) async-start(), calls=%async_computation.13 | async-start | bytes 2621440 | tf_op jit(solution)/shard_map/all_gather | solution.py:272
  385.5 64.3 %all-gather.19.cloned.1.call-start = ((), (), s32[]{:S(2)}) async-start(), calls=%async_computation.14 | async-start | bytes 2621440 | tf_op jit(solution)/shard_map/all_gather | solution.py:303
  427.0 198.5 %reduce-scatter.29.cloned.1.call-start = ((), (), s32[]{:S(2)}) async-start(), calls=%async_computation.22 | async-start | bytes 2621440 | tf_op jit(solution)/shard_map/reduce_scatter | solution.py:290
  440.4 187.3 %reduce-scatter.25.cloned.1.call-start = ((), (), s32[]{:S(2)}) async-start(), calls=%async_computation.20 | async-start | bytes 2621440 | tf_op jit(solution)/shard_map/reduce_scatter | solution.py:287
  516.8 157.7 %reduce-scatter.23.cloned.1.call-start = ((), (), s32[]{:S(2)}) async-start(), calls=%async_computation.19 | async-start | bytes 147456 | tf_op jit(solution)/shard_map/reduce_scatter | solution.py:339
  617.2 120.9 %reduce-scatter.21.cloned.1.call-start = ((), (), s32[]{:S(2)}) async-start(), calls=%async_computation.18 | async-start | bytes 147456 | tf_op jit(solution)/shard_map/reduce_scatter | solution.py:333
  618.7 182.9 %reduce-scatter.19.cloned.1.call-start = ((), (), s32[]{:S(2)}) async-start(), calls=%async_computation.17 | async-start | bytes 147456 | tf_op jit(solution)/shard_map/reduce_scatter | solution.py:330
  622.0 243.7 %reduce-scatter.17.cloned.1.call-start = ((), (), s32[]{:S(2)}) async-start(), calls=%async_computation.16 | async-start | bytes 147456 | tf_op jit(solution)/shard_map/reduce_scatter | solution.py:327
  625.4 304.8 %reduce-scatter.31.cloned.1.call-start = ((), (), s32[]{:S(2)}) async-start(), calls=%async_computation.23 | async-start | bytes 589824
  627.6 366.8 %reduce-scatter.27.cloned.1.call-start = ((), (), s32[]{:S(2)}) async-start(), calls=%async_computation.21 | async-start | bytes 589824 | tf_op jit(solution)/shard_map/reduce_scatter | solution.py:336
  628.4 412.3 %reduce-scatter.15.cloned.1.call-start = ((), (), s32[]{:S(2)}) async-start(), calls=%async_computation.15 | async-start | bytes 5242880 | tf_op jit(solution)/shard_map/reduce_scatter | solution.py:316
  634.0 406.6 %copy-start.6 = (bf16[512,512]{1,0:T(8,128)(2,1)S(1)}, bf16[512,512]{1,0:T(8,128)(2,1)}, u32[]{:S(2)}) copy-start(bf16[512,512]{1,0:T(8,128)(2,1)} %param.28) | copy-start | bytes 1572868
  634.0 406.6 %copy-start.38 = (f32[512]{0:T(512)S(1)}, f32[512]{0:T(512)}, u32[]{:S(2)}) copy-start(f32[512]{0:T(512)} %copy-done.37) | copy-start | bytes 6148
  634.0 406.6 %copy-start.40 = (f32[512]{0:T(512)S(1)}, f32[512]{0:T(512)}, u32[]{:S(2)}) copy-start(f32[512]{0:T(512)} %param.37) | copy-start | bytes 6148
  634.0 408.2 %copy-start.44 = (f32[512]{0:T(512)S(1)}, f32[512]{0:T(512)}, u32[]{:S(2)}) copy-start(f32[512]{0:T(512)} %copy-done.43) | copy-start | bytes 6148
  634.0 408.2 %copy-start.42 = (f32[512]{0:T(512)S(1)}, f32[512]{0:T(512)}, u32[]{:S(2)}) copy-start(f32[512]{0:T(512)} %copy-done.41) | copy-start | bytes 6148
  638.4 405.6 %copy-start.10 = (f32[512,512]{1,0:T(8,128)S(1)}, f32[512,512]{1,0:T(8,128)}, u32[]{:S(2)}) copy-start(f32[512,512]{1,0:T(8,128)} %copy-done.9) | copy-start | bytes 3145732
  638.4 405.6 %copy-start.20 = (bf16[512,512]{1,0:T(8,128)(2,1)S(1)}, bf16[512,512]{1,0:T(8,128)(2,1)}, u32[]{:S(2)}) copy-start(bf16[512,512]{1,0:T(8,128)(2,1)} %param.43) | copy-start | bytes 1572868
  (52 other events, 1121.0 us)
Sparse Core Ops, SparseCore 0:
  12.1 25.2 all-gather.12
  318.7 41.8 reduce-scatter.12
  362.2 22.5 all-gather.14
  386.3 22.5 all-gather.16
  427.1 22.5 all-gather.18
  452.3 31.4 reduce-scatter.28
  516.9 31.4 reduce-scatter.24
  617.3 57.1 reduce-scatter.22
  678.1 59.8 reduce-scatter.20
  741.6 59.8 reduce-scatter.18
  805.8 59.8 reduce-scatter.16
  869.3 60.9 reduce-scatter.30
  933.6 60.8 reduce-scatter.26
  997.0 43.6 reduce-scatter.14
where the time goes:
time: 1100 us; the launch traced here: 1090 us
  waiting for transfers between devices  420 us (38%)
  blocking collectives  357 us (32%)
  matrix products  121 us (11%)
  local copies, waits for them, and re-layouts  83.3 us (8%)
  other arithmetic  58.6 us (5%)
  loops' own time  36.7 us (3%)
  between operations  15.1 us (1%)
    all_gather x4, blocking collectives, prefix(): pieces = jax.tree.map(lambda part: lax.all_gather(part, axis), value)  102 us
    unnamed x15, waiting for transfers between devices  64.1 us
    reduce_scatter x1, waiting for transfers between devices, local(): lax.psum_scatter(query_w_grad.astype(jnp.bfloat16), 'dp', scatter_dimensi...  62.8 us
    reduce_scatter x1, waiting for transfers between devices, local(): lax.psum_scatter(inner_w_grad.astype(jnp.bfloat16), 'dp', scatter_dimensi...  62.5 us
    reduce_scatter x1, waiting for transfers between devices, local(): lax.psum_scatter(value_w_grad.astype(jnp.bfloat16), 'dp', scatter_dimensi...  62.3 us
    reduce_scatter x1, waiting for transfers between devices, local(): lax.psum_scatter(key_w_grad.astype(jnp.bfloat16), 'dp', scatter_dimension...  62.1 us
    reduce_scatter x1, waiting for transfers between devices, local(): lax.psum_scatter(summed + jnp.einsum('tk,dk->td', value_grad, w_value, pr...  44.7 us
    psum x1, blocking collectives, local(): lax.psum((first_gain_grad, first_shift_grad, second_gain_grad, second_shi...  39.8 us
  transfers between devices with their start and end apart: 14, of which 9 were waited for; matrix products, arithmetic and copies ran while one was open for 13% of the time, Pallas kernels for 0%

commit v1 on v0

v1 whole, which is shorter than its diff:
```python
import functools

import jax
import jax.numpy as jnp
from jax import lax
from jax.experimental import pallas as pl
from jax.experimental.pallas import tpu as pltpu
from jax.sharding import PartitionSpec as P

HEAD = 64
LANES = 128
EPSILON = 1e-05
MESH = pl.DeviceIdType.MESH
F32 = jnp.float32
BF16 = jnp.bfloat16
OUTER = 4
STATE_ROWS = HEAD + 8
VMEM_LIMIT = 56 << 20


def nn(a, b):
    return lax.dot_general(a, b, (((1,), (0,)), ((), ())), preferred_element_type=F32)


def nt(a, b):
    return lax.dot_general(a, b, (((1,), (1,)), ((), ())), preferred_element_type=F32)


def tn(a, b):
    return lax.dot_general(a, b, (((0,), (0,)), ((), ())), preferred_element_type=F32)


class Place:
    def __init__(self, dp_size, tensor_size):
        self.nd, self.nt = dp_size, tensor_size
        self.inner, self.ny = dp_size // OUTER, tensor_size // 2
        self.d, self.t = lax.axis_index("dp"), lax.axis_index("tensor")
        self.o, self.i = self.d // self.inner, self.d % self.inner
        self.y, self.c = self.t // 2, self.t % 2

    def at(self, do=0, di=0, dy=0, dc=0):
        o, i = (self.o + do) % OUTER, (self.i + di) % self.inner
        y, c = (self.y + dy) % self.ny, (self.c + dc) % 2
        return (o * self.inner + i, y * 2 + c)

    def outer_peers(self):
        return [(k, 0, 0, 0) for k in range(1, OUTER)]

    def plane_peers(self):
        return [
            (0, di, dy, 0) for di in range(self.inner) for dy in range(self.ny) if di or dy
        ]

    def group_peers(self):
        return [(0, 0, dy, dc) for dy in range(self.ny) for dc in range(2) if dy or dc]

    def dp_peers(self):
        return [(do, di, 0, 0) for do in range(OUTER) for di in range(self.inner) if do or di]

    def greet(self):
        peers = []
        for peer in (
            self.outer_peers()
            + self.plane_peers()
            + self.group_peers()
            + self.dp_peers()
        ):
            if peer not in peers:
                peers.append(peer)
        barrier = pltpu.get_barrier_semaphore()
        for peer in peers:
            pl.semaphore_signal(
                barrier, inc=1, device_id=self.at(*peer), device_id_type=MESH
            )
        pl.semaphore_wait(barrier, len(peers))


def remote(src, dst, send, recv, peer):
    return pltpu.make_async_remote_copy(
        src_ref=src,
        dst_ref=dst,
        send_sem=send,
        recv_sem=recv,
        device_id=peer,
        device_id_type=MESH,
    )


class Gather:
    def __init__(self, place, mine, held, send, got_outer, got_plane, got_core):
        self.p, self.mine, self.held = place, mine, held
        self.send, self.got_outer = send, got_outer
        self.got_plane, self.got_core = got_plane, got_core
        self.started, self.count = [], 0

    def _go(self, src, dst, recv, peer):
        copy = remote(src, dst, self.send.at[self.count], recv, peer)
        self.count += 1
        copy.start()
        self.started.append(copy)
        return copy

    def start(self):
        p = self.p
        place = self.held.at[p.t, p.o, p.i]
        self.to_outer = [
            self._go(self.mine, place, self.got_outer.at[k - 1], p.at(*peer))
            for k, peer in enumerate(p.outer_peers(), 1)
        ]
        self._spread(0, self.mine)

    def _spread(self, k, src):
        p = self.p
        o = (p.o + OUTER - k) % OUTER
        for j, peer in enumerate(p.plane_peers()):
            self._go(src, self.held.at[p.t, o, p.i], self.got_plane.at[j, k], p.at(*peer))
        self._go(src, self.held.at[p.t, o, p.i], self.got_core.at[p.y], p.at(dc=1))

    def outer_step(self):
        p = self.p
        for k in range(1, OUTER):
            o = (p.o + OUTER - k) % OUTER
            block = self.held.at[p.t, o, p.i]
            remote(block, block, self.send.at[0], self.got_outer.at[k - 1], p.at()).wait_recv()
            self._spread(k, block)

    def plane_step(self):
        p = self.p
        for k in range(OUTER):
            o = (p.o + OUTER - k) % OUTER
            for j, (_, di, dy, _) in enumerate(p.plane_peers()):
                i, y = (p.i + p.inner - di) % p.inner, (p.y + p.ny - dy) % p.ny
                block = self.held.at[y * 2 + p.c, o, i]
                remote(block, block, self.send.at[0], self.got_plane.at[j, k], p.at()).wait_recv()
                self._go(block, block, self.got_core.at[y], p.at(dc=1))

    def core_step(self):
        p = self.p
        for y in range(p.ny):
            block = self.held.at[y * 2 + 1 - p.c]
            remote(block, block, self.send.at[0], self.got_core.at[y], p.at()).wait_recv()

    def finish(self):
        for copy in self.started:
            copy.wait_send()

    @staticmethod
    def semaphores(nd, nt):
        plane = (nd // OUTER) * (nt // 2) - 1
        sends = (OUTER - 1) + OUTER * (plane + 1) + OUTER * plane
        return [
            pltpu.SemaphoreType.DMA((sends,)),
            pltpu.SemaphoreType.DMA((OUTER - 1,)),
            pltpu.SemaphoreType.DMA((plane, OUTER)),
            pltpu.SemaphoreType.DMA((nt // 2,)),
        ]


class Exchange:
    def __init__(self, place, firsts, lasts, back, own, near, far, made, entering, sems):
        self.p, self.back = place, back
        self.own, self.near, self.far = own, near, far
        self.made, self.entering = made, entering
        self.edge, self.inlet = (firsts, lasts) if back else (lasts, firsts)
        self.s_send, self.s_near, self.s_far, self.s_enter = sems
        self.started, self.count = [], 0

    def _go(self, src, dst, recv, peer):
        copy = remote(src, dst, self.s_send.at[self.count], recv, peer)
        self.count += 1
        copy.start()
        self.started.append(copy)

    def step_near(self):
        p = self.p
        for peer in p.group_peers():
            to = p.at(*peer)
            self._go(self.own.at[to[1]], self.near.at[p.t], self.s_near.at[p.t], to)
        self.near[p.t] = self.own[p.t]

    def step_far(self):
        p = self.p
        for _, _, dy, dc in p.group_peers():
            t = ((p.y + p.ny - dy) % p.ny) * 2 + (p.c + dc) % 2
            block = self.near.at[t]
            remote(block, block, self.s_send.at[0], self.s_near.at[t], p.at()).wait_recv()
        border = 0 if self.back else p.nt - 1
        ids = self.edge[border : border + 1, :]
        total = jnp.zeros((STATE_ROWS, LANES), F32)
        for j in range(p.nt):
            total = total + jnp.where(self.edge[j : j + 1, :] == ids, self.near[j], 0.0)
        rows = lax.broadcasted_iota(jnp.int32, (STATE_ROWS, LANES), 0)
        self.far[p.d] = jnp.where(rows > HEAD, jnp.broadcast_to(ids, rows.shape), total)
        for peer in p.dp_peers():
            self._go(self.far.at[p.d], self.far.at[p.d], self.s_far.at[p.d], p.at(*peer))

    def step_enter(self):
        p = self.p
        for do, di, _, _ in p.dp_peers():
            o, i = (p.o + OUTER - do) % OUTER, (p.i + p.inner - di) % p.inner
            d = o * p.inner + i
            block = self.far.at[d]
            remote(block, block, self.s_send.at[0], self.s_far.at[d], p.at()).wait_recv()
        for j in range(p.nt):
            inlet = self.inlet[j : j + 1, :]
            total = jnp.zeros((STATE_ROWS, LANES), F32)
            for d in range(p.nd):
                ids = self.far[d, HEAD + 1 : HEAD + 2, :]
                wanted = jnp.where(d > p.d if self.back else d < p.d, ids, -1.0)
                total = total + jnp.where(wanted == inlet, self.far[d], 0.0)
            for k in range(j + 1, p.nt) if self.back else range(j):
                total = total + jnp.where(self.edge[k : k + 1, :] == inlet, self.near[k], 0.0)
            self.made[j] = total
        for peer in p.group_peers():
            to = p.at(*peer)
            self._go(self.made.at[to[1]], self.entering.at[p.t], self.s_enter.at[p.t], to)
        self.entering[p.t] = self.made[p.t]

    def arrive(self):
        p = self.p
        for _, _, dy, dc in p.group_peers():
            t = ((p.y + p.ny - dy) % p.ny) * 2 + (p.c + dc) % 2
            block = self.entering.at[t]
            remote(block, block, self.s_send.at[0], self.s_enter.at[t], p.at()).wait_recv()

    def finish(self):
        for copy in self.started:
            copy.wait_send()

    @staticmethod
    def scratch(nd, nt):
        return [
            pltpu.VMEM((nt, STATE_ROWS, LANES), F32),
            pltpu.VMEM((nt, STATE_ROWS, LANES), F32),
            pltpu.VMEM((nd, STATE_ROWS, LANES), F32),
            pltpu.VMEM((nt, STATE_ROWS, LANES), F32),
        ]

    @staticmethod
    def semaphores(nd, nt):
        return [
            pltpu.SemaphoreType.DMA((2 * (nt - 1) + nd - 1,)),
            pltpu.SemaphoreType.DMA((nt,)),
            pltpu.SemaphoreType.DMA((nd,)),
            pltpu.SemaphoreType.DMA((nt,)),
        ]


def left_lanes(shape):
    return lax.broadcasted_iota(jnp.int32, shape, len(shape) - 1) < HEAD


def split_heads(block, fill):
    left = left_lanes(block.shape)
    other = jnp.full_like(block, fill)
    return jnp.where(left, block, other), jnp.where(left, other, block)


def feature(values):
    return jnp.where(values > 0.0, values + 1.0, jnp.exp(jnp.minimum(values, 0.0)))


def pack_state(product):
    left = left_lanes((HEAD, LANES))
    return jnp.where(left, product[:HEAD], product[HEAD:])


def wide_state(packed):
    left = left_lanes((HEAD, LANES))
    zero = jnp.zeros_like(packed)
    return jnp.concatenate([jnp.where(left, packed, zero), jnp.where(left, zero, packed)], axis=0)


def two_parts(values):
    high = values.astype(BF16)
    return high, (values - high.astype(F32)).astype(BF16)


def same_head():
    row = lax.broadcasted_iota(jnp.int32, (LANES, LANES), 0) < HEAD
    return row == left_lanes((LANES, LANES))


def make_mask(segc, segr, mask, rows):
    total = segc.shape[0]
    for start in range(0, total, rows):
        at = lax.broadcasted_iota(jnp.int32, (rows, total), 0) + start
        key = lax.broadcasted_iota(jnp.int32, (rows, total), 1)
        same = segc[start : start + rows, :] == segr[...]
        mask[start : start + rows, :] = jnp.where((at >= key) & same, 1.0, 0.0).astype(BF16)


def kernel_forward(
    nd, nt_,
    tokens, mine_a, mine_b, segc, segr, firsts, lasts, gain, shift,
    held_a, held_b, normed, fq, fk, vb, mixed, rden, entering,
    mask, num_s, den_s, own, near, far, made, *sems,
):
    p = Place(nd, nt_)
    rows_all = tokens.shape[0]
    ga = Gather(p, mine_a, held_a, *sems[0:4])
    gb = Gather(p, mine_b, held_b, *sems[4:8])
    ex = Exchange(p, firsts, lasts, False, own, near, far, made, entering, sems[8:12])
    p.greet()
    ga.start()
    gb.start()
    held_a[p.t, p.o, p.i] = mine_a[...]
    held_b[p.t, p.o, p.i] = mine_b[...]
    step = 128

    def norm(k, _):
        at = pl.ds(pl.multiple_of(k * step, step), step)
        x = tokens[at, :].astype(F32)
        center = x - jnp.mean(x, axis=-1, keepdims=True)
        spread = jnp.mean(center * center, axis=-1, keepdims=True)
        y = center * lax.rsqrt(spread + EPSILON) * gain[...] + shift[...]
        normed[at, :] = y.astype(BF16)
        return 0

    lax.fori_loop(0, rows_all // step, norm, 0)
    make_mask(segc, segr, mask, 128)
    ga.outer_step()
    ga.plane_step()
    gb.outer_step()
    ga.core_step()
    last = segr[:, rows_all - 1 : rows_all]
    tail = segc[...] == last
    depth = nd * mine_a.shape[0]

    def keys_values(g, _):
        w = held_a[g].reshape(depth, 3 * LANES)
        kv = nn(normed[...], w[:, LANES:])
        keys = feature(kv[:, :LANES]).astype(BF16)
        values = kv[:, LANES:].astype(BF16)
        fk[g] = keys
        vb[g] = values
        kept = jnp.where(tail, keys, jnp.zeros_like(keys))
        own[g, :HEAD, :] = pack_state(tn(kept, values))
        sums = jnp.sum(kept.astype(F32), axis=0, keepdims=True)
        own[g, HEAD:, :] = jnp.broadcast_to(sums, (STATE_ROWS - HEAD, LANES))
        return 0

    lax.fori_loop(0, nt_, keys_values, 0)
    ex.step_near()

    def queries(g, _):
        w = held_a[g].reshape(depth, 3 * LANES)
        fq[g] = feature(nn(normed[...], w[:, :LANES])).astype(BF16)
        return 0

    lax.fori_loop(0, nt_, queries, 0)
    ex.step_far()
    block = min(256, rows_all)

    def inside(g, _):
        values = split_heads(vb[g], 1.0)
        for start in range(0, rows_all, block):
            end = start + block
            now = mask[start:end, :end]
            query = split_heads(fq[g, start:end, :], 0.0)
            keys = fk[g, :end, :]
            parts = []
            for h in range(2):
                scores = nt(query[h], keys).astype(BF16) * now
                parts.append(nn(scores, values[h][:end]))
            left = left_lanes(parts[0].shape)
            num_s[g, start:end, :] = jnp.where(left, parts[0], parts[1])
            den_s[g, start:end, :] = pltpu.roll(
                jnp.where(left, parts[1], parts[0]), HEAD, 1
            )
        return 0

    lax.fori_loop(0, nt_ // 2, inside, 0)
    ex.step_enter()
    lax.fori_loop(nt_ // 2, nt_, inside, 0)
    gb.plane_step()
    ex.arrive()
    carried = segc[...] == segr[:, 0:1]

    def outside(g, _):
        state = entering[g]
        high, low = two_parts(wide_state(state[:HEAD]))
        sums = jnp.broadcast_to(jnp.transpose(state[HEAD:, :])[:, 0:1], (LANES, LANES))
        sum_high, sum_low = two_parts(jnp.where(same_head(), sums, 0.0))
        query = fq[g]
        query = jnp.where(carried, query, jnp.zeros_like(query))
        num = num_s[g] + (nn(query, high) + nn(query, low))
        den = den_s[g] + (nn(query, sum_high) + nn(query, sum_low))
        inverse = 1.0 / den
        rden[g] = inverse
        mixed[g] = num * inverse
        return 0

    lax.fori_loop(0, nt_, outside, 0)
    gb.core_step()
    ga.finish()
    gb.finish()
    ex.finish()


def forward_call(nd, nt_, tokens, mine_a, mine_b, segc, segr, firsts, lasts, gain, shift):
    rows = tokens.shape[0]
    ra, ca = mine_a.shape
    rb, cb = mine_b.shape
    inner = nd // OUTER
    vm = pl.BlockSpec(memory_space=pltpu.VMEM)
    group = (nt_, rows, LANES)
    outs = [
        jax.ShapeDtypeStruct((nt_, OUTER, inner, ra, ca), BF16),
        jax.ShapeDtypeStruct((nt_, OUTER, inner, rb, cb), BF16),
        jax.ShapeDtypeStruct(tokens.shape, BF16),
        jax.ShapeDtypeStruct(group, BF16),
        jax.ShapeDtypeStruct(group, BF16),
        jax.ShapeDtypeStruct(group, BF16),
        jax.ShapeDtypeStruct(group, F32),
        jax.ShapeDtypeStruct(group, F32),
        jax.ShapeDtypeStruct((nt_, STATE_ROWS, LANES), F32),
    ]
    return pl.pallas_call(
        functools.partial(kernel_forward, nd, nt_),
        out_shape=outs,
        in_specs=[vm] * 9,
        out_specs=[vm] * len(outs),
        scratch_shapes=[
            pltpu.VMEM((rows, rows), BF16),
            pltpu.VMEM(group, F32),
            pltpu.VMEM(group, F32),
        ]
        + Exchange.scratch(nd, nt_)
        + Gather.semaphores(nd, nt_)
        + Gather.semaphores(nd, nt_)
        + Exchange.semaphores(nd, nt_),
        compiler_params=pltpu.CompilerParams(
            collective_id=0, has_side_effects=True, vmem_limit_bytes=VMEM_LIMIT
        ),
        name="attention_forward",
    )(tokens, mine_a, mine_b, segc, segr, firsts, lasts, gain, shift)
def pad_lanes(block):
    spare = LANES - block.shape[1]
    return jnp.pad(block, ((0, 0), (0, spare))) if spare > 0 else block


def prepare(nd, nt_, tokens, segment_ids, wq, wk, wv, wo, w1, w2):
    rows = tokens.shape[0]
    t = lax.axis_index("tensor")
    mine_a = jnp.concatenate([pad_lanes(w.astype(BF16)) for w in (wq, wk, wv)], axis=1)
    mine_b = jnp.concatenate(
        [pad_lanes(wo.astype(BF16).T), w1.astype(BF16), w2.astype(BF16).T], axis=1
    )
    by_member = segment_ids.reshape(nt_, rows)
    own = lax.dynamic_slice(segment_ids, (t * rows,), (rows,))
    segc, segr = own.reshape(rows, 1), own.reshape(1, rows)
    firsts = jnp.broadcast_to(by_member[:, :1].astype(F32), (nt_, LANES))
    lasts = jnp.broadcast_to(by_member[:, -1:].astype(F32), (nt_, LANES))
    return mine_a, mine_b, segc, segr, firsts, lasts
def kernel_hidden(
    nd, nt_,
    tokens, mixed, held, cotangent, gain, shift, mixer_bias, outer_bias, inner_bias,
    out, dr, do, part, sums, inner_sums,
    res, unit, inv, h2, h2t, cot, dh2, act, dhid, dbt,
):
    rows_all, width = tokens.shape
    hidden = (held.shape[-1] - LANES) // 2
    step = 128

    def weights(g, start, size):
        return held[g, :, :, :, start : start + size].reshape(width, size)

    def enter(k, _):
        at = pl.ds(pl.multiple_of(k * step, step), step)
        r = tokens[at, :].astype(F32) + mixer_bias[...]
        for g in range(nt_):
            r = r + nt(mixed[g, at, :].astype(BF16), weights(g, 0, LANES))
        center = r - jnp.mean(r, axis=-1, keepdims=True)
        spread = jnp.mean(center * center, axis=-1, keepdims=True)
        scale = lax.rsqrt(spread + EPSILON)
        n = center * scale
        y = n * gain[...] + shift[...]
        res[at, :] = r + outer_bias[...]
        unit[at, :] = n
        inv[at, :] = scale
        h2[at, :] = y.astype(BF16)
        h2t[:, at] = jnp.transpose(y).astype(BF16)
        e = cotangent[at, :].astype(F32)
        cot[:, at] = jnp.transpose(e).astype(BF16)
        dh2[at, :] = jnp.zeros((step, width), F32)
        return 0

    lax.fori_loop(0, rows_all // step, enter, 0)
    block = min(256, rows_all)

    def feed(g, _):
        w1 = weights(g, LANES, hidden)
        w2t = weights(g, LANES + hidden, hidden)
        total = jnp.zeros((1, hidden), F32)
        for start in range(0, rows_all, block):
            end = start + block
            u = nn(h2[start:end, :], w1) + inner_bias[pl.ds(g, 1), :]
            below = 0.5 * (1.0 + lax.erf(u * 0.7071067811865476))
            slope = below + u * (jnp.exp(-0.5 * (u * u)) * 0.3989422804014327)
            a = (u * below).astype(BF16)
            du = (nn(cotangent[start:end, :], w2t) * slope).astype(BF16)
            act[start:end, :] = a
            dhid[start:end, :] = du
            total = total + jnp.sum(du.astype(F32), axis=0, keepdims=True)
            res[start:end, :] += nt(a, w2t)
            dh2[start:end, :] += nt(du, w1)
        inner_sums[pl.ds(g, 1), :] = total
        for o in range(OUTER):
            tall = width // OUTER
            lo, hi = o * tall, (o + 1) * tall
            shape = (held.shape[2], held.shape[3], hidden)
            part[g, o, :, :, LANES : LANES + hidden] = (
                nn(h2t[lo:hi, :], dhid[...]).astype(BF16).reshape(shape)
            )
            part[g, o, :, :, LANES + hidden :] = (
                nn(cot[lo:hi, :], act[...]).astype(BF16).reshape(shape)
            )
        return 0

    lax.fori_loop(0, nt_, feed, 0)
    sums[...] = jnp.zeros_like(sums)

    def leave(k, _):
        at = pl.ds(pl.multiple_of(k * step, step), step)
        out[at, :] = res[at, :].astype(BF16)
        n = unit[at, :]
        grad = dh2[at, :]
        e = cotangent[at, :].astype(F32)
        pushed = grad * gain[...]
        mean = jnp.mean(pushed, axis=-1, keepdims=True)
        along = jnp.mean(pushed * n, axis=-1, keepdims=True)
        back = e + (pushed - mean - n * along) * inv[at, :]
        dr[at, :] = back
        low = back.astype(BF16)
        wide = low.astype(F32)
        dbt[:, at] = jnp.transpose(wide).astype(BF16)
        for g in range(nt_):
            do[g, at, :] = nn(low, weights(g, 0, LANES))
        sums[2:3, :] += jnp.sum(grad * n, axis=0, keepdims=True)
        sums[3:4, :] += jnp.sum(grad, axis=0, keepdims=True)
        sums[4:5, :] += jnp.sum(wide, axis=0, keepdims=True)
        sums[5:6, :] += jnp.sum(e, axis=0, keepdims=True)
        return 0

    lax.fori_loop(0, rows_all // step, leave, 0)
    for g in range(nt_):
        shape = held.shape[1:4] + (LANES,)
        part[g, :, :, :, :LANES] = (
            nn(dbt[...], mixed[g].astype(BF16)).astype(BF16).reshape(shape)
        )


def hidden_call(nd, nt_, tokens, mixed, held, cotangent, gain, shift, mbias, obias, ibias):
    rows, width = tokens.shape
    hidden = (held.shape[-1] - LANES) // 2
    vm = pl.BlockSpec(memory_space=pltpu.VMEM)
    outs = [
        jax.ShapeDtypeStruct((rows, width), BF16),
        jax.ShapeDtypeStruct((rows, width), F32),
        jax.ShapeDtypeStruct(mixed.shape, F32),
        jax.ShapeDtypeStruct(held.shape, BF16),
        jax.ShapeDtypeStruct((8, width), F32),
        jax.ShapeDtypeStruct((nt_, hidden), F32),
    ]
    return pl.pallas_call(
        functools.partial(kernel_hidden, nd, nt_),
        out_shape=outs,
        in_specs=[vm] * 9,
        out_specs=[vm] * len(outs),
        scratch_shapes=[
            pltpu.VMEM((rows, width), F32),
            pltpu.VMEM((rows, width), F32),
            pltpu.VMEM((rows, 1), F32),
            pltpu.VMEM((rows, width), BF16),
            pltpu.VMEM((width, rows), BF16),
            pltpu.VMEM((width, rows), BF16),
            pltpu.VMEM((rows, width), F32),
            pltpu.VMEM((rows, hidden), BF16),
            pltpu.VMEM((rows, hidden), BF16),
            pltpu.VMEM((width, rows), BF16),
        ],
        compiler_params=pltpu.CompilerParams(vmem_limit_bytes=VMEM_LIMIT),
        name="hidden_layer",
    )(tokens, mixed, held, cotangent, gain, shift, mbias, obias, ibias)
class Scatter:
    def __init__(self, place, part, core, plane, own, outer, sems):
        self.p, self.part, self.core = place, part, core
        self.plane, self.own, self.outer = plane, own, outer
        self.send, self.got_core, self.got_plane, self.got_outer = sems
        self.started, self.count = [], 0

    def _go(self, src, dst, recv, peer):
        copy = remote(src, dst, self.send.at[self.count], recv, peer)
        self.count += 1
        copy.start()
        self.started.append(copy)

    def core_send(self, y):
        p = self.p
        self._go(self.part.at[y * 2 + 1 - p.c], self.core.at[y], self.got_core.at[y], p.at(dc=1))

    def core_sum(self, y):
        p = self.p
        block = self.core.at[y]
        remote(block, block, self.send.at[0], self.got_core.at[y], p.at()).wait_recv()

        def add(k, _):
            o, i = k // p.inner, k % p.inner
            mine = self.part[y * 2 + p.c, o, i].astype(F32)
            self.core[y, o, i] = (mine + self.core[y, o, i].astype(F32)).astype(BF16)
            return 0

        lax.fori_loop(0, OUTER * p.inner, add, 0)

    def plane_send(self):
        p = self.p
        for j, (_, di, dy, _) in enumerate(p.plane_peers()):
            i, y = (p.i + di) % p.inner, (p.y + dy) % p.ny
            self._go(
                self.core.at[y, :, i], self.plane.at[j], self.got_plane.at[j], p.at(0, di, dy, 0)
            )

    def plane_sum(self):
        p = self.p
        peers = len(p.plane_peers())
        for j in range(peers):
            block = self.plane.at[j]
            remote(block, block, self.send.at[0], self.got_plane.at[j], p.at()).wait_recv()
        for k in range(OUTER):
            o = (p.o + k) % OUTER
            total = self.core[p.y, o, p.i].astype(F32)
            for j in range(peers):
                total = total + self.plane[j, o].astype(F32)
            self.own[k] = total.astype(BF16)
            if k:
                self._go(
                    self.own.at[k], self.outer.at[k - 1], self.got_outer.at[k - 1], p.at(do=k)
                )

    def outer_sum(self, out):
        p = self.p
        total = self.own[0].astype(F32)
        for k in range(1, OUTER):
            block = self.outer.at[k - 1]
            remote(block, block, self.send.at[0], self.got_outer.at[k - 1], p.at()).wait_recv()
            total = total + self.outer[k - 1].astype(F32)
        out[...] = total

    def finish(self):
        for copy in self.started:
            copy.wait_send()

    @staticmethod
    def scratch(nd, nt_, rows, columns):
        inner, ny = nd // OUTER, nt_ // 2
        peers = inner * ny - 1
        return [
            pltpu.VMEM((ny, OUTER, inner, rows, columns), BF16),
            pltpu.VMEM((peers, OUTER, rows, columns), BF16),
            pltpu.VMEM((OUTER, rows, columns), BF16),
            pltpu.VMEM((OUTER - 1, rows, columns), BF16),
        ]

    @staticmethod
    def semaphores(nd, nt_):
        inner, ny = nd // OUTER, nt_ // 2
        peers = inner * ny - 1
        return [
            pltpu.SemaphoreType.DMA((ny + peers + OUTER - 1,)),
            pltpu.SemaphoreType.DMA((ny,)),
            pltpu.SemaphoreType.DMA((peers,)),
            pltpu.SemaphoreType.DMA((OUTER - 1,)),
        ]


class Total:
    def __init__(self, place, core, plane, outer, sems):
        self.p, self.core, self.plane, self.outer = place, core, plane, outer
        self.send, self.got_core, self.got_plane, self.got_outer = sems
        self.started, self.count = [], 0

    def _go(self, src, dst, recv, peer):
        copy = remote(src, dst, self.send.at[self.count], recv, peer)
        self.count += 1
        copy.start()
        self.started.append(copy)

    def start(self, value):
        self.core[0] = value
        self._go(self.core.at[0], self.core.at[1], self.got_core.at[0], self.p.at(dc=1))

    def plane_step(self):
        p = self.p
        block = self.core.at[1]
        remote(block, block, self.send.at[0], self.got_core.at[0], p.at()).wait_recv()
        here = p.i * p.ny + p.y
        self.plane[here] = self.core[0] + self.core[1]
        for peer in p.plane_peers():
            self._go(
                self.plane.at[here], self.plane.at[here], self.got_plane.at[here], p.at(*peer)
            )

    def outer_step(self):
        p = self.p
        for _, di, dy, _ in p.plane_peers():
            i, y = (p.i + p.inner - di) % p.inner, (p.y + p.ny - dy) % p.ny
            block = self.plane.at[i * p.ny + y]
            sem = self.got_plane.at[i * p.ny + y]
            remote(block, block, self.send.at[0], sem, p.at()).wait_recv()
        total = self.plane[0]
        for k in range(1, p.inner * p.ny):
            total = total + self.plane[k]
        self.outer[p.o] = total
        for peer in p.outer_peers():
            self._go(
                self.outer.at[p.o], self.outer.at[p.o], self.got_outer.at[p.o], p.at(*peer)
            )

    def result(self):
        p = self.p
        for k in range(1, OUTER):
            o = (p.o + OUTER - k) % OUTER
            block = self.outer.at[o]
            remote(block, block, self.send.at[0], self.got_outer.at[o], p.at()).wait_recv()
        total = self.outer[0]
        for k in range(1, OUTER):
            total = total + self.outer[k]
        return total

    def finish(self):
        for copy in self.started:
            copy.wait_send()

    @staticmethod
    def scratch(nd, nt_, shape):
        inner, ny = nd // OUTER, nt_ // 2
        return [
            pltpu.VMEM((2,) + shape, F32),
            pltpu.VMEM((inner * ny,) + shape, F32),
            pltpu.VMEM((OUTER,) + shape, F32),
        ]

    @staticmethod
    def semaphores(nd, nt_):
        inner, ny = nd // OUTER, nt_ // 2
        return [
            pltpu.SemaphoreType.DMA((1 + inner * ny - 1 + OUTER - 1,)),
            pltpu.SemaphoreType.DMA((1,)),
            pltpu.SemaphoreType.DMA((inner * ny,)),
            pltpu.SemaphoreType.DMA((OUTER,)),
        ]


def kernel_backward(
    nd, nt_,
    tokens, held_a, part_b, normed, fq, fk, vb, mixed, rden, do, dr, entering,
    segc, segr, firsts, lasts, gain, sums, inner_sums,
    grad_a, grad_b, grad_tokens, first_total, all_total, inner_total,
    mask, part_a, gn, gd, dk_s, dv_s, dq_s, normed_t, dh1,
    own, near, far, made, leaving,
    *more,
):
    p = Place(nd, nt_)
    rows_all, width = tokens.shape
    sa, sb, more = more[0:4], more[4:8], more[8:]
    t1, t2, t3, more = more[0:3], more[3:6], more[6:9], more[9:]
    ex = Exchange(p, firsts, lasts, True, own, near, far, made, leaving, more[0:4])
    ra = Scatter(p, part_a, *sa, more[4:8])
    rb = Scatter(p, part_b, *sb, more[8:12])
    all_sum = Total(p, *t1, more[12:16])
    inner_sum = Total(p, *t2, more[16:20])
    first_sum = Total(p, *t3, more[20:24])
    p.greet()
    for y in range(p.ny):
        rb.core_send(y)
    all_sum.start(sums[...])
    inner_sum.start(inner_sums[...])
    opening = segc[...] == segr[:, 0:1]

    def first(g, _):
        low = (do[g] * rden[g]).astype(BF16)
        gn[g] = low
        product = low.astype(F32) * mixed[g]
        left = left_lanes(product.shape)
        zero = jnp.zeros_like(product)
        one = jnp.sum(jnp.where(left, product, zero), axis=-1, keepdims=True)
        two = jnp.sum(jnp.where(left, zero, product), axis=-1, keepdims=True)
        slope = -jnp.where(left, one, two)
        gd[g] = slope
        kept = jnp.where(opening, fq[g], jnp.zeros_like(low))
        own[g, :HEAD, :] = pack_state(tn(kept, low))
        total = jnp.sum(kept.astype(F32) * slope, axis=0, keepdims=True)
        own[g, HEAD:, :] = jnp.broadcast_to(total, (STATE_ROWS - HEAD, LANES))
        return 0

    lax.fori_loop(0, nt_, first, 0)
    ex.step_near()
    make_mask(segc, segr, mask, 128)
    for start in range(0, rows_all, 128):
        normed_t[:, start : start + 128] = jnp.transpose(
            normed[start : start + 128, :].astype(F32)
        ).astype(BF16)
    for y in range(p.ny):
        rb.core_sum(y)
    rb.plane_send()
    all_sum.plane_step()
    inner_sum.plane_step()
    ex.step_far()
    block = min(256, rows_all)

    def inside(g, _):
        values, keys = vb[g], fk[g]
        key_heads = split_heads(keys, 0.0)
        state = entering[g]
        high, low = two_parts(wide_state(state[:HEAD]))
        query_t = jnp.transpose(fq[g].astype(F32)).astype(BF16)
        grad_t = jnp.transpose(gn[g].astype(F32)).astype(BF16)
        dk_t = jnp.zeros((LANES, rows_all), F32)
        dv_t = jnp.zeros((LANES, rows_all), F32)
        for start in range(0, rows_all, block):
            end = start + block
            now = mask[start:end, :end]
            query, grad = fq[g, start:end, :], gn[g, start:end, :]
            slope = gd[g, start:end, :]
            query_heads, grad_heads = split_heads(query, 0.0), split_heads(grad, 0.0)
            carried = segc[start:end, :] == segr[:, 0:1]
            dq = jnp.where(
                carried,
                nt(grad, high) + nt(grad, low) + slope * state[HEAD : HEAD + 1, :],
                0.0,
            )
            dk_parts, dv_parts = [], []
            for h in range(2):
                lanes = slice(h * HEAD, h * HEAD + 1)
                rows = slice(h * HEAD, (h + 1) * HEAD)
                weight = nt(query_heads[h], keys[:end]).astype(BF16) * now
                share = (nt(grad_heads[h], values[:end]) + slope[:, lanes]).astype(BF16) * now
                dq = dq + nn(share, key_heads[h][:end])
                dk_parts.append(nn(query_t[rows, start:end], share))
                dv_parts.append(nn(grad_t[rows, start:end], weight))
            dk_now = jnp.concatenate(dk_parts, axis=0)
            dv_now = jnp.concatenate(dv_parts, axis=0)
            if end < rows_all:
                pad = jnp.zeros((LANES, rows_all - end), F32)
                dk_now = jnp.concatenate([dk_now, pad], axis=1)
                dv_now = jnp.concatenate([dv_now, pad], axis=1)
            dk_t, dv_t = dk_t + dk_now, dv_t + dv_now
            dq_s[g, start:end, :] = (
                dq * jnp.minimum(query.astype(F32), 1.0)
            ).astype(BF16)
        dk_s[g] = jnp.transpose(dk_t)
        dv_s[g] = jnp.transpose(dv_t)
        return 0

    lax.fori_loop(0, nt_ // 2, inside, 0)
    ex.step_enter()
    lax.fori_loop(nt_ // 2, nt_, inside, 0)
    rb.plane_sum()
    all_sum.outer_step()
    inner_sum.outer_step()
    ex.arrive()
    closing = segc[...] == segr[:, rows_all - 1 : rows_all]
    dh1[...] = jnp.zeros_like(dh1)

    def outside(g, _):
        state = leaving[g]
        high, low = two_parts(wide_state(state[:HEAD]))
        keys, values = fk[g], vb[g]
        dk = nt(values, high) + nt(values, low) + state[HEAD : HEAD + 1, :]
        dv = nn(keys, high) + nn(keys, low)
        dk = dk_s[g] + jnp.where(closing, dk, 0.0)
        dv = dv_s[g] + jnp.where(closing, dv, 0.0)
        dk = dk * jnp.minimum(keys.astype(F32), 1.0)
        joint = jnp.concatenate([dq_s[g], dk.astype(BF16), dv.astype(BF16)], axis=1)
        w = held_a[g].reshape(width, 3 * LANES)
        part_a[g] = nn(normed_t[...], joint).astype(BF16).reshape(part_a.shape[1:])
        dh1[...] += nt(joint, w)
        return 0

    lax.fori_loop(0, nt_, outside, 0)
    for y in range(p.ny):
        ra.core_send(y)
    first_total[...] = jnp.zeros_like(first_total)
    step = 128

    def leave(k, _):
        at = pl.ds(pl.multiple_of(k * step, step), step)
        x = tokens[at, :].astype(F32)
        center = x - jnp.mean(x, axis=-1, keepdims=True)
        spread = jnp.mean(center * center, axis=-1, keepdims=True)
        scale = lax.rsqrt(spread + EPSILON)
        n = center * scale
        grad = dh1[at, :]
        pushed = grad * gain[...]
        mean = jnp.mean(pushed, axis=-1, keepdims=True)
        along = jnp.mean(pushed * n, axis=-1, keepdims=True)
        back = (pushed - mean - n * along) * scale
        grad_tokens[at, :] = (dr[at, :] + back).astype(BF16)
        first_total[0:1, :] += jnp.sum(grad * n, axis=0, keepdims=True)
        first_total[1:2, :] += jnp.sum(grad, axis=0, keepdims=True)
        return 0

    lax.fori_loop(0, rows_all // step, leave, 0)
    first_sum.start(first_total[...])
    for y in range(p.ny):
        ra.core_sum(y)
    ra.plane_send()
    first_sum.plane_step()
    rb.outer_sum(grad_b)
    all_total[...] = all_sum.result()
    inner_total[...] = inner_sum.result()
    ra.plane_sum()
    first_sum.outer_step()
    ra.outer_sum(grad_a)
    first_total[...] = first_sum.result()
    for each in (ra, rb, all_sum, inner_sum, first_sum, ex):
        each.finish()


def backward_call(nd, nt_, *args):
    tokens, held_a, part_b = args[:3]
    inner_sums = args[-1]
    rows, width = tokens.shape
    ra, ca = held_a.shape[-2:]
    rb, cb = part_b.shape[-2:]
    vm = pl.BlockSpec(memory_space=pltpu.VMEM)
    group = (nt_, rows, LANES)
    outs = [
        jax.ShapeDtypeStruct((ra, ca), F32),
        jax.ShapeDtypeStruct((rb, cb), F32),
        jax.ShapeDtypeStruct((rows, width), BF16),
        jax.ShapeDtypeStruct((8, width), F32),
        jax.ShapeDtypeStruct((8, width), F32),
        jax.ShapeDtypeStruct(inner_sums.shape, F32),
    ]
    return pl.pallas_call(
        functools.partial(kernel_backward, nd, nt_),
        out_shape=outs,
        in_specs=[vm] * len(args),
        out_specs=[vm] * len(outs),
        scratch_shapes=[
            pltpu.VMEM((rows, rows), BF16),
            pltpu.VMEM(held_a.shape, BF16),
            pltpu.VMEM(group, BF16),
            pltpu.VMEM(group, F32),
            pltpu.VMEM(group, F32),
            pltpu.VMEM(group, F32),
            pltpu.VMEM(group, BF16),
            pltpu.VMEM((width, rows), BF16),
            pltpu.VMEM((rows, width), F32),
        ]
        + Exchange.scratch(nd, nt_)
        + [pltpu.VMEM((nt_, STATE_ROWS, LANES), F32)]
        + Scatter.scratch(nd, nt_, ra, ca)
        + Scatter.scratch(nd, nt_, rb, cb)
        + Total.scratch(nd, nt_, (8, width))
        + Total.scratch(nd, nt_, inner_sums.shape)
        + Total.scratch(nd, nt_, (8, width))
        + Exchange.semaphores(nd, nt_)
        + Scatter.semaphores(nd, nt_)
        + Scatter.semaphores(nd, nt_)
        + Total.semaphores(nd, nt_)
        + Total.semaphores(nd, nt_)
        + Total.semaphores(nd, nt_),
        compiler_params=pltpu.CompilerParams(
            collective_id=1, has_side_effects=True, vmem_limit_bytes=VMEM_LIMIT
        ),
        name="attention_backward",
    )(*args)
def local(
    nd, nt_,
    tokens, segment_ids, query_weight, key_weight, value_weight, output_weight,
    inner_weight, outer_weight, inner_bias, first_gain, first_shift,
    second_gain, second_shift, mixer_bias, outer_bias, grad_out,
):
    mine_a, mine_b, segc, segr, firsts, lasts = prepare(
        nd, nt_, tokens, segment_ids, query_weight, key_weight, value_weight,
        output_weight, inner_weight, outer_weight,
    )
    held_a, held_b, normed, fq, fk, vb, mixed, rden, entering = forward_call(
        nd, nt_, tokens, mine_a, mine_b, segc, segr, firsts, lasts,
        first_gain[None], first_shift[None],
    )
    hidden = inner_weight.shape[1]
    layer_out, dr, do, part_b, sums, inner_sums = hidden_call(
        nd, nt_, tokens, mixed, held_b, grad_out, second_gain[None], second_shift[None],
        mixer_bias[None], outer_bias[None], inner_bias.reshape(nt_, hidden),
    )
    grad_a, grad_b, grad_tokens, first_total, all_total, inner_total = backward_call(
        nd, nt_, tokens, held_a, part_b, normed, fq, fk, vb, mixed, rden, do, dr, entering,
        segc, segr, firsts, lasts, first_gain[None], sums, inner_sums,
    )
    head = query_weight.shape[1]
    return (
        layer_out,
        grad_tokens,
        grad_a[:, :head],
        grad_a[:, LANES : LANES + head],
        grad_a[:, 2 * LANES : 2 * LANES + head],
        grad_b[:, :head].T,
        grad_b[:, LANES : LANES + hidden],
        grad_b[:, LANES + hidden :].T,
        inner_total.reshape(inner_bias.shape),
        first_total[0],
        first_total[1],
        all_total[2],
        all_total[3],
        all_total[4],
        all_total[5],
    )


def solution(mesh):
    rows = P(("dp", "tensor"), None)
    one, two, all_of = P("dp", "tensor"), P("tensor", "dp"), P()
    weights = (one, one, one, two, one, two)
    return jax.shard_map(
        functools.partial(local, mesh.shape["dp"], mesh.shape["tensor"]),
        mesh=mesh,
        in_specs=(rows, P("dp")) + weights + (all_of,) * 7 + (rows,),
        out_specs=(rows, rows) + weights + (all_of,) * 7,
        check_vma=False,
    )
```

time: 1100 us -> 176 us (0.16)
  waiting for transfers between devices: 420 us -> 0 us
  blocking collectives: 357 us -> 0 us
  Pallas kernels: 0 us -> 156 us
  matrix products: 121 us -> 0 us
  local copies, waits for them, and re-layouts: 83.3 us -> 12.7 us
  other arithmetic: 58.6 us -> 6.36 us
  loops' own time: 36.7 us -> 0 us
  between operations: 15.1 us -> 0.68 us
    reduce_scatter x9 -> x0, waiting for transfers between devices: 331 us -> none  [the longest x1 62.8 us: local(): lax.psum_scatter(query_w_grad.astype(jnp.bfloat16), 'dp', scatter_dimensi...]
    all_gather x10 -> x0, blocking collectives: 294 us -> none  [the longest x4 102 us: prefix(): pieces = jax.tree.map(lambda part: lax.all_gather(part, axis), value)]
    pallas_call x0 -> x3, Pallas kernels: none -> 156 us  [the longest x1 75.9 us: backward_call(): pl.pallas_call(functools.partial(kernel_backward, nd, nt_), out_shape=out...]
    dot_general x45 -> x0, matrix products: 121 us -> none  [the longest x1 14 us: local(): jnp.einsum('td,fd->tf', grad_out, w_outer_full, preferred_element_type=jn...]
    unnamed x15 -> x0, waiting for transfers between devices: 64.1 us -> none
    psum x1 -> x0, blocking collectives: 39.8 us -> none  [local(): lax.psum((first_gain_grad, first_shift_grad, second_gain_grad, second_shi...]
    another operation x6 -> x0, loops' own time: 36.7 us -> none  [the longest x2 27.7 us: prefix(): return lax.fori_loop(0, count - 1, turn, so_far)]
    all_gather x4 -> x0, waiting for transfers between devices: 25.7 us -> none  [the longest x1 16.3 us: local(): lax.all_gather(w_outer, 'tensor', axis=0, tiled=True)]
  transfers between devices with their start and end apart: 14 -> 0, of which waited for: 9 -> 0; matrix products, arithmetic and copies ran while one was open for 13% -> 0% of each run, Pallas kernels for 0% -> 0%
where the time goes in v1:
time: 176 us; the launch traced here: 175 us
  Pallas kernels  156 us (89%)
  local copies, waits for them, and re-layouts  12.7 us (7%)
  other arithmetic  6.36 us (4%)
    pallas_call x1, Pallas kernels, backward_call(): pl.pallas_call(functools.partial(kernel_backward, nd, nt_), out_shape=out...  75.9 us
    pallas_call x1, Pallas kernels, forward_call(): pl.pallas_call(functools.partial(kernel_forward, nd, nt_), out_shape=outs...  61.6 us
    pallas_call x1, Pallas kernels, hidden_call(): pl.pallas_call(functools.partial(kernel_hidden, nd, nt_), out_shape=outs,...  18.3 us

profile of v1, /device:TPU:0, one launch (start us, length us, event | category | flops | bytes accessed | tf_op | source)
XLA Modules:
  0.0 175.5 jit_solution(5544857797030814392)
XLA Ops:
  0.6 0.8 dynamic_slice.3
  1.4 1.3 reshape.48.inner_bias
  2.7 0.7 reshape.47
  3.4 0.2 fusion
  3.6 0.7 broadcast_in_dim.36.lasts
  4.3 0.6 broadcast_in_dim.34.firsts
  4.9 0.8 convert_element_type.24
  5.7 0.8 convert_element_type.25
  6.4 0.8 convert_element_type.26
  7.2 0.6 pad_maximum_fusion.1.mine_a
  7.8 0.8 convert_bitcast_fusion.1
  8.6 0.9 convert_element_type.28
  9.5 0.9 convert_bitcast_fusion
  10.4 0.7 pad_maximum_fusion.mine_b
  11.1 0.9 copy.33.segc
  12.0 0.0 copy-done
  12.0 61.6 %attention_forward.1 = (bf16[4,4,2,64,384]{4,3,2,1,0:T(8,128)(2,1)}, bf16[4,4,2,64,1152]{4,3,2,1,0:T(8,128)(2,1)}, bf16[512,512]{1,0:T(8,128)(2,1)}, bf16[4,512,...) custom-call(bf16[512,512]{1,0:T(8,128)(2,1)} %tokens.5, ...), custom_call_target="tpu_custom_call" | custom-call | tf_op jit(solution)/shard_map/attention_forward/pallas_call | solution.py:419
  73.5 18.3 %hidden_layer.1 = (bf16[512,512]{1,0:T(8,128)(2,1)}, f32[512,512]{1,0:T(8,128)}, f32[4,512,128]{2,1,0:T(8,128)}, bf16[4,4,2,64,1152]{4,3,2,1,0:T(8,128)(2,1)}, f32[8,512]{1,0:T(8,128)}, /*index=5*/f32[4,512]{1,0:T(4,128)}) custom-call(bf16[512,512]{1,0:T(8,128)(2,1)} %tokens.5, f32[4,512,128]{2,1,0:T(8,128)} %get-tuple-element.36.mixed, ...), custom_call_target="tpu_custom_call" | custom-call | tf_op jit(solution)/shard_map/hidden_layer/pallas_call | solution.py:566
  91.9 75.9 %attention_backward.1 = (f32[64,384]{1,0:T(8,128)}, f32[64,1152]{1,0:T(8,128)}, bf16[512,512]{1,0:T(8,128)(2,1)}, f32[8,512]{1,0:T(8,128)}, f32[8,512]{1,0:T(8,128)}, /*index=5*/f32[4,512]{1,0:T(4,128)}) custom-call(bf16[512,512]{1,0:T(8,128)(2,1)} %tokens.5, bf16[4,4,2,64,384]{4,3,2,1,0:T(8,128)(2,1)} %get-tuple-element.39.held_a, ...), custom_call_target="tpu_custom_call" | custom-call | tf_op jit(solution)/shard_map/attention_backward/pallas_call | solution.py:937
  167.7 1.3 copy.35
  169.0 1.5 fusion.3
  170.5 1.5 fusion.2
  171.9 1.7 slice_bitcast_fusion
  173.6 1.9 %copy.37 = bf16[512,512]{1,0:T(8,128)(2,1)} copy(bf16[512,512]{1,0:T(8,128)(2,1)} %get-tuple-element.89) | data formatting | bytes 1048576
  (1 shorter events, 0.0 us)
Async XLA Ops:
  1.4 10.5 %copy-start = (s32[512]{0:T(512)}, s32[512]{0:T(512)S(1)}, u32[]{:S(2)}) copy-start(s32[512]{0:T(512)S(1)} %dynamic_slice.3) | copy-start | bytes 6148

commit v2 on v1

v2 whole, which is shorter than its diff:
```python
import functools

import jax
import jax.numpy as jnp
from jax import lax
from jax.experimental import pallas as pl
from jax.experimental.pallas import tpu as pltpu
from jax.sharding import PartitionSpec as P

HEAD = 64
LANES = 128
EPSILON = 1e-05
MESH = pl.DeviceIdType.MESH
F32 = jnp.float32
BF16 = jnp.bfloat16
OUTER = 4
STATE_ROWS = HEAD + 8
VMEM_LIMIT = 56 << 20


def nn(a, b):
    return lax.dot_general(a, b, (((1,), (0,)), ((), ())), preferred_element_type=F32)


def nt(a, b):
    return lax.dot_general(a, b, (((1,), (1,)), ((), ())), preferred_element_type=F32)


def tn(a, b):
    return lax.dot_general(a, b, (((0,), (0,)), ((), ())), preferred_element_type=F32)


class Place:
    def __init__(self, dp_size, tensor_size):
        self.nd, self.nt = dp_size, tensor_size
        self.inner, self.ny = dp_size // OUTER, tensor_size // 2
        self.d, self.t = lax.axis_index("dp"), lax.axis_index("tensor")
        self.o, self.i = self.d // self.inner, self.d % self.inner
        self.y, self.c = self.t // 2, self.t % 2
        self.barrier = pltpu.get_barrier_semaphore()

    def at(self, do=0, di=0, dy=0, dc=0):
        o, i = (self.o + do) % OUTER, (self.i + di) % self.inner
        return self.to(o, i, (self.y + dy) % self.ny, (self.c + dc) % 2)

    def to(self, o, i, y, c):
        return (o * self.inner + i, y * 2 + c)

    def nearest(self, k):
        if k == 0:
            return self.o
        high = self.o // 2
        edge = self.o + high * (3 - 2 * self.o)
        place = k * (1 - edge) + (k // 2) * k * edge
        return place + high * (3 - 2 * place)

    def outer_peers(self):
        return [(k, 0, 0, 0) for k in range(1, OUTER)]

    def plane_peers(self):
        return [
            (0, di, dy, 0) for di in range(self.inner) for dy in range(self.ny) if di or dy
        ]

    def group_peers(self):
        return [(0, 0, dy, dc) for dy in range(self.ny) for dc in range(2) if dy or dc]

    def dp_peers(self):
        return [(do, di, 0, 0) for do in range(OUTER) for di in range(self.inner) if do or di]

    def peers(self):
        found = []
        for peer in (
            self.outer_peers() + self.plane_peers() + self.group_peers() + self.dp_peers()
        ):
            if peer not in found:
                found.append(peer)
        return found

    def greet(self):
        for peer in self.peers():
            pl.semaphore_signal(
                self.barrier, inc=1, device_id=self.at(*peer), device_id_type=MESH
            )

    def meet(self):
        pl.semaphore_wait(self.barrier, len(self.peers()))


def remote(src, dst, send, recv, peer):
    return pltpu.make_async_remote_copy(
        src_ref=src,
        dst_ref=dst,
        send_sem=send,
        recv_sem=recv,
        device_id=peer,
        device_id_type=MESH,
    )


class Sender:
    def __init__(self, place, send):
        self.p, self.send, self.started = place, send, []

    def go(self, src, dst, recv, peer):
        copy = remote(src, dst, self.send.at[len(self.started)], recv, peer)
        copy.start()
        self.started.append(copy)

    def got(self, block, recv):
        remote(block, block, self.send.at[0], recv, self.p.at()).wait_recv()

    def finish(self):
        for copy in self.started:
            copy.wait_send()


class Gather(Sender):
    def __init__(self, place, held, sems):
        super().__init__(place, sems[0])
        self.held = held
        self.got_outer, self.got_i, self.got_y, self.got_d, self.got_core = sems[1:]

    def _block(self, k, i, y):
        p = self.p
        return self.held.at[y * 2 + p.c, p.nearest(k), i]

    def outer_start(self):
        p = self.p
        mine = self._block(0, p.i, p.y)
        for k in range(1, OUTER):
            to = p.to(p.nearest(k), p.i, p.y, p.c)
            self.go(mine, mine, self.got_outer.at[p.o], to)

    def spread(self, k):
        p = self.p
        block = self._block(k, p.i, p.y)
        if k:
            self.got(block, self.got_outer.at[p.nearest(k)])
        for di in range(1, p.inner):
            self.go(block, block, self.got_i.at[di - 1, k], p.at(di=di))
        for dy in range(1, p.ny):
            self.go(block, block, self.got_y.at[dy - 1, k], p.at(dy=dy))
        self.go(block, block, self.got_core.at[p.y], p.at(dc=1))

    def turn(self, k):
        p = self.p
        for di in range(1, p.inner):
            block = self._block(k, (p.i + p.inner - di) % p.inner, p.y)
            self.got(block, self.got_i.at[di - 1, k])
            if k < 2:
                for dy in range(1, p.ny):
                    self.go(block, block, self.got_d.at[di - 1, dy - 1, k], p.at(dy=dy))
            self.go(block, block, self.got_core.at[p.y], p.at(dc=1))
        for dy in range(1, p.ny):
            y = (p.y + p.ny - dy) % p.ny
            block = self._block(k, p.i, y)
            self.got(block, self.got_y.at[dy - 1, k])
            if k >= 2:
                for di in range(1, p.inner):
                    self.go(block, block, self.got_d.at[di - 1, dy - 1, k], p.at(di=di))
            self.go(block, block, self.got_core.at[y], p.at(dc=1))

    def corner(self, k):
        p = self.p
        for di in range(1, p.inner):
            for dy in range(1, p.ny):
                y = (p.y + p.ny - dy) % p.ny
                block = self._block(k, (p.i + p.inner - di) % p.inner, y)
                self.got(block, self.got_d.at[di - 1, dy - 1, k])
                self.go(block, block, self.got_core.at[y], p.at(dc=1))

    def core_done(self):
        p = self.p
        for y in range(p.ny):
            self.got(self.held.at[y * 2 + 1 - p.c], self.got_core.at[y])

    @staticmethod
    def semaphores(nd, nt_):
        di, dy = nd // OUTER - 1, nt_ // 2 - 1
        sends = (OUTER - 1) + OUTER * (di + dy + 1 + di + dy) + 2 * OUTER * di * dy
        return [
            pltpu.SemaphoreType.DMA((sends,)),
            pltpu.SemaphoreType.DMA((OUTER,)),
            pltpu.SemaphoreType.DMA((di, OUTER)),
            pltpu.SemaphoreType.DMA((dy, OUTER)),
            pltpu.SemaphoreType.DMA((di, dy, OUTER)),
            pltpu.SemaphoreType.DMA((nt_ // 2,)),
        ]


class Scatter(Sender):
    def __init__(self, place, bufs, sems):
        super().__init__(place, sems[0])
        (self.give, self.core, self.in_i, self.in_y, self.sum_i, self.sum_y,
         self.then_y, self.then_i, self.own, self.outer) = bufs
        self.got_core, self.got_i, self.got_y, self.got_ty, self.got_ti, self.got_outer = sems[1:]

    def core_send(self, y):
        self.go(self.give.at[y], self.core.at[y], self.got_core.at[y], self.p.at(dc=1))

    def core_wait(self, y):
        self.got(self.core.at[y], self.got_core.at[y])

    def first(self, dy):
        p = self.p
        y = (p.y + dy) % p.ny
        if dy:
            for k in range(2, OUTER):
                o = (p.o + k) % OUTER
                self.go(
                    self.core.at[y, o], self.in_y.at[dy - 1, k - 2],
                    self.got_y.at[dy - 1, k - 2], p.at(dy=dy),
                )
        for k in range(2):
            o = (p.o + k) % OUTER
            for di in range(1, p.inner):
                i = (p.i + di) % p.inner
                self.go(
                    self.core.at[y, o, i], self.in_i.at[di - 1, k, dy],
                    self.got_i.at[di - 1, k, dy], p.at(di=di),
                )

    def second_y(self):
        p = self.p
        for k in range(2, OUTER):
            o = (p.o + k) % OUTER
            for dy in range(1, p.ny):
                self.got(self.in_y.at[dy - 1, k - 2], self.got_y.at[dy - 1, k - 2])
            for di in list(range(1, p.inner)) + [0]:
                i = (p.i + di) % p.inner
                total = self.core[p.y, o, i].astype(F32)
                for dy in range(1, p.ny):
                    total = total + self.in_y[dy - 1, k - 2, i].astype(F32)
                self.sum_y[k - 2, di] = total.astype(BF16)
                if di:
                    self.go(
                        self.sum_y.at[k - 2, di], self.then_i.at[di - 1, k - 2],
                        self.got_ti.at[di - 1, k - 2], p.at(di=di),
                    )

    def second_i(self):
        p = self.p
        for dy in list(range(1, p.ny)) + [0]:
            y = (p.y + dy) % p.ny
            for k in range(2):
                o = (p.o + k) % OUTER
                total = self.core[y, o, p.i].astype(F32)
                for di in range(1, p.inner):
                    self.got(self.in_i.at[di - 1, k, dy], self.got_i.at[di - 1, k, dy])
                    total = total + self.in_i[di - 1, k, dy].astype(F32)
                self.sum_i[k, dy] = total.astype(BF16)
                if dy:
                    self.go(
                        self.sum_i.at[k, dy], self.then_y.at[dy - 1, k],
                        self.got_ty.at[dy - 1, k], p.at(dy=dy),
                    )

    def third(self):
        p = self.p
        for k in (2, 3, 1, 0):
            if k < 2:
                total = self.sum_i[k, 0].astype(F32)
                for dy in range(1, p.ny):
                    self.got(self.then_y.at[dy - 1, k], self.got_ty.at[dy - 1, k])
                    total = total + self.then_y[dy - 1, k].astype(F32)
            else:
                total = self.sum_y[k - 2, 0].astype(F32)
                for di in range(1, p.inner):
                    self.got(self.then_i.at[di - 1, k - 2], self.got_ti.at[di - 1, k - 2])
                    total = total + self.then_i[di - 1, k - 2].astype(F32)
            self.own[k] = total.astype(BF16)
            if k:
                self.go(
                    self.own.at[k], self.outer.at[k - 1], self.got_outer.at[k - 1], p.at(do=k)
                )

    def last(self):
        total = self.own[0].astype(F32)
        for k in range(1, OUTER):
            self.got(self.outer.at[k - 1], self.got_outer.at[k - 1])
            total = total + self.outer[k - 1].astype(F32)
        return total

    @staticmethod
    def scratch(nd, nt_, rows, columns):
        inner, ny = nd // OUTER, nt_ // 2
        leads = [
            (ny, OUTER, inner), (ny, OUTER, inner), (inner - 1, 2, ny), (ny - 1, 2, inner),
            (2, ny), (2, inner), (ny - 1, 2), (inner - 1, 2), (OUTER,), (OUTER - 1,),
        ]
        return [pltpu.VMEM(lead + (rows, columns), BF16) for lead in leads]

    @staticmethod
    def semaphores(nd, nt_):
        inner, ny = nd // OUTER, nt_ // 2
        di, dy = inner - 1, ny - 1
        sends = ny + 2 * dy + 2 * di * ny + 2 * di + 2 * dy + OUTER - 1
        shapes = [(sends,), (ny,), (di, 2, ny), (dy, 2), (dy, 2), (di, 2), (OUTER - 1,)]
        return [pltpu.SemaphoreType.DMA(shape) for shape in shapes]


class Exchange:
    def __init__(self, place, firsts, lasts, back, own, near, far, made, entering, sems):
        self.p, self.back = place, back
        self.own, self.near, self.far = own, near, far
        self.made, self.entering = made, entering
        self.edge, self.inlet = (firsts, lasts) if back else (lasts, firsts)
        self.s_send, self.s_near, self.s_far, self.s_enter = sems
        self.started, self.count = [], 0

    def _go(self, src, dst, recv, peer):
        copy = remote(src, dst, self.s_send.at[self.count], recv, peer)
        self.count += 1
        copy.start()
        self.started.append(copy)

    def step_near(self):
        p = self.p
        for peer in p.group_peers():
            to = p.at(*peer)
            self._go(self.own.at[to[1]], self.near.at[p.t], self.s_near.at[p.t], to)
        self.near[p.t] = self.own[p.t]

    def step_far(self):
        p = self.p
        for _, _, dy, dc in p.group_peers():
            t = ((p.y + p.ny - dy) % p.ny) * 2 + (p.c + dc) % 2
            block = self.near.at[t]
            remote(block, block, self.s_send.at[0], self.s_near.at[t], p.at()).wait_recv()
        border = 0 if self.back else p.nt - 1
        ids = self.edge[border : border + 1, :]
        total = jnp.zeros((STATE_ROWS, LANES), F32)
        for j in range(p.nt):
            total = total + jnp.where(self.edge[j : j + 1, :] == ids, self.near[j], 0.0)
        rows = lax.broadcasted_iota(jnp.int32, (STATE_ROWS, LANES), 0)
        self.far[p.d] = jnp.where(rows > HEAD, jnp.broadcast_to(ids, rows.shape), total)
        for peer in p.dp_peers():
            self._go(self.far.at[p.d], self.far.at[p.d], self.s_far.at[p.d], p.at(*peer))

    def step_enter(self):
        p = self.p
        for do, di, _, _ in p.dp_peers():
            o, i = (p.o + OUTER - do) % OUTER, (p.i + p.inner - di) % p.inner
            d = o * p.inner + i
            block = self.far.at[d]
            remote(block, block, self.s_send.at[0], self.s_far.at[d], p.at()).wait_recv()
        for j in range(p.nt):
            inlet = self.inlet[j : j + 1, :]
            total = jnp.zeros((STATE_ROWS, LANES), F32)
            for d in range(p.nd):
                ids = self.far[d, HEAD + 1 : HEAD + 2, :]
                wanted = jnp.where(d > p.d if self.back else d < p.d, ids, -1.0)
                total = total + jnp.where(wanted == inlet, self.far[d], 0.0)
            for k in range(j + 1, p.nt) if self.back else range(j):
                total = total + jnp.where(self.edge[k : k + 1, :] == inlet, self.near[k], 0.0)
            self.made[j] = total
        for peer in p.group_peers():
            to = p.at(*peer)
            self._go(self.made.at[to[1]], self.entering.at[p.t], self.s_enter.at[p.t], to)
        self.entering[p.t] = self.made[p.t]

    def arrive(self):
        p = self.p
        for _, _, dy, dc in p.group_peers():
            t = ((p.y + p.ny - dy) % p.ny) * 2 + (p.c + dc) % 2
            block = self.entering.at[t]
            remote(block, block, self.s_send.at[0], self.s_enter.at[t], p.at()).wait_recv()

    def finish(self):
        for copy in self.started:
            copy.wait_send()

    @staticmethod
    def scratch(nd, nt):
        return [
            pltpu.VMEM((nt, STATE_ROWS, LANES), F32),
            pltpu.VMEM((nt, STATE_ROWS, LANES), F32),
            pltpu.VMEM((nd, STATE_ROWS, LANES), F32),
            pltpu.VMEM((nt, STATE_ROWS, LANES), F32),
        ]

    @staticmethod
    def semaphores(nd, nt):
        return [
            pltpu.SemaphoreType.DMA((2 * (nt - 1) + nd - 1,)),
            pltpu.SemaphoreType.DMA((nt,)),
            pltpu.SemaphoreType.DMA((nd,)),
            pltpu.SemaphoreType.DMA((nt,)),
        ]


def left_lanes(shape):
    return lax.broadcasted_iota(jnp.int32, shape, len(shape) - 1) < HEAD


def split_heads(block, fill):
    left = left_lanes(block.shape)
    other = jnp.full_like(block, fill)
    return jnp.where(left, block, other), jnp.where(left, other, block)


def feature(values):
    return jnp.where(values > 0.0, values + 1.0, jnp.exp(jnp.minimum(values, 0.0)))


def pack_state(product):
    left = left_lanes((HEAD, LANES))
    return jnp.where(left, product[:HEAD], product[HEAD:])


def wide_state(packed):
    left = left_lanes((HEAD, LANES))
    zero = jnp.zeros_like(packed)
    return jnp.concatenate([jnp.where(left, packed, zero), jnp.where(left, zero, packed)], axis=0)


def two_parts(values):
    high = values.astype(BF16)
    return high, (values - high.astype(F32)).astype(BF16)


def same_head():
    row = lax.broadcasted_iota(jnp.int32, (LANES, LANES), 0) < HEAD
    return row == left_lanes((LANES, LANES))


def make_mask(segc, segr, mask, rows):
    total = segc.shape[0]
    for start in range(0, total, rows):
        at = lax.broadcasted_iota(jnp.int32, (rows, total), 0) + start
        key = lax.broadcasted_iota(jnp.int32, (rows, total), 1)
        same = segc[start : start + rows, :] == segr[...]
        mask[start : start + rows, :] = jnp.where((at >= key) & same, 1.0, 0.0).astype(BF16)


class Total:
    def __init__(self, place, core, plane, outer, sems):
        self.p, self.core, self.plane, self.outer = place, core, plane, outer
        self.send, self.got_core, self.got_plane, self.got_outer = sems
        self.started, self.count = [], 0

    def _go(self, src, dst, recv, peer):
        copy = remote(src, dst, self.send.at[self.count], recv, peer)
        self.count += 1
        copy.start()
        self.started.append(copy)

    def start(self, value):
        self.core[0] = value
        self._go(self.core.at[0], self.core.at[1], self.got_core.at[0], self.p.at(dc=1))

    def plane_step(self):
        p = self.p
        block = self.core.at[1]
        remote(block, block, self.send.at[0], self.got_core.at[0], p.at()).wait_recv()
        here = p.i * p.ny + p.y
        self.plane[here] = self.core[0] + self.core[1]
        for peer in p.plane_peers():
            self._go(
                self.plane.at[here], self.plane.at[here], self.got_plane.at[here], p.at(*peer)
            )

    def outer_step(self):
        p = self.p
        for _, di, dy, _ in p.plane_peers():
            i, y = (p.i + p.inner - di) % p.inner, (p.y + p.ny - dy) % p.ny
            block = self.plane.at[i * p.ny + y]
            sem = self.got_plane.at[i * p.ny + y]
            remote(block, block, self.send.at[0], sem, p.at()).wait_recv()
        total = self.plane[0]
        for k in range(1, p.inner * p.ny):
            total = total + self.plane[k]
        self.outer[p.o] = total
        for peer in p.outer_peers():
            self._go(
                self.outer.at[p.o], self.outer.at[p.o], self.got_outer.at[p.o], p.at(*peer)
            )

    def result(self):
        p = self.p
        for k in range(1, OUTER):
            o = (p.o + OUTER - k) % OUTER
            block = self.outer.at[o]
            remote(block, block, self.send.at[0], self.got_outer.at[o], p.at()).wait_recv()
        total = self.outer[0]
        for k in range(1, OUTER):
            total = total + self.outer[k]
        return total

    def finish(self):
        for copy in self.started:
            copy.wait_send()

    @staticmethod
    def scratch(nd, nt_, shape):
        inner, ny = nd // OUTER, nt_ // 2
        return [
            pltpu.VMEM((2,) + shape, F32),
            pltpu.VMEM((inner * ny,) + shape, F32),
            pltpu.VMEM((OUTER,) + shape, F32),
        ]

    @staticmethod
    def semaphores(nd, nt_):
        inner, ny = nd // OUTER, nt_ // 2
        return [
            pltpu.SemaphoreType.DMA((1 + inner * ny - 1 + OUTER - 1,)),
            pltpu.SemaphoreType.DMA((1,)),
            pltpu.SemaphoreType.DMA((inner * ny,)),
            pltpu.SemaphoreType.DMA((OUTER,)),
        ]


def kernel_whole(
    nd, nt_,
    tokens, segments, wq, wk, wv, wo, w1, w2, inner_bias, gain1, shift1, gain2, shift2,
    mixer_bias, outer_bias, cotangent,
    out, grad_tokens, grad_q, grad_k, grad_v, grad_o, grad_1, grad_2,
    grad_ib, grad_g1, grad_s1, grad_g2, grad_s2, grad_mb, grad_ob,
    *scratch,
):
    it = iter(scratch)

    def take(count):
        return [next(it) for _ in range(count)]

    (held_kv, held_qo, held_2, held_1) = take(4)
    (segc, edges, mask, normed, normed_t, fq, fk, vb, num_s, den_s) = take(10)
    (res, unit, inv, h2, h2t, cot, dh2, act, dhid, dbt) = take(10)
    (do, dr, gn, gd, dk_s, dv_s, dq_s, dh1, sums, first_sums) = take(10)
    own, near, far, made, entering = take(5)
    own_b, near_b, far_b, made_b, leaving = take(5)
    bufs_f, bufs_qo, bufs_kv = take(10), take(10), take(10)
    bufs_t1, bufs_t2 = take(3), take(3)
    p = Place(nd, nt_)
    kv, qo = Gather(p, held_kv, take(6)), Gather(p, held_qo, take(6))
    g2, g1 = Gather(p, held_2, take(6)), Gather(p, held_1, take(6))
    firsts, lasts = edges.at[0], edges.at[1]
    ex = Exchange(p, firsts, lasts, False, own, near, far, made, entering, take(4))
    xb = Exchange(p, firsts, lasts, True, own_b, near_b, far_b, made_b, leaving, take(4))
    sf = Scatter(p, bufs_f, take(7))
    sqo, skv = Scatter(p, bufs_qo, take(7)), Scatter(p, bufs_kv, take(7))
    all_sum, first_sum = Total(p, *bufs_t1, take(4)), Total(p, *bufs_t2, take(4))

    rows_all, width = tokens.shape
    head, hidden = wq.shape[1], w1.shape[1]
    part_rows = wq.shape[0]
    block_shape = (OUTER, p.inner, part_rows)
    step, block = 128, min(256, rows_all)

    p.greet()
    here = (p.t, p.o, p.i)
    if head < LANES:
        blank = jnp.zeros((part_rows, 2 * LANES), BF16)
        held_kv[here] = blank
        held_qo[here] = blank
    held_kv[here + (slice(None), slice(0, head))] = wk[...].astype(BF16)
    held_kv[here + (slice(None), slice(LANES, LANES + head))] = wv[...].astype(BF16)
    p.meet()
    kv.outer_start()
    kv.spread(0)
    held_qo[here + (slice(None), slice(0, head))] = wq[...].astype(BF16)
    held_qo[here + (slice(None), slice(LANES, LANES + head))] = jnp.transpose(wo[...]).astype(BF16)
    held_2[here] = jnp.transpose(w2[...]).astype(BF16)
    held_1[here] = w1[...].astype(BF16)
    qo.outer_start()
    g2.outer_start()
    g1.outer_start()

    segr = segments[:, pl.ds(pl.multiple_of(p.t * rows_all, LANES), rows_all)].astype(F32)
    for start in range(0, rows_all, LANES):
        wide = jnp.broadcast_to(segr[:, start : start + LANES], (8, LANES))
        segc[start : start + LANES, :] = jnp.transpose(wide)[:, 0:1]
    for j in range(nt_):
        for e, at in enumerate((j * rows_all, (j + 1) * rows_all - 1)):
            edge = segments[:, at : at + 1].astype(F32)
            edges[e, j : j + 1, :] = jnp.broadcast_to(edge, (1, LANES))
    first_id, last_id = segr[:, 0:1], segr[:, rows_all - 1 : rows_all]

    def norm(k, _):
        at = pl.ds(pl.multiple_of(k * step, step), step)
        x = tokens[at, :].astype(F32)
        center = x - jnp.mean(x, axis=-1, keepdims=True)
        spread = jnp.mean(center * center, axis=-1, keepdims=True)
        y = center * lax.rsqrt(spread + EPSILON) * gain1[...] + shift1[...]
        normed[at, :] = y.astype(BF16)
        normed_t[:, at] = jnp.transpose(y).astype(BF16)
        cot[:, at] = jnp.transpose(cotangent[at, :].astype(F32)).astype(BF16)
        return 0

    lax.fori_loop(0, rows_all // step, norm, 0)
    for start in range(0, rows_all, 128):
        later = lax.broadcasted_iota(jnp.int32, (128, rows_all), 0) + start
        earlier = lax.broadcasted_iota(jnp.int32, (128, rows_all), 1)
        same = segc[start : start + 128, :] == segr
        mask[start : start + 128, :] = jnp.where((later >= earlier) & same, 1.0, 0.0).astype(BF16)
    for k in range(1, OUTER):
        kv.spread(k)
    for k in range(OUTER):
        kv.turn(k)
    for k in range(OUTER):
        qo.spread(k)
    for k in range(OUTER):
        kv.corner(k)
    kv.core_done()

    def keys_values(g, _):
        w = held_kv[g].reshape(width, 2 * LANES)
        both = nn(normed[...], w)
        keys = feature(both[:, :LANES]).astype(BF16)
        values = both[:, LANES:].astype(BF16)
        fk[g] = keys
        vb[g] = values
        kept = jnp.where(segc[...] == last_id, keys, jnp.zeros_like(keys))
        own[g, :HEAD, :] = pack_state(tn(kept, values))
        total = jnp.sum(kept.astype(F32), axis=0, keepdims=True)
        own[g, HEAD:, :] = jnp.broadcast_to(total, (STATE_ROWS - HEAD, LANES))
        return 0

    lax.fori_loop(0, nt_, keys_values, 0)
    ex.step_near()
    for k in range(OUTER):
        qo.turn(k)
    for k in range(OUTER):
        g2.spread(k)
    for k in range(OUTER):
        qo.corner(k)
    qo.core_done()

    def queries(g, _):
        w = held_qo[g].reshape(width, 2 * LANES)
        fq[g] = feature(nn(normed[...], w[:, :LANES])).astype(BF16)
        return 0

    lax.fori_loop(0, nt_, queries, 0)
    ex.step_far()
    for k in range(OUTER):
        g1.spread(k)

    def inside(g, _):
        values = split_heads(vb[g], 1.0)
        for start in range(0, rows_all, block):
            end = start + block
            now = mask[start:end, :end]
            query = split_heads(fq[g, start:end, :], 0.0)
            keys = fk[g, :end, :]
            parts = []
            for h in range(2):
                scores = nt(query[h], keys).astype(BF16) * now
                parts.append(nn(scores, values[h][:end]))
            left = left_lanes(parts[0].shape)
            num_s[g, start:end, :] = jnp.where(left, parts[0], parts[1])
            den_s[g, start:end, :] = pltpu.roll(
                jnp.where(left, parts[1], parts[0]), HEAD, 1
            )
        return 0

    lax.fori_loop(0, nt_ // 2, inside, 0)
    for k in range(OUTER):
        g2.turn(k)
    ex.step_enter()
    lax.fori_loop(nt_ // 2, nt_, inside, 0)
    for k in range(OUTER):
        g1.turn(k)
    for k in range(OUTER):
        g2.corner(k)
    ex.arrive()

    def outside(g, _):
        state = entering[g]
        high, low = two_parts(wide_state(state[:HEAD]))
        total = jnp.broadcast_to(jnp.transpose(state[HEAD:, :])[:, 0:1], (LANES, LANES))
        sum_high, sum_low = two_parts(jnp.where(same_head(), total, 0.0))
        query = fq[g]
        query = jnp.where(segc[...] == first_id, query, jnp.zeros_like(query))
        num = num_s[g] + (nn(query, high) + nn(query, low))
        den = den_s[g] + (nn(query, sum_high) + nn(query, sum_low))
        inverse = 1.0 / den
        den_s[g] = inverse
        num_s[g] = num * inverse
        return 0

    lax.fori_loop(0, nt_, outside, 0)
    mixed, rden = num_s, den_s
    for k in range(OUTER):
        g1.corner(k)

    def output_weight(g):
        return held_qo[g, :, :, :, LANES:].reshape(width, LANES)

    def enter(k, _):
        at = pl.ds(pl.multiple_of(k * step, step), step)
        r = tokens[at, :].astype(F32) + mixer_bias[...]
        for g in range(nt_):
            r = r + nt(mixed[g, at, :].astype(BF16), output_weight(g))
        center = r - jnp.mean(r, axis=-1, keepdims=True)
        spread = jnp.mean(center * center, axis=-1, keepdims=True)
        scale = lax.rsqrt(spread + EPSILON)
        n = center * scale
        y = n * gain2[...] + shift2[...]
        res[at, :] = r + outer_bias[...]
        unit[at, :] = n
        inv[at, :] = scale
        h2[at, :] = y.astype(BF16)
        h2t[:, at] = jnp.transpose(y).astype(BF16)
        dh2[at, :] = jnp.zeros((step, width), F32)
        return 0

    lax.fori_loop(0, rows_all // step, enter, 0)
    sums[...] = jnp.zeros_like(sums)
    g2.core_done()
    g1.core_done()
    tall = width // OUTER

    def feed(g):
        wi = held_1[g].reshape(width, hidden)
        wt = held_2[g].reshape(width, hidden)
        total = jnp.zeros((1, hidden), F32)
        bias = inner_bias[:, pl.ds(pl.multiple_of(g * hidden, LANES), hidden)]
        for start in range(0, rows_all, block):
            end = start + block
            u = nn(h2[start:end, :], wi) + bias
            below = 0.5 * (1.0 + lax.erf(u * 0.7071067811865476))
            slope = below + u * (jnp.exp(-0.5 * (u * u)) * 0.3989422804014327)
            a = (u * below).astype(BF16)
            du = (nn(cotangent[start:end, :], wt) * slope).astype(BF16)
            act[start:end, :] = a
            dhid[start:end, :] = du
            total = total + jnp.sum(du.astype(F32), axis=0, keepdims=True)
            res[start:end, :] += nt(a, wt)
            dh2[start:end, :] += nt(du, wi)
        sums[pl.ds(8 + g, 1), 0:hidden] = total

    shape = (p.inner, part_rows, hidden)

    def feed_grads(y, mine):
        for o in range(OUTER):
            for s, (left, right) in enumerate(((h2t, dhid), (cot, act))):
                lanes = slice(s * hidden, (s + 1) * hidden)
                value = nn(left[o * tall : (o + 1) * tall, :], right[...]).reshape(shape)
                if mine:
                    value = value + sf.core[y, o, :, :, lanes].astype(F32)
                    sf.core[y, o, :, :, lanes] = value.astype(BF16)
                else:
                    sf.give[y, o, :, :, lanes] = value.astype(BF16)

    for dy in list(range(1, p.ny)) + [0]:
        y = (p.y + dy) % p.ny
        feed(y * 2 + 1 - p.c)
        feed_grads(y, False)
        sf.core_send(y)
        feed(y * 2 + p.c)
        sf.core_wait(y)
        feed_grads(y, True)
        sf.first(dy)

    def leave(k, _):
        at = pl.ds(pl.multiple_of(k * step, step), step)
        out[at, :] = res[at, :].astype(BF16)
        n = unit[at, :]
        grad = dh2[at, :]
        e = cotangent[at, :].astype(F32)
        pushed = grad * gain2[...]
        mean = jnp.mean(pushed, axis=-1, keepdims=True)
        along = jnp.mean(pushed * n, axis=-1, keepdims=True)
        back = e + (pushed - mean - n * along) * inv[at, :]
        dr[at, :] = back
        low = back.astype(BF16)
        wide = low.astype(F32)
        dbt[:, at] = jnp.transpose(wide).astype(BF16)
        for g in range(nt_):
            do[g, at, :] = nn(low, output_weight(g))
        sums[2:3, :] += jnp.sum(grad * n, axis=0, keepdims=True)
        sums[3:4, :] += jnp.sum(grad, axis=0, keepdims=True)
        sums[4:5, :] += jnp.sum(wide, axis=0, keepdims=True)
        sums[5:6, :] += jnp.sum(e, axis=0, keepdims=True)
        return 0

    lax.fori_loop(0, rows_all // step, leave, 0)

    def first(g, _):
        low = (do[g] * rden[g]).astype(BF16)
        gn[g] = low
        product = low.astype(F32) * mixed[g]
        left = left_lanes(product.shape)
        zero = jnp.zeros_like(product)
        one = jnp.sum(jnp.where(left, product, zero), axis=-1, keepdims=True)
        two = jnp.sum(jnp.where(left, zero, product), axis=-1, keepdims=True)
        slope = -jnp.where(left, one, two)
        gd[g] = slope
        kept = jnp.where(segc[...] == first_id, fq[g], jnp.zeros_like(low))
        own_b[g, :HEAD, :] = pack_state(tn(kept, low))
        total = jnp.sum(kept.astype(F32) * slope, axis=0, keepdims=True)
        own_b[g, HEAD:, :] = jnp.broadcast_to(total, (STATE_ROWS - HEAD, LANES))
        return 0

    lax.fori_loop(0, nt_, first, 0)
    xb.step_near()
    all_sum.start(sums[...])

    def inside_back(g, _):
        values, keys = vb[g], fk[g]
        key_heads = split_heads(keys, 0.0)
        state = entering[g]
        high, low = two_parts(wide_state(state[:HEAD]))
        query_t = jnp.transpose(fq[g].astype(F32)).astype(BF16)
        grad_t = jnp.transpose(gn[g].astype(F32)).astype(BF16)
        dk_t = jnp.zeros((LANES, rows_all), F32)
        dv_t = jnp.zeros((LANES, rows_all), F32)
        for start in range(0, rows_all, block):
            end = start + block
            now = mask[start:end, :end]
            query, grad = fq[g, start:end, :], gn[g, start:end, :]
            slope = gd[g, start:end, :]
            query_heads, grad_heads = split_heads(query, 0.0), split_heads(grad, 0.0)
            dq = jnp.where(
                segc[start:end, :] == first_id,
                nt(grad, high) + nt(grad, low) + slope * state[HEAD : HEAD + 1, :],
                0.0,
            )
            dk_parts, dv_parts = [], []
            for h in range(2):
                lanes = slice(h * HEAD, h * HEAD + 1)
                part = slice(h * HEAD, (h + 1) * HEAD)
                weight = nt(query_heads[h], keys[:end]).astype(BF16) * now
                share = (nt(grad_heads[h], values[:end]) + slope[:, lanes]).astype(BF16) * now
                dq = dq + nn(share, key_heads[h][:end])
                dk_parts.append(nn(query_t[part, start:end], share))
                dv_parts.append(nn(grad_t[part, start:end], weight))
            dk_now = jnp.concatenate(dk_parts, axis=0)
            dv_now = jnp.concatenate(dv_parts, axis=0)
            if end < rows_all:
                pad = jnp.zeros((LANES, rows_all - end), F32)
                dk_now = jnp.concatenate([dk_now, pad], axis=1)
                dv_now = jnp.concatenate([dv_now, pad], axis=1)
            dk_t, dv_t = dk_t + dk_now, dv_t + dv_now
            dq_s[g, start:end, :] = (dq * jnp.minimum(query.astype(F32), 1.0)).astype(BF16)
        dk_s[g] = jnp.transpose(dk_t)
        dv_s[g] = jnp.transpose(dv_t)
        return 0

    lax.fori_loop(0, nt_ // 2, inside_back, 0)
    xb.step_far()
    all_sum.plane_step()
    sf.second_y()
    lax.fori_loop(nt_ // 2, nt_, inside_back, 0)
    xb.step_enter()
    all_sum.outer_step()
    sf.second_i()

    def attention_grads(scatter, dc, joint):
        for dy in list(range(1, p.ny)) + [0]:
            y = (p.y + dy) % p.ny
            g = y * 2 + (p.c + dc) % 2
            values = joint(g)
            if not dc:
                scatter.core_wait(y)
            for s, (left, right) in enumerate(values):
                lanes = slice(s * LANES, (s + 1) * LANES)
                value = nn(left, right).reshape(block_shape + (LANES,))
                if dc:
                    scatter.give[y, :, :, :, lanes] = value.astype(BF16)
                else:
                    value = value + scatter.core[y, :, :, :, lanes].astype(F32)
                    scatter.core[y, :, :, :, lanes] = value.astype(BF16)
            if dc:
                scatter.core_send(y)
            else:
                scatter.first(dy)

    def query_output(g):
        return ((normed_t[...], dq_s[g]), (dbt[...], mixed[g].astype(BF16)))

    attention_grads(sqo, 1, query_output)
    attention_grads(sqo, 0, query_output)
    sf.third()

    def query_back(g, _):
        dh1[...] += nt(dq_s[g], held_qo[g, :, :, :, :LANES].reshape(width, LANES))
        return 0

    dh1[...] = jnp.zeros_like(dh1)
    lax.fori_loop(0, nt_, query_back, 0)
    sqo.second_y()
    sqo.second_i()
    xb.arrive()

    def key_value(g):
        state = leaving[g]
        high, low = two_parts(wide_state(state[:HEAD]))
        keys, values = fk[g], vb[g]
        dk = nt(values, high) + nt(values, low) + state[HEAD : HEAD + 1, :]
        dv = nn(keys, high) + nn(keys, low)
        closing = segc[...] == last_id
        dk = dk_s[g] + jnp.where(closing, dk, 0.0)
        dv = dv_s[g] + jnp.where(closing, dv, 0.0)
        dk = (dk * jnp.minimum(keys.astype(F32), 1.0)).astype(BF16)
        dv = dv.astype(BF16)
        joint = jnp.concatenate([dk, dv], axis=1)
        dh1[...] += nt(joint, held_kv[g].reshape(width, 2 * LANES))
        return ((normed_t[...], dk), (normed_t[...], dv))

    attention_grads(skv, 1, key_value)
    attention_grads(skv, 0, key_value)
    sqo.third()
    first_sums[...] = jnp.zeros_like(first_sums)

    def finish(k, _):
        at = pl.ds(pl.multiple_of(k * step, step), step)
        x = tokens[at, :].astype(F32)
        center = x - jnp.mean(x, axis=-1, keepdims=True)
        spread = jnp.mean(center * center, axis=-1, keepdims=True)
        scale = lax.rsqrt(spread + EPSILON)
        n = center * scale
        grad = dh1[at, :]
        pushed = grad * gain1[...]
        mean = jnp.mean(pushed, axis=-1, keepdims=True)
        along = jnp.mean(pushed * n, axis=-1, keepdims=True)
        back = (pushed - mean - n * along) * scale
        grad_tokens[at, :] = (dr[at, :] + back).astype(BF16)
        first_sums[0:1, :] += jnp.sum(grad * n, axis=0, keepdims=True)
        first_sums[1:2, :] += jnp.sum(grad, axis=0, keepdims=True)
        return 0

    lax.fori_loop(0, rows_all // step, finish, 0)
    first_sum.start(first_sums[...])
    skv.second_y()
    first_sum.plane_step()
    skv.second_i()
    total = sf.last()
    grad_1[...] = total[:, :hidden]
    grad_2[...] = jnp.transpose(total[:, hidden:])
    skv.third()
    first_sum.outer_step()
    total = sqo.last()
    grad_q[...] = total[:, :head]
    grad_o[...] = jnp.transpose(total[:, LANES:])[:head, :]
    total = all_sum.result()
    grad_g2[...] = total[2:3, :]
    grad_s2[...] = total[3:4, :]
    grad_mb[...] = total[4:5, :]
    grad_ob[...] = total[5:6, :]
    for g in range(nt_):
        grad_ib[:, g * hidden : (g + 1) * hidden] = total[8 + g : 9 + g, :hidden]
    total = skv.last()
    grad_k[...] = total[:, :head]
    grad_v[...] = total[:, LANES : LANES + head]
    total = first_sum.result()
    grad_g1[...] = total[0:1, :]
    grad_s1[...] = total[1:2, :]
    for each in (kv, qo, g2, g1, ex, xb, sf, sqo, skv, all_sum, first_sum):
        each.finish()


def local(nd, nt_, *args):
    (tokens, segments, wq, wk, wv, wo, w1, w2, inner_bias, *vectors, cotangent) = args
    rows, width = tokens.shape
    inner = nd // OUTER
    part_rows, hidden = w1.shape
    vm = pl.BlockSpec(memory_space=pltpu.VMEM)
    group = (nt_, rows, LANES)
    row = jax.ShapeDtypeStruct((1, width), F32)
    outs = [
        jax.ShapeDtypeStruct(tokens.shape, BF16),
        jax.ShapeDtypeStruct(tokens.shape, BF16),
        *[jax.ShapeDtypeStruct(w.shape, F32) for w in (wq, wk, wv, wo, w1, w2)],
        jax.ShapeDtypeStruct((1, nt_ * hidden), F32),
        *[row] * 6,
    ]
    held = (nt_, OUTER, inner, part_rows)
    state = pltpu.VMEM((nt_, STATE_ROWS, LANES), F32)
    square = (rows, width)
    scratch = [
        pltpu.VMEM(held + (2 * LANES,), BF16),
        pltpu.VMEM(held + (2 * LANES,), BF16),
        pltpu.VMEM(held + (hidden,), BF16),
        pltpu.VMEM(held + (hidden,), BF16),
        pltpu.VMEM((rows, 1), F32),
        pltpu.VMEM((2, nt_, LANES), F32),
        pltpu.VMEM((rows, rows), BF16),
        pltpu.VMEM(square, BF16),
        pltpu.VMEM((width, rows), BF16),
        pltpu.VMEM(group, BF16),
        pltpu.VMEM(group, BF16),
        pltpu.VMEM(group, BF16),
        pltpu.VMEM(group, F32),
        pltpu.VMEM(group, F32),
        pltpu.VMEM(square, F32),
        pltpu.VMEM(square, F32),
        pltpu.VMEM((rows, 1), F32),
        pltpu.VMEM(square, BF16),
        pltpu.VMEM((width, rows), BF16),
        pltpu.VMEM((width, rows), BF16),
        pltpu.VMEM(square, F32),
        pltpu.VMEM((rows, hidden), BF16),
        pltpu.VMEM((rows, hidden), BF16),
        pltpu.VMEM((width, rows), BF16),
        pltpu.VMEM(group, F32),
        pltpu.VMEM(square, F32),
        pltpu.VMEM(group, BF16),
        pltpu.VMEM(group, F32),
        pltpu.VMEM(group, F32),
        pltpu.VMEM(group, F32),
        pltpu.VMEM(group, BF16),
        pltpu.VMEM(square, F32),
        pltpu.VMEM((8 + max(8, nt_), width), F32),
        pltpu.VMEM((8, width), F32),
    ]
    for _ in range(2):
        scratch += Exchange.scratch(nd, nt_) + [state]
    scratch += Scatter.scratch(nd, nt_, part_rows, 2 * hidden)
    scratch += Scatter.scratch(nd, nt_, part_rows, 2 * LANES)
    scratch += Scatter.scratch(nd, nt_, part_rows, 2 * LANES)
    scratch += Total.scratch(nd, nt_, (8 + max(8, nt_), width))
    scratch += Total.scratch(nd, nt_, (8, width))
    for _ in range(4):
        scratch += Gather.semaphores(nd, nt_)
    for _ in range(2):
        scratch += Exchange.semaphores(nd, nt_)
    for _ in range(3):
        scratch += Scatter.semaphores(nd, nt_)
    for _ in range(2):
        scratch += Total.semaphores(nd, nt_)
    operands = (
        tokens, segments[None], wq, wk, wv, wo, w1, w2, inner_bias[None],
        *[v[None] for v in vectors], cotangent,
    )
    results = pl.pallas_call(
        functools.partial(kernel_whole, nd, nt_),
        out_shape=outs,
        in_specs=[vm] * len(operands),
        out_specs=[vm] * len(outs),
        scratch_shapes=scratch,
        compiler_params=pltpu.CompilerParams(
            collective_id=0, has_side_effects=True, vmem_limit_bytes=VMEM_LIMIT
        ),
        name="whole_layer",
    )(*operands)
    return tuple(results[:8]) + tuple(v.reshape(-1) for v in results[8:])


def solution(mesh):
    rows = P(("dp", "tensor"), None)
    one, two, all_of = P("dp", "tensor"), P("tensor", "dp"), P()
    weights = (one, one, one, two, one, two)
    return jax.shard_map(
        functools.partial(local, mesh.shape["dp"], mesh.shape["tensor"]),
        mesh=mesh,
        in_specs=(rows, P("dp")) + weights + (all_of,) * 7 + (rows,),
        out_specs=(rows, rows) + weights + (all_of,) * 7,
        check_vma=False,
    )
```

time: 176 us -> 125 us (0.71)
  Pallas kernels: 156 us -> 108 us
  other arithmetic: 6.36 us -> 0 us
  local copies, waits for them, and re-layouts: 12.7 us -> 15.7 us
    pallas_call x3 -> x1, Pallas kernels: 156 us -> 108 us  [local(): pl.pallas_call(functools.partial(kernel_whole, nd, nt_), out_shape=outs,...]
    unnamed x4 -> x43, local copies, waits for them, and re-layouts: 3.17 us -> 15.7 us
    convert_element_type x5 -> x0, other arithmetic: 3.38 us -> none  [the longest x3 2.28 us: prepare(): w.astype(BF16)]
    slice x2 -> x0, local copies, waits for them, and re-layouts: 2.93 us -> none  [the longest x1 1.47 us: local(): all_total[5]]
    reshape x3 -> x0, local copies, waits for them, and re-layouts: 2.87 us -> none  [the longest x1 1.3 us: local(): inner_bias.reshape(nt_, hidden)]
where the time goes in v2:
time: 125 us
  Pallas kernels  108 us (86%)
  local copies, waits for them, and re-layouts  15.7 us (13%)
    pallas_call x1, Pallas kernels, local(): pl.pallas_call(functools.partial(kernel_whole, nd, nt_), out_shape=outs,...  108 us
    unnamed x43, local copies, waits for them, and re-layouts  15.7 us

profile of v2, /device:TPU:0, one launch (start us, length us, event | category | flops | bytes accessed | tf_op | source)
XLA Modules:
  0.0 124.9 jit_solution(15317679260259167615)
XLA Ops:
  0.6 1.5 %copy.31.wo = f32[128,64]{1,0:T(8,128)} copy(f32[128,64]{0,1:T(8,128)} %param.21) | data formatting | bytes 65536 | tf_op args[5]
  2.1 1.7 %copy.32.w2 = f32[512,64]{1,0:T(8,128)} copy(f32[512,64]{0,1:T(8,128)} %param.23) | data formatting | bytes 262144 | tf_op args[7]
  3.9 108.5 %whole_layer.1 = (bf16[512,512]{1,0:T(8,128)(2,1)}, bf16[512,512]{1,0:T(8,128)(2,1)}, f32[64,128]{1,0:T(8,128)}, f32[64,128]{1,0:T(8,128)}, f32[64,128]{1,0:T(8,...) custom-call(bf16[512,512]{1,0:T(8,128)(2,1)} %tokens.1, ...), custom_call_target="tpu_custom_call" | custom-call | tf_op jit(solution)/shard_map/whole_layer/pallas_call | solution.py:1029
  112.4 1.6 %copy.33 = f32[128,64]{0,1:T(8,128)} copy(f32[128,64]{1,0:T(8,128)} %get-tuple-element.50) | data formatting | bytes 65536
  114.0 1.7 %copy.34 = f32[512,64]{0,1:T(8,128)} copy(f32[512,64]{1,0:T(8,128)} %get-tuple-element.52) | data formatting | bytes 262144
  115.7 0.8 copy.48
  116.5 0.4 copy-done
  116.9 0.8 copy.49
  117.7 0.6 copy.50
  118.3 0.6 copy.51
  119.0 0.6 copy.52
  119.6 0.7 copy.53
  120.3 0.6 copy.54
  121.0 0.6 copy.55
  121.5 0.1 copy-done.11
  121.6 0.6 copy.56
  122.2 0.1 copy-done.10
  122.3 0.6 copy.57
  122.9 0.1 copy-done.9
  123.0 0.6 copy.58
  123.6 0.1 copy-done.8
  123.6 0.6 copy.59
  124.2 0.1 copy-done.7
  124.3 0.6 copy.60
  (20 shorter events, 0.1 us)
Async XLA Ops:
  112.4 3.3 %copy-start.1 = (bf16[512,512]{1,0:T(8,128)(2,1)S(1)}, bf16[512,512]{1,0:T(8,128)(2,1)}, u32[]{:S(2)}) copy-start(bf16[512,512]{1,0:T(8,128)(2,1)} %get-tuple-element.75) | copy-start | bytes 1572868
  115.7 1.2 copy-start
  116.9 0.8 copy-start.5
  116.9 1.4 %copy-start.4 = (f32[64,128]{1,0:T(8,128)S(1)}, f32[64,128]{1,0:T(8,128)}, u32[]{:S(2)}) copy-start(f32[64,128]{1,0:T(8,128)} %get-tuple-element.78) | copy-start | bytes 98308
  116.9 2.0 %copy-start.3 = (f32[64,128]{1,0:T(8,128)S(1)}, f32[64,128]{1,0:T(8,128)}, u32[]{:S(2)}) copy-start(f32[64,128]{1,0:T(8,128)} %get-tuple-element.79) | copy-start | bytes 98308
  117.7 1.9 %copy-start.2 = (f32[64,512]{1,0:T(8,128)S(1)}, f32[64,512]{1,0:T(8,128)}, u32[]{:S(2)}) copy-start(f32[64,512]{1,0:T(8,128)} %get-tuple-element.81) | copy-start | bytes 393220
  119.6 0.7 copy-start.6
  120.3 0.7 copy-start.12
  120.9 0.7 copy-start.11
  121.6 0.7 copy-start.10
  122.3 0.7 copy-start.9
  123.0 0.7 copy-start.8
  123.6 0.7 copy-start.7

commit v3 on v2

v3 whole, which is shorter than its diff:
```python
import functools

import jax
import jax.numpy as jnp
from jax import lax
from jax.experimental import pallas as pl
from jax.experimental.pallas import tpu as pltpu
from jax.sharding import PartitionSpec as P

HEAD = 64
LANES = 128
EPSILON = 1e-05
MESH = pl.DeviceIdType.MESH
F32 = jnp.float32
BF16 = jnp.bfloat16
OUTER = 4
EVEN_WAYS = ((0, 1), (2, 3))
WIDE_WAYS = ((0, 1, 3), (2,))
VMEM_LIMIT = 56 << 20


def nn(a, b):
    return lax.dot_general(a, b, (((1,), (0,)), ((), ())), preferred_element_type=F32)


def nt(a, b):
    return lax.dot_general(a, b, (((1,), (1,)), ((), ())), preferred_element_type=F32)


def tn(a, b):
    return lax.dot_general(a, b, (((0,), (0,)), ((), ())), preferred_element_type=F32)


class Place:
    def __init__(self, dp_size, tensor_size):
        self.nd, self.nt = dp_size, tensor_size
        self.inner, self.ny = dp_size // OUTER, tensor_size // 2
        self.d, self.t = lax.axis_index("dp"), lax.axis_index("tensor")
        self.o, self.i = self.d // self.inner, self.d % self.inner
        self.y, self.c = self.t // 2, self.t % 2
        self.barrier = pltpu.get_barrier_semaphore()

    def at(self, do=0, di=0, dy=0, dc=0):
        o, i = (self.o + do) % OUTER, (self.i + di) % self.inner
        return self.to(o, i, (self.y + dy) % self.ny, (self.c + dc) % 2)

    def to(self, o, i, y, c):
        return (o * self.inner + i, y * 2 + c)

    def nearest(self, k):
        if k == 0:
            return self.o
        high = self.o // 2
        edge = self.o + high * (3 - 2 * self.o)
        place = k * (1 - edge) + (k // 2) * k * edge
        return place + high * (3 - 2 * place)

    def outer_peers(self):
        return [(k, 0, 0, 0) for k in range(1, OUTER)]

    def plane_peers(self):
        return [
            (0, di, dy, 0) for di in range(self.inner) for dy in range(self.ny) if di or dy
        ]

    def peers(self):
        return self.outer_peers() + [
            (0, di, dy, dc)
            for di in range(self.inner)
            for dy in range(self.ny)
            for dc in range(2)
            if di or dy or dc
        ]

    def greet(self):
        for peer in self.peers():
            pl.semaphore_signal(
                self.barrier, inc=1, device_id=self.at(*peer), device_id_type=MESH
            )

    def meet(self):
        pl.semaphore_wait(self.barrier, len(self.peers()))


def remote(src, dst, send, recv, peer):
    return pltpu.make_async_remote_copy(
        src_ref=src,
        dst_ref=dst,
        send_sem=send,
        recv_sem=recv,
        device_id=peer,
        device_id_type=MESH,
    )


class Sender:
    def __init__(self, place, send):
        self.p, self.send, self.started = place, send, []

    def go(self, src, dst, recv, peer):
        copy = remote(src, dst, self.send.at[len(self.started)], recv, peer)
        copy.start()
        self.started.append(copy)

    def got(self, block, recv):
        remote(block, block, self.send.at[0], recv, self.p.at()).wait_recv()

    def finish(self):
        for copy in self.started:
            copy.wait_send()


class Gather(Sender):
    def __init__(self, place, held, sems):
        super().__init__(place, sems[0])
        self.held = held
        self.got_outer, self.got_i, self.got_y, self.got_d, self.got_core = sems[1:]

    def _block(self, k, i, y):
        p = self.p
        return self.held.at[y * 2 + p.c, p.nearest(k), i]

    def outer_start(self):
        p = self.p
        mine = self._block(0, p.i, p.y)
        for k in range(1, OUTER):
            to = p.to(p.nearest(k), p.i, p.y, p.c)
            self.go(mine, mine, self.got_outer.at[p.o], to)

    def spread(self, k):
        p = self.p
        block = self._block(k, p.i, p.y)
        if k:
            self.got(block, self.got_outer.at[p.nearest(k)])
        for di in range(1, p.inner):
            self.go(block, block, self.got_i.at[di - 1, k], p.at(di=di))
        for dy in range(1, p.ny):
            self.go(block, block, self.got_y.at[dy - 1, k], p.at(dy=dy))
        self.go(block, block, self.got_core.at[p.y], p.at(dc=1))

    def turn(self, k):
        p = self.p
        for di in range(1, p.inner):
            block = self._block(k, (p.i + p.inner - di) % p.inner, p.y)
            self.got(block, self.got_i.at[di - 1, k])
            if k < 2:
                for dy in range(1, p.ny):
                    self.go(block, block, self.got_d.at[di - 1, dy - 1, k], p.at(dy=dy))
            self.go(block, block, self.got_core.at[p.y], p.at(dc=1))
        for dy in range(1, p.ny):
            y = (p.y + p.ny - dy) % p.ny
            block = self._block(k, p.i, y)
            self.got(block, self.got_y.at[dy - 1, k])
            if k >= 2:
                for di in range(1, p.inner):
                    self.go(block, block, self.got_d.at[di - 1, dy - 1, k], p.at(di=di))
            self.go(block, block, self.got_core.at[y], p.at(dc=1))

    def corner(self, k):
        p = self.p
        for di in range(1, p.inner):
            for dy in range(1, p.ny):
                y = (p.y + p.ny - dy) % p.ny
                block = self._block(k, (p.i + p.inner - di) % p.inner, y)
                self.got(block, self.got_d.at[di - 1, dy - 1, k])
                self.go(block, block, self.got_core.at[y], p.at(dc=1))

    def core_done(self, dy):
        p = self.p
        y = (p.y + dy) % p.ny
        self.got(self.held.at[y * 2 + 1 - p.c], self.got_core.at[y])

    @staticmethod
    def semaphores(nd, nt_):
        di, dy = nd // OUTER - 1, nt_ // 2 - 1
        sends = (OUTER - 1) + OUTER * (di + dy + 1 + di + dy) + 2 * OUTER * di * dy
        return [
            pltpu.SemaphoreType.DMA((sends,)),
            pltpu.SemaphoreType.DMA((OUTER,)),
            pltpu.SemaphoreType.DMA((di, OUTER)),
            pltpu.SemaphoreType.DMA((dy, OUTER)),
            pltpu.SemaphoreType.DMA((di, dy, OUTER)),
            pltpu.SemaphoreType.DMA((nt_ // 2,)),
        ]


class Scatter(Sender):
    def __init__(self, place, by_i, by_y, bufs, sems):
        super().__init__(place, sems[0])
        self.by_i, self.by_y = by_i, by_y
        (self.give, self.core, self.in_i, self.in_y, self.sum_i, self.sum_y,
         self.then_y, self.then_i, self.own, self.outer) = bufs
        self.got_core, self.got_i, self.got_y, self.got_ty, self.got_ti, self.got_outer = sems[1:]

    def core_send(self, y):
        self.go(self.give.at[y], self.core.at[y], self.got_core.at[y], self.p.at(dc=1))

    def core_wait(self, y):
        self.got(self.core.at[y], self.got_core.at[y])

    def first_i(self, dy, k):
        p, at = self.p, self.by_i.index(k)
        y, o = (p.y + dy) % p.ny, (p.o + k) % OUTER
        for di in range(1, p.inner):
            self.go(
                self.core.at[y, o, (p.i + di) % p.inner], self.in_i.at[di - 1, at, dy],
                self.got_i.at[di - 1, at, dy], p.at(di=di),
            )

    def first_y(self, dy, k, di):
        p, at = self.p, self.by_y.index(k)
        y, o, i = (p.y + dy) % p.ny, (p.o + k) % OUTER, (p.i + di) % p.inner
        self.go(
            self.core.at[y, o, i], self.in_y.at[dy - 1, at, di],
            self.got_y.at[dy - 1, at, di], p.at(dy=dy),
        )

    def first(self, dy):
        for k in self.by_y:
            for di in range(self.p.inner) if dy else ():
                self.first_y(dy, k, di)
        for k in self.by_i:
            self.first_i(dy, k)

    def second_y(self, k):
        p, at = self.p, self.by_y.index(k)
        o = (p.o + k) % OUTER
        for di in list(range(1, p.inner)) + [0]:
            total = self.core[p.y, o, (p.i + di) % p.inner].astype(F32)
            for dy in range(1, p.ny):
                block = self.in_y.at[dy - 1, at, di]
                self.got(block, self.got_y.at[dy - 1, at, di])
                total = total + block[...].astype(F32)
            self.sum_y[at, di] = total.astype(BF16)
            if di:
                self.go(
                    self.sum_y.at[at, di], self.then_i.at[di - 1, at],
                    self.got_ti.at[di - 1, at], p.at(di=di),
                )

    def second_i(self, k, dy):
        p, at = self.p, self.by_i.index(k)
        total = self.core[(p.y + dy) % p.ny, (p.o + k) % OUTER, p.i].astype(F32)
        for di in range(1, p.inner):
            block = self.in_i.at[di - 1, at, dy]
            self.got(block, self.got_i.at[di - 1, at, dy])
            total = total + block[...].astype(F32)
        self.sum_i[at, dy] = total.astype(BF16)
        if dy:
            self.go(
                self.sum_i.at[at, dy], self.then_y.at[dy - 1, at],
                self.got_ty.at[dy - 1, at], p.at(dy=dy),
            )

    def second(self):
        for k in self.by_y:
            self.second_y(k)
        for dy in list(range(1, self.p.ny)) + [0]:
            for k in self.by_i:
                self.second_i(k, dy)

    def third(self, k):
        p = self.p
        if k in self.by_i:
            at, count, place, sems = self.by_i.index(k), p.ny, self.then_y, self.got_ty
            total = self.sum_i[at, 0].astype(F32)
        else:
            at, count, place, sems = self.by_y.index(k), p.inner, self.then_i, self.got_ti
            total = self.sum_y[at, 0].astype(F32)
        for j in range(count - 1):
            self.got(place.at[j, at], sems.at[j, at])
            total = total + place[j, at].astype(F32)
        self.own[k] = total.astype(BF16)
        if k:
            self.go(self.own.at[k], self.outer.at[k - 1], self.got_outer.at[k - 1], p.at(do=k))

    def last(self):
        total = self.own[0].astype(F32)
        for k in range(1, OUTER):
            self.got(self.outer.at[k - 1], self.got_outer.at[k - 1])
            total = total + self.outer[k - 1].astype(F32)
        return total

    @staticmethod
    def scratch(nd, nt_, by_i, by_y, rows, columns):
        inner, ny = nd // OUTER, nt_ // 2
        ki, ky = len(by_i), len(by_y)
        leads = [
            (ny, OUTER, inner), (ny, OUTER, inner), (inner - 1, ki, ny), (ny - 1, ky, inner),
            (ki, ny), (ky, inner), (ny - 1, ki), (inner - 1, ky), (OUTER,), (OUTER - 1,),
        ]
        return [pltpu.VMEM(lead + (rows, columns), BF16) for lead in leads]

    @staticmethod
    def semaphores(nd, nt_, by_i, by_y):
        inner, ny = nd // OUTER, nt_ // 2
        di, dy, ki, ky = inner - 1, ny - 1, len(by_i), len(by_y)
        sends = ny + ky * dy * inner + ki * di * ny + ky * di + ki * dy + OUTER - 1
        shapes = [
            (sends,), (ny,), (di, ki, ny), (dy, ky, inner), (dy, ki), (di, ky), (OUTER - 1,),
        ]
        return [pltpu.SemaphoreType.DMA(shape) for shape in shapes]


class Exchange(Sender):
    def __init__(self, place, back, bufs, sems):
        super().__init__(place, sems[0])
        self.back = back
        self.own, self.near, self.far, self.made, self.entering = bufs
        self.s_near, self.s_far, self.s_enter = sems[1:]
        self.rows = HEAD // place.inner
        self.members = place.inner * place.nt
        self.me = place.i * place.nt + place.t

    def put(self, g, packed, total, edge, inlet):
        p = self.p
        row = lax.broadcasted_iota(jnp.int32, (8, LANES), 0)
        foot = jnp.where(row == 0, total, jnp.where(row == 1, edge, inlet))
        for sub in range(p.inner):
            self.own[g * p.inner + sub, : self.rows, :] = packed[
                sub * self.rows : (sub + 1) * self.rows
            ]
            self.own[g * p.inner + sub, self.rows :, :] = foot

    def state(self, g):
        p = self.p
        at = pl.ds(g * p.inner, p.inner)
        packed = self.entering[at, : self.rows, :].reshape(HEAD, LANES)
        return packed, self.entering[g * p.inner, self.rows :, :]

    def _peers(self):
        p = self.p
        return [
            (di, dy, dc)
            for di in range(p.inner) for dy in range(p.ny) for dc in range(2) if di or dy or dc
        ]

    def _member(self, di, dy, dc):
        p = self.p
        i, y = (p.i + p.inner - di) % p.inner, (p.y + p.ny - dy) % p.ny
        return i * p.nt + y * 2 + (p.c + dc) % 2

    def _edge(self, block):
        return block[self.rows + 1 : self.rows + 2, :]

    def _inlet(self, block):
        return block[self.rows + 2 : self.rows + 3, :]

    def _hand(self, blocks, place, sems):
        p = self.p
        for di, dy, dc in self._peers():
            to = p.at(0, di, dy, dc)
            member = (to[0] % p.inner) * p.nt + to[1]
            self.go(blocks.at[member], place.at[self.me], sems.at[self.me], to)
        place[self.me] = blocks[self.me]

    def step_near(self):
        self._hand(self.own, self.near, self.s_near)

    def step_far(self):
        p = self.p
        for peer in self._peers():
            m = self._member(*peer)
            self.got(self.near.at[m], self.s_near.at[m])
        border = self.near[0 if self.back else self.members - 1]
        total = jnp.zeros_like(border)
        for j in range(self.members):
            block = self.near[j]
            total = total + jnp.where(self._edge(block) == self._edge(border), block, 0.0)
        row = lax.broadcasted_iota(jnp.int32, total.shape, 0)
        self.far[p.o] = jnp.where(row > self.rows, border, total)
        for k in range(1, OUTER):
            o = p.nearest(k)
            self.go(self.far.at[p.o], self.far.at[p.o], self.s_far.at[p.o], p.to(o, p.i, p.y, p.c))

    def step_enter(self):
        p = self.p
        for k in range(1, OUTER):
            o = p.nearest(k)
            self.got(self.far.at[o], self.s_far.at[o])
        order = list(range(self.members))
        if self.back:
            order.reverse()
        inlet = self._inlet(self.near[order[0]])
        incoming = jnp.zeros(self.near.shape[1:], F32)
        for o in range(OUTER):
            block = self.far[o]
            ids = jnp.where(o > p.o if self.back else o < p.o, self._edge(block), -1.0)
            incoming = incoming + jnp.where(ids == inlet, block, 0.0)
        for place, j in enumerate(order):
            block = self.near[j]
            if place:
                inlet = self._inlet(block)
                incoming = jnp.where(edge == inlet, running, 0.0)
            self.made[j] = incoming
            edge = self._edge(block)
            running = block + jnp.where(edge == inlet, incoming, 0.0)
        self._hand(self.made, self.entering, self.s_enter)

    def arrive(self):
        for peer in self._peers():
            m = self._member(*peer)
            self.got(self.entering.at[m], self.s_enter.at[m])

    @staticmethod
    def scratch(nd, nt_):
        inner = nd // OUTER
        shape = (HEAD // inner + 8, LANES)
        counts = [inner * nt_, inner * nt_, OUTER, inner * nt_, inner * nt_]
        return [pltpu.VMEM((count,) + shape, F32) for count in counts]

    @staticmethod
    def semaphores(nd, nt_):
        members = nd // OUTER * nt_
        counts = [2 * (members - 1) + OUTER - 1, members, OUTER, members]
        return [pltpu.SemaphoreType.DMA((count,)) for count in counts]


def left_lanes(shape):
    return lax.broadcasted_iota(jnp.int32, shape, len(shape) - 1) < HEAD


def split_heads(block, fill):
    left = left_lanes(block.shape)
    other = jnp.full_like(block, fill)
    return jnp.where(left, block, other), jnp.where(left, other, block)


def feature(values):
    return jnp.where(values > 0.0, values + 1.0, jnp.exp(jnp.minimum(values, 0.0)))


def pack_state(product):
    left = left_lanes((HEAD, LANES))
    return jnp.where(left, product[:HEAD], product[HEAD:])


def wide_state(packed):
    left = left_lanes((HEAD, LANES))
    zero = jnp.zeros_like(packed)
    return jnp.concatenate([jnp.where(left, packed, zero), jnp.where(left, zero, packed)], axis=0)


def two_parts(values):
    high = values.astype(BF16)
    return high, (values - high.astype(F32)).astype(BF16)


def same_head():
    row = lax.broadcasted_iota(jnp.int32, (LANES, LANES), 0) < HEAD
    return row == left_lanes((LANES, LANES))


class Total(Sender):
    def __init__(self, place, bufs, sems):
        super().__init__(place, sems[0])
        self.mine, self.core, self.plane, self.outer, self.whole = bufs
        self.got_core, self.got_plane, self.got_outer, self.got_whole = sems[1:]

    def start(self, value):
        p = self.p
        self.mine[...] = value.reshape(self.mine.shape)
        self.go(self.mine.at[1 - p.c], self.core, self.got_core.at[0], p.at(dc=1))

    def plane_step(self):
        p = self.p
        self.got(self.core, self.got_core.at[0])
        here = p.i * p.ny + p.y
        self.plane[here] = self.mine[p.c] + self.core[...]
        for peer in p.plane_peers():
            self.go(
                self.plane.at[here], self.plane.at[here], self.got_plane.at[here], p.at(*peer)
            )

    def outer_step(self):
        p = self.p
        for _, di, dy, _ in p.plane_peers():
            place = (p.i + p.inner - di) % p.inner * p.ny + (p.y + p.ny - dy) % p.ny
            self.got(self.plane.at[place], self.got_plane.at[place])
        total = self.plane[0]
        for k in range(1, p.inner * p.ny):
            total = total + self.plane[k]
        self.outer[p.o] = total
        for k in range(1, OUTER):
            to = p.to(p.nearest(k), p.i, p.y, p.c)
            self.go(self.outer.at[p.o], self.outer.at[p.o], self.got_outer.at[p.o], to)

    def core_step(self):
        p = self.p
        for k in range(1, OUTER):
            o = p.nearest(k)
            self.got(self.outer.at[o], self.got_outer.at[o])
        total = self.outer[0]
        for k in range(1, OUTER):
            total = total + self.outer[k]
        self.whole[p.c] = total
        self.go(self.whole.at[p.c], self.whole.at[p.c], self.got_whole.at[p.c], p.at(dc=1))

    def result(self):
        other = 1 - self.p.c
        self.got(self.whole.at[other], self.got_whole.at[other])
        return self.whole[...].reshape(-1, self.whole.shape[-1])

    @staticmethod
    def scratch(nd, nt_, rows, columns):
        leads = [(2,), (), (nd // OUTER * (nt_ // 2),), (OUTER,), (2,)]
        return [pltpu.VMEM(lead + (rows // 2, columns), F32) for lead in leads]

    @staticmethod
    def semaphores(nd, nt_):
        plane = nd // OUTER * (nt_ // 2)
        counts = [plane + OUTER, 1, plane, OUTER, 2]
        return [pltpu.SemaphoreType.DMA((count,)) for count in counts]


def kernel_whole(
    nd, nt_,
    tokens_in, segments, wq_in, wk_in, wv_in, wo_in, w1_in, w2_in,
    inner_bias, gain1, shift1, gain2, shift2, mixer_bias, outer_bias, cotangent_in,
    out_to, tokens_to, grad_q, grad_k, grad_v, grad_o, grad_1, grad_2,
    grad_ib, grad_g1, grad_s1, grad_g2, grad_s2, grad_mb, grad_ob,
    *scratch,
):
    it = iter(scratch)

    def take(count):
        return [next(it) for _ in range(count)]

    (held_kv, held_qo, held_2, held_1) = take(4)
    (tokens, wq, wk, wv, wo, w1, w2, cotangent, out, grad_tokens) = take(10)
    (segc, mask, normed, normed_t, fq, fk, vb, num_s, den_s) = take(9)
    (res, unit, inv, h2, h2t, cot, dh2, act, dhid, dbt) = take(10)
    (do, dr, gn, gd, dk_s, dv_s, dq_s, dkv_s, dh1, sums, first_sums) = take(11)
    bufs_x, bufs_xb = take(5), take(5)
    bufs_f, bufs_qo, bufs_kv = take(10), take(10), take(10)
    bufs_t1, bufs_t2 = take(5), take(5)
    p = Place(nd, nt_)
    kv, qo = Gather(p, held_kv, take(6)), Gather(p, held_qo, take(6))
    g2, g1 = Gather(p, held_2, take(6)), Gather(p, held_1, take(6))
    ex = Exchange(p, False, bufs_x, take(4))
    xb = Exchange(p, True, bufs_xb, take(4))
    sf = Scatter(p, *WIDE_WAYS, bufs_f, take(7))
    sqo = Scatter(p, *EVEN_WAYS, bufs_qo, take(7))
    skv = Scatter(p, *EVEN_WAYS, bufs_kv, take(7))
    all_sum, first_sum = Total(p, bufs_t1, take(5)), Total(p, bufs_t2, take(5))

    rows_all, width = tokens.shape
    head, hidden = wq.shape[1], w1.shape[1]
    part_rows = wq.shape[0]
    block_shape = (OUTER, p.inner, part_rows)
    step, block = 128, min(256, rows_all)

    (in_sems, out_sems) = take(2)
    p.greet()
    loads = [
        pltpu.make_async_copy(src, dst, in_sems.at[n])
        for n, (src, dst) in enumerate((
            (wk_in, wk), (wv_in, wv), (tokens_in, tokens), (wq_in, wq), (wo_in, wo),
            (w2_in, w2), (w1_in, w1), (cotangent_in, cotangent),
        ))
    ]
    for load in loads:
        load.start()
    here = (p.t, p.o, p.i)
    if head < LANES:
        blank = jnp.zeros((part_rows, 2 * LANES), BF16)
        held_kv[here] = blank
        held_qo[here] = blank
    loads[0].wait()
    loads[1].wait()
    held_kv[here + (slice(None), slice(0, head))] = wk[...].astype(BF16)
    held_kv[here + (slice(None), slice(LANES, LANES + head))] = wv[...].astype(BF16)
    for load in loads[3:7]:
        load.wait()
    held_qo[here + (slice(None), slice(0, head))] = wq[...].astype(BF16)
    held_qo[here + (slice(None), slice(LANES, LANES + head))] = wo[...].astype(BF16)
    held_2[here] = w2[...].astype(BF16)
    held_1[here] = w1[...].astype(BF16)
    loads[2].wait()
    segr = segments[:, pl.ds(pl.multiple_of(p.t * rows_all, LANES), rows_all)].astype(F32)
    for start in range(0, rows_all, LANES):
        wide = jnp.broadcast_to(segr[:, start : start + LANES], (8, LANES))
        segc[start : start + LANES, :] = jnp.transpose(wide)[:, 0:1]
    first_id, last_id = segr[:, 0:1], segr[:, rows_all - 1 : rows_all]

    def norm(k, _):
        at = pl.ds(pl.multiple_of(k * step, step), step)
        x = tokens[at, :].astype(F32)
        center = x - jnp.mean(x, axis=-1, keepdims=True)
        spread = jnp.mean(center * center, axis=-1, keepdims=True)
        y = center * lax.rsqrt(spread + EPSILON) * gain1[...] + shift1[...]
        normed[at, :] = y.astype(BF16)
        normed_t[:, at] = jnp.transpose(y).astype(BF16)
        return 0

    lax.fori_loop(0, rows_all // step, norm, 0)
    for start in range(0, rows_all, 128):
        later = lax.broadcasted_iota(jnp.int32, (128, rows_all), 0) + start
        earlier = lax.broadcasted_iota(jnp.int32, (128, rows_all), 1)
        same = segc[start : start + 128, :] == segr
        mask[start : start + 128, :] = jnp.where((later >= earlier) & same, 1.0, 0.0).astype(BF16)
    p.meet()
    kv.outer_start()
    kv.spread(0)
    qo.outer_start()
    qo.spread(0)
    g2.outer_start()
    g2.spread(0)
    g1.outer_start()
    for k in range(1, OUTER):
        kv.spread(k)
    g1.spread(0)
    for k in range(OUTER):
        kv.turn(k)
    for k in range(1, OUTER):
        qo.spread(k)
    for k in range(OUTER):
        kv.corner(k)
    for dy in range(p.ny):
        kv.core_done(dy)

    def keys_values(g, _):
        w = held_kv[g].reshape(width, 2 * LANES)
        both = nn(normed[...], w)
        keys = feature(both[:, :LANES]).astype(BF16)
        values = both[:, LANES:].astype(BF16)
        fk[g] = keys
        vb[g] = values
        kept = jnp.where(segc[...] == last_id, keys, jnp.zeros_like(keys))
        total = jnp.sum(kept.astype(F32), axis=0, keepdims=True)
        ex.put(g, pack_state(tn(kept, values)), total, last_id, first_id)
        return 0

    lax.fori_loop(0, nt_, keys_values, 0)
    ex.step_near()
    for k in range(OUTER):
        qo.turn(k)
    for k in range(1, OUTER):
        g2.spread(k)
    loads[7].wait()
    for start in range(0, rows_all, step):
        turned = jnp.transpose(cotangent[start : start + step, :].astype(F32))
        cot[:, start : start + step] = turned.astype(BF16)
    ex.step_far()
    g1.spread(1)
    for k in range(OUTER):
        qo.corner(k)
    for dy in range(p.ny):
        qo.core_done(dy)

    def queries(g, _):
        w = held_qo[g].reshape(width, 2 * LANES)
        fq[g] = feature(nn(normed[...], w[:, :LANES])).astype(BF16)
        return 0

    lax.fori_loop(0, nt_, queries, 0)

    def inside(g, _):
        values = split_heads(vb[g], 1.0)
        for start in range(0, rows_all, block):
            end = start + block
            now = mask[start:end, :end]
            query = split_heads(fq[g, start:end, :], 0.0)
            keys = fk[g, :end, :]
            parts = []
            for h in range(2):
                scores = nt(query[h], keys).astype(BF16) * now
                parts.append(nn(scores, values[h][:end]))
            left = left_lanes(parts[0].shape)
            num_s[g, start:end, :] = jnp.where(left, parts[0], parts[1])
            den_s[g, start:end, :] = pltpu.roll(
                jnp.where(left, parts[1], parts[0]), HEAD, 1
            )
        return 0

    lax.fori_loop(0, nt_ // 2, inside, 0)
    ex.step_enter()
    for k in range(2, OUTER):
        g1.spread(k)
    for k in range(OUTER):
        g2.turn(k)
    lax.fori_loop(nt_ // 2, nt_, inside, 0)
    for k in range(2):
        g1.turn(k)
    ex.arrive()

    def outside(g, _):
        packed, foot = ex.state(g)
        high, low = two_parts(wide_state(packed))
        total = jnp.broadcast_to(jnp.transpose(foot)[:, 0:1], (LANES, LANES))
        sum_high, sum_low = two_parts(jnp.where(same_head(), total, 0.0))
        query = fq[g]
        query = jnp.where(segc[...] == first_id, query, jnp.zeros_like(query))
        num = num_s[g] + (nn(query, high) + nn(query, low))
        den = den_s[g] + (nn(query, sum_high) + nn(query, sum_low))
        inverse = 1.0 / den
        den_s[g] = inverse
        num_s[g] = num * inverse
        return 0

    lax.fori_loop(0, nt_, outside, 0)
    mixed, rden = num_s, den_s
    for k in range(2, OUTER):
        g1.turn(k)

    def output_weight(g):
        return held_qo[g, :, :, :, LANES:].reshape(width, LANES)

    def enter(k, _):
        at = pl.ds(pl.multiple_of(k * step, step), step)
        r = tokens[at, :].astype(F32) + mixer_bias[...]
        for g in range(nt_):
            r = r + nt(mixed[g, at, :].astype(BF16), output_weight(g))
        center = r - jnp.mean(r, axis=-1, keepdims=True)
        spread = jnp.mean(center * center, axis=-1, keepdims=True)
        scale = lax.rsqrt(spread + EPSILON)
        n = center * scale
        y = n * gain2[...] + shift2[...]
        res[at, :] = r + outer_bias[...]
        unit[at, :] = n
        inv[at, :] = scale
        h2[at, :] = y.astype(BF16)
        h2t[:, at] = jnp.transpose(y).astype(BF16)
        dh2[at, :] = jnp.zeros((step, width), F32)
        return 0

    lax.fori_loop(0, rows_all // step, enter, 0)
    sums[...] = jnp.zeros_like(sums)
    g2.core_done(0)
    g1.core_done(0)
    tall = width // OUTER

    def feed(g):
        wi = held_1[g].reshape(width, hidden)
        wt = held_2[g].reshape(width, hidden)
        total = jnp.zeros((1, hidden), F32)
        bias = inner_bias[:, pl.ds(pl.multiple_of(g * hidden, LANES), hidden)]
        for start in range(0, rows_all, block):
            end = start + block
            u = nn(h2[start:end, :], wi) + bias
            below = 0.5 * (1.0 + lax.erf(u * 0.7071067811865476))
            slope = below + u * (jnp.exp(-0.5 * (u * u)) * 0.3989422804014327)
            a = (u * below).astype(BF16)
            du = (nn(cotangent[start:end, :], wt) * slope).astype(BF16)
            act[start:end, :] = a
            dhid[start:end, :] = du
            total = total + jnp.sum(du.astype(F32), axis=0, keepdims=True)
            res[start:end, :] += nt(a, wt)
            dh2[start:end, :] += nt(du, wi)
        sums[pl.ds(8 + g, 1), 0:hidden] = total

    shape = (p.inner, part_rows, hidden)

    def feed_grads(y, mine):
        for o in range(OUTER):
            for s, (left, right) in enumerate(((h2t, dhid), (cot, act))):
                lanes = slice(s * hidden, (s + 1) * hidden)
                value = nn(left[o * tall : (o + 1) * tall, :], right[...]).reshape(shape)
                if mine:
                    value = value + sf.core[y, o, :, :, lanes].astype(F32)
                    sf.core[y, o, :, :, lanes] = value.astype(BF16)
                else:
                    sf.give[y, o, :, :, lanes] = value.astype(BF16)

    for dy in range(p.ny):
        y = (p.y + dy) % p.ny
        if dy:
            g2.core_done(dy)
            g1.core_done(dy)
        feed(y * 2 + 1 - p.c)
        feed_grads(y, False)
        sf.core_send(y)
        if not dy:
            for k in range(OUTER):
                g2.corner(k)
                g1.corner(k)
        feed(y * 2 + p.c)
        sf.core_wait(y)
        feed_grads(y, True)
        if dy:
            sf.first_y(dy, 2, 0)
        else:
            for k in sf.by_i:
                sf.first_i(0, k)

    def leave(k, _):
        at = pl.ds(pl.multiple_of(k * step, step), step)
        out[at, :] = res[at, :].astype(BF16)
        n = unit[at, :]
        grad = dh2[at, :]
        e = cotangent[at, :].astype(F32)
        pushed = grad * gain2[...]
        mean = jnp.mean(pushed, axis=-1, keepdims=True)
        along = jnp.mean(pushed * n, axis=-1, keepdims=True)
        back = e + (pushed - mean - n * along) * inv[at, :]
        dr[at, :] = back
        low = back.astype(BF16)
        wide = low.astype(F32)
        dbt[:, at] = jnp.transpose(wide).astype(BF16)
        for g in range(nt_):
            do[g, at, :] = nn(low, output_weight(g))
        sums[2:3, :] += jnp.sum(grad * n, axis=0, keepdims=True)
        sums[3:4, :] += jnp.sum(grad, axis=0, keepdims=True)
        sums[4:5, :] += jnp.sum(wide, axis=0, keepdims=True)
        sums[5:6, :] += jnp.sum(e, axis=0, keepdims=True)
        return 0

    lax.fori_loop(0, rows_all // step, leave, 0)
    store_out = pltpu.make_async_copy(out, out_to, out_sems.at[0])
    store_out.start()

    def first(g, _):
        low = (do[g] * rden[g]).astype(BF16)
        gn[g] = low
        product = low.astype(F32) * mixed[g]
        left = left_lanes(product.shape)
        zero = jnp.zeros_like(product)
        one = jnp.sum(jnp.where(left, product, zero), axis=-1, keepdims=True)
        two = jnp.sum(jnp.where(left, zero, product), axis=-1, keepdims=True)
        slope = -jnp.where(left, one, two)
        gd[g] = slope
        kept = jnp.where(segc[...] == first_id, fq[g], jnp.zeros_like(low))
        total = jnp.sum(kept.astype(F32) * slope, axis=0, keepdims=True)
        xb.put(g, pack_state(tn(kept, low)), total, first_id, last_id)
        return 0

    lax.fori_loop(0, nt_, first, 0)
    xb.step_near()
    for dy in range(1, p.ny):
        for di in range(1, p.inner):
            sf.first_y(dy, 2, di)
        for k in sf.by_i:
            sf.first_i(dy, k)
    all_sum.start(sums[...])

    def inside_back(g, _):
        values, keys = vb[g], fk[g]
        key_heads = split_heads(keys, 0.0)
        packed, foot = ex.state(g)
        high, low = two_parts(wide_state(packed))
        query_t = jnp.transpose(fq[g].astype(F32)).astype(BF16)
        grad_t = jnp.transpose(gn[g].astype(F32)).astype(BF16)
        dk_t = jnp.zeros((LANES, rows_all), F32)
        dv_t = jnp.zeros((LANES, rows_all), F32)
        for start in range(0, rows_all, block):
            end = start + block
            now = mask[start:end, :end]
            query, grad = fq[g, start:end, :], gn[g, start:end, :]
            slope = gd[g, start:end, :]
            query_heads, grad_heads = split_heads(query, 0.0), split_heads(grad, 0.0)
            dq = jnp.where(
                segc[start:end, :] == first_id,
                nt(grad, high) + nt(grad, low) + slope * foot[0:1, :],
                0.0,
            )
            dk_parts, dv_parts = [], []
            for h in range(2):
                lanes = slice(h * HEAD, h * HEAD + 1)
                part = slice(h * HEAD, (h + 1) * HEAD)
                weight = nt(query_heads[h], keys[:end]).astype(BF16) * now
                share = (nt(grad_heads[h], values[:end]) + slope[:, lanes]).astype(BF16) * now
                dq = dq + nn(share, key_heads[h][:end])
                dk_parts.append(nn(query_t[part, start:end], share))
                dv_parts.append(nn(grad_t[part, start:end], weight))
            dk_now = jnp.concatenate(dk_parts, axis=0)
            dv_now = jnp.concatenate(dv_parts, axis=0)
            if end < rows_all:
                pad = jnp.zeros((LANES, rows_all - end), F32)
                dk_now = jnp.concatenate([dk_now, pad], axis=1)
                dv_now = jnp.concatenate([dv_now, pad], axis=1)
            dk_t, dv_t = dk_t + dk_now, dv_t + dv_now
            dq_s[g, start:end, :] = (dq * jnp.minimum(query.astype(F32), 1.0)).astype(BF16)
        dk_s[g] = jnp.transpose(dk_t)
        dv_s[g] = jnp.transpose(dv_t)
        return 0

    lax.fori_loop(0, nt_ // 2, inside_back, 0)
    xb.step_far()
    all_sum.plane_step()
    for k in sf.by_i:
        sf.second_i(k, 0)
    lax.fori_loop(nt_ // 2, nt_, inside_back, 0)
    for dy in range(1, p.ny):
        sf.second_i(0, dy)
    xb.step_enter()
    sf.second_y(2)
    for dy in range(1, p.ny):
        sf.second_i(1, dy)

    def attention_grads(scatter, dc, joint):
        for dy in list(range(1, p.ny)) + [0]:
            y = (p.y + dy) % p.ny
            g = y * 2 + (p.c + dc) % 2
            values = joint(g)
            if not dc:
                scatter.core_wait(y)
            for s, (left, right) in enumerate(values):
                lanes = slice(s * LANES, (s + 1) * LANES)
                value = nn(left, right).reshape(block_shape + (LANES,))
                if dc:
                    scatter.give[y, :, :, :, lanes] = value.astype(BF16)
                else:
                    value = value + scatter.core[y, :, :, :, lanes].astype(F32)
                    scatter.core[y, :, :, :, lanes] = value.astype(BF16)
            if dc:
                scatter.core_send(y)
            else:
                scatter.first(dy)

    def query_output(g):
        return ((normed_t[...], dq_s[g]), (dbt[...], mixed[g].astype(BF16)))

    attention_grads(sqo, 1, query_output)
    attention_grads(sqo, 0, query_output)
    all_sum.outer_step()

    def query_back(g, _):
        dh1[...] += nt(dq_s[g], held_qo[g, :, :, :, :LANES].reshape(width, LANES))
        return 0

    dh1[...] = jnp.zeros_like(dh1)
    lax.fori_loop(0, nt_, query_back, 0)
    for dy in range(1, p.ny):
        sf.second_i(3, dy)
    xb.arrive()

    def key_value(g):
        packed, foot = xb.state(g)
        high, low = two_parts(wide_state(packed))
        keys, values = fk[g], vb[g]
        dk = nt(values, high) + nt(values, low) + foot[0:1, :]
        dv = nn(keys, high) + nn(keys, low)
        closing = segc[...] == last_id
        dk = dk_s[g] + jnp.where(closing, dk, 0.0)
        dv = dv_s[g] + jnp.where(closing, dv, 0.0)
        dk = (dk * jnp.minimum(keys.astype(F32), 1.0)).astype(BF16)
        dv = dv.astype(BF16)
        dkv_s[g, :, :LANES] = dk
        dkv_s[g, :, LANES:] = dv
        return ((normed_t[...], dk), (normed_t[...], dv))

    attention_grads(skv, 1, key_value)
    sf.third(2)
    sf.third(1)
    attention_grads(skv, 0, key_value)
    sf.third(3)

    def key_value_back(g, _):
        dh1[...] += nt(dkv_s[g], held_kv[g].reshape(width, 2 * LANES))
        return 0

    lax.fori_loop(0, nt_, key_value_back, 0)
    first_sums[...] = jnp.zeros_like(first_sums)

    def finish(k, _):
        at = pl.ds(pl.multiple_of(k * step, step), step)
        x = tokens[at, :].astype(F32)
        center = x - jnp.mean(x, axis=-1, keepdims=True)
        spread = jnp.mean(center * center, axis=-1, keepdims=True)
        scale = lax.rsqrt(spread + EPSILON)
        n = center * scale
        grad = dh1[at, :]
        pushed = grad * gain1[...]
        mean = jnp.mean(pushed, axis=-1, keepdims=True)
        along = jnp.mean(pushed * n, axis=-1, keepdims=True)
        back = (pushed - mean - n * along) * scale
        grad_tokens[at, :] = (dr[at, :] + back).astype(BF16)
        first_sums[0:1, :] += jnp.sum(grad * n, axis=0, keepdims=True)
        first_sums[8:9, :] += jnp.sum(grad, axis=0, keepdims=True)
        return 0

    lax.fori_loop(0, rows_all // step, finish, 0)
    store_tokens = pltpu.make_async_copy(grad_tokens, tokens_to, out_sems.at[1])
    store_tokens.start()
    first_sum.start(first_sums[...])
    sqo.second()
    first_sum.plane_step()
    skv.second()
    for k in (2, 3, 1):
        sqo.third(k)
    for k in (2, 3, 1):
        skv.third(k)
    first_sum.outer_step()
    for scatter in (sf, sqo, skv):
        scatter.third(0)
    all_sum.core_step()
    total = sf.last()
    grad_1[...] = total[:, :hidden]
    grad_2[...] = total[:, hidden:]
    total = sqo.last()
    grad_q[...] = total[:, :head]
    grad_o[...] = total[:, LANES : LANES + head]
    first_sum.core_step()
    total = all_sum.result()
    grad_g2[...] = total[2:3, :]
    grad_s2[...] = total[3:4, :]
    grad_mb[...] = total[4:5, :]
    grad_ob[...] = total[5:6, :]
    for g in range(nt_):
        grad_ib[:, g * hidden : (g + 1) * hidden] = total[8 + g : 9 + g, :hidden]
    total = skv.last()
    grad_k[...] = total[:, :head]
    grad_v[...] = total[:, LANES : LANES + head]
    total = first_sum.result()
    grad_g1[...] = total[0:1, :]
    grad_s1[...] = total[8:9, :]
    store_out.wait()
    store_tokens.wait()
    for each in (kv, qo, g2, g1, ex, xb, sf, sqo, skv, all_sum, first_sum):
        each.finish()


def kernel_outputs(count, *refs):
    given, made, held = (refs[k * count : (k + 1) * count] for k in range(3))
    loaded, stored = refs[3 * count :]
    loads = [pltpu.make_async_copy(given[k], held[k], loaded.at[k]) for k in range(count)]
    stores = [pltpu.make_async_copy(held[k], made[k], stored.at[k]) for k in range(count)]
    for load in loads:
        load.start()
    for load, store in zip(loads, stores):
        load.wait()
        store.start()
    for store in stores:
        store.wait()


def local(nd, nt_, *args):
    (tokens, segments, wq, wk, wv, wo, w1, w2, inner_bias, *vectors, cotangent) = args
    rows, width = tokens.shape
    inner = nd // OUTER
    part_rows, hidden = w1.shape
    vm, hbm = (pl.BlockSpec(memory_space=space) for space in (pltpu.VMEM, pl.ANY))
    group = (nt_, rows, LANES)
    total_rows = 8 + max(8, nt_)
    head = wq.shape[1]
    row = jax.ShapeDtypeStruct((1, width), F32)
    narrow = jax.ShapeDtypeStruct((part_rows, head), F32)
    wide = jax.ShapeDtypeStruct((part_rows, hidden), F32)
    outs = [
        jax.ShapeDtypeStruct(tokens.shape, BF16),
        jax.ShapeDtypeStruct(tokens.shape, BF16),
        narrow, narrow, narrow, narrow, wide, wide,
        jax.ShapeDtypeStruct((1, nt_ * hidden), F32),
        *[row] * 6,
    ]
    held = (nt_, OUTER, inner, part_rows)
    square = (rows, width)
    scratch = [
        pltpu.VMEM(held + (2 * LANES,), BF16),
        pltpu.VMEM(held + (2 * LANES,), BF16),
        pltpu.VMEM(held + (hidden,), BF16),
        pltpu.VMEM(held + (hidden,), BF16),
        pltpu.VMEM(square, BF16),
        *[pltpu.VMEM(w.shape, F32) for w in (wq, wk, wv, wo.T, w1, w2.T)],
        pltpu.VMEM(square, BF16),
        pltpu.VMEM(square, BF16),
        pltpu.VMEM(square, BF16),
        pltpu.VMEM((rows, 1), F32),
        pltpu.VMEM((rows, rows), BF16),
        pltpu.VMEM(square, BF16),
        pltpu.VMEM((width, rows), BF16),
        pltpu.VMEM(group, BF16),
        pltpu.VMEM(group, BF16),
        pltpu.VMEM(group, BF16),
        pltpu.VMEM(group, F32),
        pltpu.VMEM(group, F32),
        pltpu.VMEM(square, F32),
        pltpu.VMEM(square, F32),
        pltpu.VMEM((rows, 1), F32),
        pltpu.VMEM(square, BF16),
        pltpu.VMEM((width, rows), BF16),
        pltpu.VMEM((width, rows), BF16),
        pltpu.VMEM(square, F32),
        pltpu.VMEM((rows, hidden), BF16),
        pltpu.VMEM((rows, hidden), BF16),
        pltpu.VMEM((width, rows), BF16),
        pltpu.VMEM(group, F32),
        pltpu.VMEM(square, F32),
        pltpu.VMEM(group, BF16),
        pltpu.VMEM(group, F32),
        pltpu.VMEM(group, F32),
        pltpu.VMEM(group, F32),
        pltpu.VMEM(group, BF16),
        pltpu.VMEM((nt_, rows, 2 * LANES), BF16),
        pltpu.VMEM(square, F32),
        pltpu.VMEM((total_rows, width), F32),
        pltpu.VMEM((16, width), F32),
    ]
    for _ in range(2):
        scratch += Exchange.scratch(nd, nt_)
    scratch += Scatter.scratch(nd, nt_, *WIDE_WAYS, part_rows, 2 * hidden)
    scratch += Scatter.scratch(nd, nt_, *EVEN_WAYS, part_rows, 2 * LANES)
    scratch += Scatter.scratch(nd, nt_, *EVEN_WAYS, part_rows, 2 * LANES)
    scratch += Total.scratch(nd, nt_, total_rows, width)
    scratch += Total.scratch(nd, nt_, 16, width)
    for _ in range(4):
        scratch += Gather.semaphores(nd, nt_)
    for _ in range(2):
        scratch += Exchange.semaphores(nd, nt_)
    for ways in (WIDE_WAYS, EVEN_WAYS, EVEN_WAYS):
        scratch += Scatter.semaphores(nd, nt_, *ways)
    for _ in range(2):
        scratch += Total.semaphores(nd, nt_)
    scratch += [pltpu.SemaphoreType.DMA((8,)), pltpu.SemaphoreType.DMA((2,))]
    operands = (
        tokens, segments[None], wq, wk, wv, wo.T, w1, w2.T, inner_bias[None],
        *[v[None] for v in vectors], cotangent,
    )
    results = pl.pallas_call(
        functools.partial(kernel_whole, nd, nt_),
        out_shape=outs,
        in_specs=[hbm, vm] + [hbm] * 6 + [vm] * 7 + [hbm],
        out_specs=[hbm, hbm] + [vm] * (len(outs) - 2),
        scratch_shapes=scratch,
        compiler_params=pltpu.CompilerParams(
            collective_id=0, has_side_effects=True, vmem_limit_bytes=VMEM_LIMIT
        ),
        name="whole_layer",
    )(*operands)
    final = pl.pallas_call(
        functools.partial(kernel_outputs, len(outs)),
        out_shape=outs,
        in_specs=[hbm] * len(outs),
        out_specs=[hbm] * len(outs),
        scratch_shapes=[pltpu.VMEM(o.shape, o.dtype) for o in outs]
        + [pltpu.SemaphoreType.DMA((len(outs),))] * 2,
        name="outputs",
    )(*results)
    return (
        *final[:5], final[5].T, final[6], final[7].T, *[v.reshape(-1) for v in final[8:]],
    )


def solution(mesh):
    rows = P(("dp", "tensor"), None)
    one, two, all_of = P("dp", "tensor"), P("tensor", "dp"), P()
    weights = (one, one, one, two, one, two)
    return jax.shard_map(
        functools.partial(local, mesh.shape["dp"], mesh.shape["tensor"]),
        mesh=mesh,
        in_specs=(rows, P("dp")) + weights + (all_of,) * 7 + (rows,),
        out_specs=(rows, rows) + weights + (all_of,) * 7,
        check_vma=False,
    )
```

time: 125 us -> 102 us (0.82)
  local copies, waits for them, and re-layouts: 15.7 us -> 0 us
  Pallas kernels: 108 us -> 101 us
    unnamed x43 -> x0, local copies, waits for them, and re-layouts: 15.7 us -> none
    pallas_call x1, Pallas kernels: 108 us -> 98.2 us  [local(): pl.pallas_call(functools.partial(kernel_whole, nd, nt_), out_shape=outs,...]
    pallas_call x0 -> x1, Pallas kernels: none -> 2.43 us  [local(): pl.pallas_call(functools.partial(kernel_outputs, len(outs)), out_shape=ou...]
where the time goes in v3:
time: 102 us; the launch traced here: 101 us
  Pallas kernels  101 us (99%)
    pallas_call x1, Pallas kernels, local(): pl.pallas_call(functools.partial(kernel_whole, nd, nt_), out_shape=outs,...  98.2 us
    pallas_call x1, Pallas kernels, local(): pl.pallas_call(functools.partial(kernel_outputs, len(outs)), out_shape=ou...  2.43 us

profile of v3, /device:TPU:0, one launch (start us, length us, event | category | flops | bytes accessed | tf_op | source)
XLA Modules:
  0.0 101.5 jit_solution(9859242629734752786)
XLA Ops:
  0.7 98.2 %whole_layer.1 = (bf16[512,512]{1,0:T(8,128)(2,1)}, bf16[512,512]{1,0:T(8,128)(2,1)}, f32[64,128]{1,0:T(8,128)}, f32[64,128]{1,0:T(8,128)}, f32[64,128]{1,0:T(8,...) custom-call(bf16[512,512]{1,0:T(8,128)(2,1)} %tokens_in.1, ...), custom_call_target="tpu_custom_call" | custom-call | tf_op jit(solution)/shard_map/whole_layer/pallas_call | solution.py:1109
  98.9 2.4 %outputs.1 = (bf16[512,512]{1,0:T(8,128)(2,1)}, bf16[512,512]{1,0:T(8,128)(2,1)}, f32[64,128]{1,0:T(8,128)}, f32[64,128]{1,0:T(8,128)}, f32[64,128]{1,0:T(8,128)...) custom-call(bf16[512,512]{1,0:T(8,128)(2,1)} %get-tuple-element.45.r, ...), custom_call_target="tpu_custom_call" | custom-call | tf_op jit(solution)/shard_map/outputs/pallas_call | solution.py:1120

commit v4 on v3

--- a/solution.py
+++ b/solution.py
@@ -14,8 +14,9 @@
 F32 = jnp.float32
 BF16 = jnp.bfloat16
 OUTER = 4
+KV_STRAIGHT = True
 EVEN_WAYS = ((0, 1), (2, 3))
-WIDE_WAYS = ((0, 1, 3), (2,))
+WIDE_WAYS = ((2, 0, 1), (3,))
 VMEM_LIMIT = 56 << 20
 
 
@@ -111,9 +112,9 @@
 
 
 class Gather(Sender):
-    def __init__(self, place, held, sems):
+    def __init__(self, place, held, sems, straight=False):
         super().__init__(place, sems[0])
-        self.held = held
+        self.held, self.straight = held, straight
         self.got_outer, self.got_i, self.got_y, self.got_d, self.got_core = sems[1:]
 
     def _block(self, k, i, y):
@@ -136,6 +137,8 @@
             self.go(block, block, self.got_i.at[di - 1, k], p.at(di=di))
         for dy in range(1, p.ny):
             self.go(block, block, self.got_y.at[dy - 1, k], p.at(dy=dy))
+            for di in range(1, p.inner) if self.straight else ():
+                self.go(block, block, self.got_d.at[di - 1, dy - 1, k], p.at(di=di, dy=dy))
         self.go(block, block, self.got_core.at[p.y], p.at(dc=1))
 
     def turn(self, k):
@@ -143,7 +146,7 @@
         for di in range(1, p.inner):
             block = self._block(k, (p.i + p.inner - di) % p.inner, p.y)
             self.got(block, self.got_i.at[di - 1, k])
-            if k < 2:
+            if k < 2 and not self.straight:
                 for dy in range(1, p.ny):
                     self.go(block, block, self.got_d.at[di - 1, dy - 1, k], p.at(dy=dy))
             self.go(block, block, self.got_core.at[p.y], p.at(dc=1))
@@ -151,7 +154,7 @@
             y = (p.y + p.ny - dy) % p.ny
             block = self._block(k, p.i, y)
             self.got(block, self.got_y.at[dy - 1, k])
-            if k >= 2:
+            if k >= 2 and not self.straight:
                 for di in range(1, p.inner):
                     self.go(block, block, self.got_d.at[di - 1, dy - 1, k], p.at(di=di))
             self.go(block, block, self.got_core.at[y], p.at(dc=1))
@@ -515,19 +518,20 @@
 
 def kernel_whole(
     nd, nt_,
-    tokens_in, segments, wq_in, wk_in, wv_in, wo_in, w1_in, w2_in,
-    inner_bias, gain1, shift1, gain2, shift2, mixer_bias, outer_bias, cotangent_in,
-    out_to, tokens_to, grad_q, grad_k, grad_v, grad_o, grad_1, grad_2,
-    grad_ib, grad_g1, grad_s1, grad_g2, grad_s2, grad_mb, grad_ob,
-    *scratch,
+    *refs,
 ):
+    given, results, scratch = refs[:16], refs[16:31], refs[31:]
     it = iter(scratch)
 
     def take(count):
         return [next(it) for _ in range(count)]
 
     (held_kv, held_qo, held_2, held_1) = take(4)
-    (tokens, wq, wk, wv, wo, w1, w2, cotangent, out, grad_tokens) = take(10)
+    operands, made = take(16), take(15)
+    (tokens, segments, wq, wk, wv, wo, w1, w2, inner_bias,
+     gain1, shift1, gain2, shift2, mixer_bias, outer_bias, cotangent) = operands
+    (out, grad_tokens, grad_q, grad_k, grad_v, grad_o, grad_1, grad_2,
+     grad_ib, grad_g1, grad_s1, grad_g2, grad_s2, grad_mb, grad_ob) = made
     (segc, mask, normed, normed_t, fq, fk, vb, num_s, den_s) = take(9)
     (res, unit, inv, h2, h2t, cot, dh2, act, dhid, dbt) = take(10)
     (do, dr, gn, gd, dk_s, dv_s, dq_s, dkv_s, dh1, sums, first_sums) = take(11)
@@ -535,7 +539,7 @@
     bufs_f, bufs_qo, bufs_kv = take(10), take(10), take(10)
     bufs_t1, bufs_t2 = take(5), take(5)
     p = Place(nd, nt_)
-    kv, qo = Gather(p, held_kv, take(6)), Gather(p, held_qo, take(6))
+    kv, qo = Gather(p, held_kv, take(6), KV_STRAIGHT), Gather(p, held_qo, take(6))
     g2, g1 = Gather(p, held_2, take(6)), Gather(p, held_1, take(6))
     ex = Exchange(p, False, bufs_x, take(4))
     xb = Exchange(p, True, bufs_xb, take(4))
@@ -553,30 +557,33 @@
     (in_sems, out_sems) = take(2)
     p.greet()
     loads = [
-        pltpu.make_async_copy(src, dst, in_sems.at[n])
-        for n, (src, dst) in enumerate((
-            (wk_in, wk), (wv_in, wv), (tokens_in, tokens), (wq_in, wq), (wo_in, wo),
-            (w2_in, w2), (w1_in, w1), (cotangent_in, cotangent),
-        ))
+        pltpu.make_async_copy(given[n], operands[n], in_sems.at[n]) for n in range(len(given))
     ]
-    for load in loads:
-        load.start()
+    stores = [
+        pltpu.make_async_copy(made[n], results[n], out_sems.at[n]) for n in range(len(made))
+    ]
+    early = (3, 4)
+    for n in early + tuple(n for n in range(len(given)) if n not in early):
+        loads[n].start()
     here = (p.t, p.o, p.i)
     if head < LANES:
         blank = jnp.zeros((part_rows, 2 * LANES), BF16)
         held_kv[here] = blank
         held_qo[here] = blank
-    loads[0].wait()
-    loads[1].wait()
+    for n in early:
+        loads[n].wait()
     held_kv[here + (slice(None), slice(0, head))] = wk[...].astype(BF16)
     held_kv[here + (slice(None), slice(LANES, LANES + head))] = wv[...].astype(BF16)
-    for load in loads[3:7]:
-        load.wait()
+    p.meet()
+    kv.outer_start()
+    kv.spread(0)
+    for n in range(len(loads) - 1):
+        if n not in early:
+            loads[n].wait()
     held_qo[here + (slice(None), slice(0, head))] = wq[...].astype(BF16)
     held_qo[here + (slice(None), slice(LANES, LANES + head))] = wo[...].astype(BF16)
     held_2[here] = w2[...].astype(BF16)
     held_1[here] = w1[...].astype(BF16)
-    loads[2].wait()
     segr = segments[:, pl.ds(pl.multiple_of(p.t * rows_all, LANES), rows_all)].astype(F32)
     for start in range(0, rows_all, LANES):
         wide = jnp.broadcast_to(segr[:, start : start + LANES], (8, LANES))
@@ -599,23 +606,20 @@
         earlier = lax.broadcasted_iota(jnp.int32, (128, rows_all), 1)
         same = segc[start : start + 128, :] == segr
         mask[start : start + 128, :] = jnp.where((later >= earlier) & same, 1.0, 0.0).astype(BF16)
-    p.meet()
-    kv.outer_start()
-    kv.spread(0)
+    for k in range(1, OUTER):
+        kv.spread(k)
     qo.outer_start()
     qo.spread(0)
     g2.outer_start()
-    g2.spread(0)
-    g1.outer_start()
-    for k in range(1, OUTER):
-        kv.spread(k)
-    g1.spread(0)
     for k in range(OUTER):
         kv.turn(k)
     for k in range(1, OUTER):
         qo.spread(k)
+    g1.outer_start()
     for k in range(OUTER):
         kv.corner(k)
+    g2.spread(0)
+    g1.spread(0)
     for dy in range(p.ny):
         kv.core_done(dy)
 
@@ -637,7 +641,7 @@
         qo.turn(k)
     for k in range(1, OUTER):
         g2.spread(k)
-    loads[7].wait()
+    loads[-1].wait()
     for start in range(0, rows_all, step):
         turned = jnp.transpose(cotangent[start : start + step, :].astype(F32))
         cot[:, start : start + step] = turned.astype(BF16)
@@ -777,11 +781,11 @@
         feed(y * 2 + p.c)
         sf.core_wait(y)
         feed_grads(y, True)
+        sf.first_i(dy, 2)
         if dy:
-            sf.first_y(dy, 2, 0)
+            sf.first_y(dy, 3, 0)
         else:
-            for k in sf.by_i:
-                sf.first_i(0, k)
+            sf.first_i(0, 0)
 
     def leave(k, _):
         at = pl.ds(pl.multiple_of(k * step, step), step)
@@ -806,8 +810,7 @@
         return 0
 
     lax.fori_loop(0, rows_all // step, leave, 0)
-    store_out = pltpu.make_async_copy(out, out_to, out_sems.at[0])
-    store_out.start()
+    stores[0].start()
 
     def first(g, _):
         low = (do[g] * rden[g]).astype(BF16)
@@ -827,9 +830,7 @@
     lax.fori_loop(0, nt_, first, 0)
     xb.step_near()
     for dy in range(1, p.ny):
-        for di in range(1, p.inner):
-            sf.first_y(dy, 2, di)
-        for k in sf.by_i:
+        for k in range(2):
             sf.first_i(dy, k)
     all_sum.start(sums[...])
 
@@ -874,18 +875,22 @@
         dv_s[g] = jnp.transpose(dv_t)
         return 0
 
-    lax.fori_loop(0, nt_ // 2, inside_back, 0)
+    quarter = nt_ // 4
+    lax.fori_loop(0, quarter, inside_back, 0)
+    for dy in range(1, p.ny):
+        sf.second_i(2, dy)
+        for di in range(1, p.inner):
+            sf.first_y(dy, 3, di)
+    lax.fori_loop(quarter, 2 * quarter, inside_back, 0)
     xb.step_far()
     all_sum.plane_step()
-    for k in sf.by_i:
-        sf.second_i(k, 0)
-    lax.fori_loop(nt_ // 2, nt_, inside_back, 0)
+    sf.second_i(2, 0)
+    lax.fori_loop(2 * quarter, nt_, inside_back, 0)
+    xb.step_enter()
+    sf.third(2)
     for dy in range(1, p.ny):
         sf.second_i(0, dy)
-    xb.step_enter()
-    sf.second_y(2)
-    for dy in range(1, p.ny):
-        sf.second_i(1, dy)
+    sf.first_i(0, 1)
 
     def attention_grads(scatter, dc, joint):
         for dy in list(range(1, p.ny)) + [0]:
@@ -911,7 +916,11 @@
         return ((normed_t[...], dq_s[g]), (dbt[...], mixed[g].astype(BF16)))
 
     attention_grads(sqo, 1, query_output)
+    for dy in range(1, p.ny):
+        sf.second_i(1, dy)
+    sf.second_y(3)
     attention_grads(sqo, 0, query_output)
+    sf.second_i(0, 0)
     all_sum.outer_step()
 
     def query_back(g, _):
@@ -920,8 +929,7 @@
 
     dh1[...] = jnp.zeros_like(dh1)
     lax.fori_loop(0, nt_, query_back, 0)
-    for dy in range(1, p.ny):
-        sf.second_i(3, dy)
+    sf.second_i(1, 0)
     xb.arrive()
 
     def key_value(g):
@@ -940,7 +948,6 @@
         return ((normed_t[...], dk), (normed_t[...], dv))
 
     attention_grads(skv, 1, key_value)
-    sf.third(2)
     sf.third(1)
     attention_grads(skv, 0, key_value)
     sf.third(3)
@@ -970,17 +977,16 @@
         return 0
 
     lax.fori_loop(0, rows_all // step, finish, 0)
-    store_tokens = pltpu.make_async_copy(grad_tokens, tokens_to, out_sems.at[1])
-    store_tokens.start()
+    stores[1].start()
     first_sum.start(first_sums[...])
     sqo.second()
     first_sum.plane_step()
     skv.second()
     for k in (2, 3, 1):
         sqo.third(k)
+    first_sum.outer_step()
     for k in (2, 3, 1):
         skv.third(k)
-    first_sum.outer_step()
     for scatter in (sf, sqo, skv):
         scatter.third(0)
     all_sum.core_step()
@@ -1004,8 +1010,10 @@
     total = first_sum.result()
     grad_g1[...] = total[0:1, :]
     grad_s1[...] = total[8:9, :]
-    store_out.wait()
-    store_tokens.wait()
+    for store in stores[2:]:
+        store.start()
+    for store in stores:
+        store.wait()
     for each in (kv, qo, g2, g1, ex, xb, sf, sqo, skv, all_sum, first_sum):
         each.finish()
 
@@ -1029,7 +1037,7 @@
     rows, width = tokens.shape
     inner = nd // OUTER
     part_rows, hidden = w1.shape
-    vm, hbm = (pl.BlockSpec(memory_space=space) for space in (pltpu.VMEM, pl.ANY))
+    hbm = pl.BlockSpec(memory_space=pl.ANY)
     group = (nt_, rows, LANES)
     total_rows = 8 + max(8, nt_)
     head = wq.shape[1]
@@ -1043,6 +1051,10 @@
         jax.ShapeDtypeStruct((1, nt_ * hidden), F32),
         *[row] * 6,
     ]
+    operands = (
+        tokens, segments[None], wq, wk, wv, wo.T, w1, w2.T, inner_bias[None],
+        *[v[None] for v in vectors], cotangent,
+    )
     held = (nt_, OUTER, inner, part_rows)
     square = (rows, width)
     scratch = [
@@ -1050,11 +1062,8 @@
         pltpu.VMEM(held + (2 * LANES,), BF16),
         pltpu.VMEM(held + (hidden,), BF16),
         pltpu.VMEM(held + (hidden,), BF16),
-        pltpu.VMEM(square, BF16),
-        *[pltpu.VMEM(w.shape, F32) for w in (wq, wk, wv, wo.T, w1, w2.T)],
-        pltpu.VMEM(square, BF16),
-        pltpu.VMEM(square, BF16),
-        pltpu.VMEM(square, BF16),
+        *[pltpu.VMEM(v.shape, v.dtype) for v in operands],
+        *[pltpu.VMEM(v.shape, v.dtype) for v in outs],
         pltpu.VMEM((rows, 1), F32),
         pltpu.VMEM((rows, rows), BF16),
         pltpu.VMEM(square, BF16),
@@ -1101,16 +1110,12 @@
         scratch += Scatter.semaphores(nd, nt_, *ways)
     for _ in range(2):
         scratch += Total.semaphores(nd, nt_)
-    scratch += [pltpu.SemaphoreType.DMA((8,)), pltpu.SemaphoreType.DMA((2,))]
-    operands = (
-        tokens, segments[None], wq, wk, wv, wo.T, w1, w2.T, inner_bias[None],
-        *[v[None] for v in vectors], cotangent,
-    )
+    scratch += [pltpu.SemaphoreType.DMA((len(v),)) for v in (operands, outs)]
     results = pl.pallas_call(
         functools.partial(kernel_whole, nd, nt_),
         out_shape=outs,
-        in_specs=[hbm, vm] + [hbm] * 6 + [vm] * 7 + [hbm],
-        out_specs=[hbm, hbm] + [vm] * (len(outs) - 2),
+        in_specs=[hbm] * len(operands),
+        out_specs=[hbm] * len(outs),
         scratch_shapes=scratch,
         compiler_params=pltpu.CompilerParams(
             collective_id=0, has_side_effects=True, vmem_limit_bytes=VMEM_LIMIT

time: 102 us -> 95 us (0.931)
  Pallas kernels: 101 us -> 94 us
    pallas_call x1, Pallas kernels: 98.2 us -> 91.6 us  [local(): pl.pallas_call(functools.partial(kernel_whole, nd, nt_), out_shape=outs,...]
where the time goes in v4:
time: 95 us; the launch traced here: 94.8 us
  Pallas kernels  94 us (99%)
    pallas_call x1, Pallas kernels, local(): pl.pallas_call(functools.partial(kernel_whole, nd, nt_), out_shape=outs,...  91.6 us
    pallas_call x1, Pallas kernels, local(): pl.pallas_call(functools.partial(kernel_outputs, len(outs)), out_shape=ou...  2.43 us

profile of v4, /device:TPU:0, one launch (start us, length us, event | category | flops | bytes accessed | tf_op | source)
XLA Modules:
  0.0 94.8 jit_solution(18257817546254524518)
XLA Ops:
  0.7 91.6 %whole_layer.1 = (bf16[512,512]{1,0:T(8,128)(2,1)}, bf16[512,512]{1,0:T(8,128)(2,1)}, f32[64,128]{1,0:T(8,128)}, f32[64,128]{1,0:T(8,128)}, f32[64,128]{1,0:T(8,...) custom-call(bf16[512,512]{1,0:T(8,128)(2,1)} %refs_0_.1, ...), custom_call_target="tpu_custom_call" | custom-call | tf_op jit(solution)/shard_map/whole_layer/pallas_call | solution.py:1114
  92.3 2.4 %outputs.1 = (bf16[512,512]{1,0:T(8,128)(2,1)}, bf16[512,512]{1,0:T(8,128)(2,1)}, f32[64,128]{1,0:T(8,128)}, f32[64,128]{1,0:T(8,128)}, f32[64,128]{1,0:T(8,128)...) custom-call(bf16[512,512]{1,0:T(8,128)(2,1)} %get-tuple-element.45.r, ...), custom_call_target="tpu_custom_call" | custom-call | tf_op jit(solution)/shard_map/outputs/pallas_call | solution.py:1125

commit v5 on v4

--- a/solution.py
+++ b/solution.py
@@ -447,6 +447,10 @@
 def two_parts(values):
     high = values.astype(BF16)
     return high, (values - high.astype(F32)).astype(BF16)
+
+
+def twice(values):
+    return jnp.concatenate([values, values], axis=1)
 
 
 def same_head():
@@ -611,19 +615,7 @@
     qo.outer_start()
     qo.spread(0)
     g2.outer_start()
-    for k in range(OUTER):
-        kv.turn(k)
-    for k in range(1, OUTER):
-        qo.spread(k)
-    g1.outer_start()
-    for k in range(OUTER):
-        kv.corner(k)
-    g2.spread(0)
-    g1.spread(0)
-    for dy in range(p.ny):
-        kv.core_done(dy)
-
-    def keys_values(g, _):
+    def keys_values(g):
         w = held_kv[g].reshape(width, 2 * LANES)
         both = nn(normed[...], w)
         keys = feature(both[:, :LANES]).astype(BF16)
@@ -633,12 +625,34 @@
         kept = jnp.where(segc[...] == last_id, keys, jnp.zeros_like(keys))
         total = jnp.sum(kept.astype(F32), axis=0, keepdims=True)
         ex.put(g, pack_state(tn(kept, values)), total, last_id, first_id)
-        return 0
-
-    lax.fori_loop(0, nt_, keys_values, 0)
+
+    def columns(dy, dc):
+        return (p.y + dy) % p.ny * 2 + (p.c + dc) % 2
+
+    for k in range(OUTER):
+        kv.turn(k)
+    for k in range(1, OUTER):
+        qo.spread(k)
+    g1.outer_start()
+    keys_values(columns(0, 0))
+    for k in range(OUTER):
+        kv.corner(k)
+    g2.spread(0)
+    g1.spread(0)
+    for dy in range(1, p.ny):
+        keys_values(columns(dy, 0))
+    for dy in range(p.ny):
+        kv.core_done(dy)
+        keys_values(columns(dy, 1))
+
+    def queries(g):
+        w = held_qo[g].reshape(width, 2 * LANES)
+        fq[g] = feature(nn(normed[...], w[:, :LANES])).astype(BF16)
+
     ex.step_near()
     for k in range(OUTER):
         qo.turn(k)
+    queries(columns(0, 0))
     for k in range(1, OUTER):
         g2.spread(k)
     loads[-1].wait()
@@ -649,15 +663,12 @@
     g1.spread(1)
     for k in range(OUTER):
         qo.corner(k)
+    for dy in range(1, p.ny):
+        queries(columns(dy, 0))
     for dy in range(p.ny):
         qo.core_done(dy)
-
-    def queries(g, _):
-        w = held_qo[g].reshape(width, 2 * LANES)
-        fq[g] = feature(nn(normed[...], w[:, :LANES])).astype(BF16)
-        return 0
-
-    lax.fori_loop(0, nt_, queries, 0)
+        queries(columns(dy, 1))
+
 
     def inside(g, _):
         values = split_heads(vb[g], 1.0)
@@ -690,13 +701,14 @@
 
     def outside(g, _):
         packed, foot = ex.state(g)
-        high, low = two_parts(wide_state(packed))
         total = jnp.broadcast_to(jnp.transpose(foot)[:, 0:1], (LANES, LANES))
-        sum_high, sum_low = two_parts(jnp.where(same_head(), total, 0.0))
+        total = jnp.where(same_head(), total, 0.0)
+        parts = two_parts(jnp.concatenate([wide_state(packed), total], axis=1))
         query = fq[g]
         query = jnp.where(segc[...] == first_id, query, jnp.zeros_like(query))
-        num = num_s[g] + (nn(query, high) + nn(query, low))
-        den = den_s[g] + (nn(query, sum_high) + nn(query, sum_low))
+        carried = nn(twice(query), jnp.concatenate(parts, axis=0))
+        num = num_s[g] + carried[:, :LANES]
+        den = den_s[g] + carried[:, LANES:]
         inverse = 1.0 / den
         den_s[g] = inverse
         num_s[g] = num * inverse
@@ -707,14 +719,14 @@
     for k in range(2, OUTER):
         g1.turn(k)
 
-    def output_weight(g):
-        return held_qo[g, :, :, :, LANES:].reshape(width, LANES)
+    def output_weight():
+        parts = [held_qo[g, :, :, :, LANES:].reshape(width, LANES) for g in range(nt_)]
+        return jnp.concatenate(parts, axis=1)
 
     def enter(k, _):
         at = pl.ds(pl.multiple_of(k * step, step), step)
-        r = tokens[at, :].astype(F32) + mixer_bias[...]
-        for g in range(nt_):
-            r = r + nt(mixed[g, at, :].astype(BF16), output_weight(g))
+        low = jnp.concatenate([mixed[g, at, :].astype(BF16) for g in range(nt_)], axis=1)
+        r = tokens[at, :].astype(F32) + mixer_bias[...] + nt(low, output_weight())
         center = r - jnp.mean(r, axis=-1, keepdims=True)
         spread = jnp.mean(center * center, axis=-1, keepdims=True)
         scale = lax.rsqrt(spread + EPSILON)
@@ -801,8 +813,9 @@
         low = back.astype(BF16)
         wide = low.astype(F32)
         dbt[:, at] = jnp.transpose(wide).astype(BF16)
+        pulled = nn(low, output_weight())
         for g in range(nt_):
-            do[g, at, :] = nn(low, output_weight(g))
+            do[g, at, :] = pulled[:, g * LANES : (g + 1) * LANES]
         sums[2:3, :] += jnp.sum(grad * n, axis=0, keepdims=True)
         sums[3:4, :] += jnp.sum(grad, axis=0, keepdims=True)
         sums[4:5, :] += jnp.sum(wide, axis=0, keepdims=True)
@@ -815,12 +828,9 @@
     def first(g, _):
         low = (do[g] * rden[g]).astype(BF16)
         gn[g] = low
-        product = low.astype(F32) * mixed[g]
-        left = left_lanes(product.shape)
-        zero = jnp.zeros_like(product)
-        one = jnp.sum(jnp.where(left, product, zero), axis=-1, keepdims=True)
-        two = jnp.sum(jnp.where(left, zero, product), axis=-1, keepdims=True)
-        slope = -jnp.where(left, one, two)
+        product = jnp.concatenate(two_parts(low.astype(F32) * mixed[g]), axis=1)
+        minus = jnp.where(same_head(), -1.0, 0.0).astype(BF16)
+        slope = nn(product, jnp.concatenate([minus, minus], axis=0))
         gd[g] = slope
         kept = jnp.where(segc[...] == first_id, fq[g], jnp.zeros_like(low))
         total = jnp.sum(kept.astype(F32) * slope, axis=0, keepdims=True)
@@ -838,7 +848,7 @@
         values, keys = vb[g], fk[g]
         key_heads = split_heads(keys, 0.0)
         packed, foot = ex.state(g)
-        high, low = two_parts(wide_state(packed))
+        state = jnp.concatenate(two_parts(wide_state(packed)), axis=1)
         query_t = jnp.transpose(fq[g].astype(F32)).astype(BF16)
         grad_t = jnp.transpose(gn[g].astype(F32)).astype(BF16)
         dk_t = jnp.zeros((LANES, rows_all), F32)
@@ -851,7 +861,7 @@
             query_heads, grad_heads = split_heads(query, 0.0), split_heads(grad, 0.0)
             dq = jnp.where(
                 segc[start:end, :] == first_id,
-                nt(grad, high) + nt(grad, low) + slope * foot[0:1, :],
+                nt(twice(grad), state) + slope * foot[0:1, :],
                 0.0,
             )
             dk_parts, dv_parts = [], []
@@ -934,10 +944,10 @@
 
     def key_value(g):
         packed, foot = xb.state(g)
-        high, low = two_parts(wide_state(packed))
+        parts = two_parts(wide_state(packed))
         keys, values = fk[g], vb[g]
-        dk = nt(values, high) + nt(values, low) + foot[0:1, :]
-        dv = nn(keys, high) + nn(keys, low)
+        dk = nt(twice(values), jnp.concatenate(parts, axis=1)) + foot[0:1, :]
+        dv = nn(twice(keys), jnp.concatenate(parts, axis=0))
         closing = segc[...] == last_id
         dk = dk_s[g] + jnp.where(closing, dk, 0.0)
         dv = dv_s[g] + jnp.where(closing, dv, 0.0)

time: 95 us -> 93.4 us (0.983)
  Pallas kernels: 94 us -> 92.4 us
    pallas_call x1, Pallas kernels: 91.6 us -> 89.9 us  [local(): pl.pallas_call(functools.partial(kernel_whole, nd, nt_), out_shape=outs,...]
where the time goes in v5:
time: 93.4 us; the launch traced here: 93.2 us
  Pallas kernels  92.4 us (99%)
    pallas_call x1, Pallas kernels, local(): pl.pallas_call(functools.partial(kernel_whole, nd, nt_), out_shape=outs,...  89.9 us
    pallas_call x1, Pallas kernels, local(): pl.pallas_call(functools.partial(kernel_outputs, len(outs)), out_shape=ou...  2.43 us

profile of v5, /device:TPU:0, one launch (start us, length us, event | category | flops | bytes accessed | tf_op | source)
XLA Modules:
  0.0 93.2 jit_solution(2799943833705608089)
XLA Ops:
  0.7 89.9 %whole_layer.1 = (bf16[512,512]{1,0:T(8,128)(2,1)}, bf16[512,512]{1,0:T(8,128)(2,1)}, f32[64,128]{1,0:T(8,128)}, f32[64,128]{1,0:T(8,128)}, f32[64,128]{1,0:T(8,...) custom-call(bf16[512,512]{1,0:T(8,128)(2,1)} %refs_0_.1, ...), custom_call_target="tpu_custom_call" | custom-call | tf_op jit(solution)/shard_map/whole_layer/pallas_call | solution.py:1124
  90.6 2.4 %outputs.1 = (bf16[512,512]{1,0:T(8,128)(2,1)}, bf16[512,512]{1,0:T(8,128)(2,1)}, f32[64,128]{1,0:T(8,128)}, f32[64,128]{1,0:T(8,128)}, f32[64,128]{1,0:T(8,128)...) custom-call(bf16[512,512]{1,0:T(8,128)(2,1)} %get-tuple-element.45.r, ...), custom_call_target="tpu_custom_call" | custom-call | tf_op jit(solution)/shard_map/outputs/pallas_call | solution.py:1135

commit v6 on v5

--- a/solution.py
+++ b/solution.py
@@ -372,7 +372,7 @@
             total = total + jnp.where(self._edge(block) == self._edge(border), block, 0.0)
         row = lax.broadcasted_iota(jnp.int32, total.shape, 0)
         self.far[p.o] = jnp.where(row > self.rows, border, total)
-        for k in range(1, OUTER):
+        for k in range(OUTER - 1, 0, -1):
             o = p.nearest(k)
             self.go(self.far.at[p.o], self.far.at[p.o], self.s_far.at[p.o], p.to(o, p.i, p.y, p.c))
 
@@ -556,7 +556,7 @@
     head, hidden = wq.shape[1], w1.shape[1]
     part_rows = wq.shape[0]
     block_shape = (OUTER, p.inner, part_rows)
-    step, block = 128, min(256, rows_all)
+    step, block, tile = 128, min(512, rows_all), min(256, rows_all)
 
     (in_sems, out_sems) = take(2)
     p.greet()
@@ -672,8 +672,8 @@
 
     def inside(g, _):
         values = split_heads(vb[g], 1.0)
-        for start in range(0, rows_all, block):
-            end = start + block
+        for start in range(0, rows_all, tile):
+            end = start + tile
             now = mask[start:end, :end]
             query = split_heads(fq[g, start:end, :], 0.0)
             keys = fk[g, :end, :]
@@ -853,8 +853,8 @@
         grad_t = jnp.transpose(gn[g].astype(F32)).astype(BF16)
         dk_t = jnp.zeros((LANES, rows_all), F32)
         dv_t = jnp.zeros((LANES, rows_all), F32)
-        for start in range(0, rows_all, block):
-            end = start + block
+        for start in range(0, rows_all, tile):
+            end = start + tile
             now = mask[start:end, :end]
             query, grad = fq[g, start:end, :], gn[g, start:end, :]
             slope = gd[g, start:end, :]

time: 93.4 us -> 93.2 us (level)
  no operation moved by 1% of the time
where the time goes in v6:
time: 93.2 us; the launch traced here: 93 us
  Pallas kernels  92.2 us (99%)
    pallas_call x1, Pallas kernels, local(): pl.pallas_call(functools.partial(kernel_whole, nd, nt_), out_shape=outs,...  89.8 us
    pallas_call x1, Pallas kernels, local(): pl.pallas_call(functools.partial(kernel_outputs, len(outs)), out_shape=ou...  2.43 us

profile of v6, /device:TPU:0, one launch (start us, length us, event | category | flops | bytes accessed | tf_op | source)
XLA Modules:
  0.0 93.0 jit_solution(5022827099942534653)
XLA Ops:
  0.7 89.8 %whole_layer.1 = (bf16[512,512]{1,0:T(8,128)(2,1)}, bf16[512,512]{1,0:T(8,128)(2,1)}, f32[64,128]{1,0:T(8,128)}, f32[64,128]{1,0:T(8,128)}, f32[64,128]{1,0:T(8,...) custom-call(bf16[512,512]{1,0:T(8,128)(2,1)} %refs_0_.1, ...), custom_call_target="tpu_custom_call" | custom-call | tf_op jit(solution)/shard_map/whole_layer/pallas_call | solution.py:1124
  90.4 2.4 %outputs.1 = (bf16[512,512]{1,0:T(8,128)(2,1)}, bf16[512,512]{1,0:T(8,128)(2,1)}, f32[64,128]{1,0:T(8,128)}, f32[64,128]{1,0:T(8,128)}, f32[64,128]{1,0:T(8,128)...) custom-call(bf16[512,512]{1,0:T(8,128)(2,1)} %get-tuple-element.45.r, ...), custom_call_target="tpu_custom_call" | custom-call | tf_op jit(solution)/shard_map/outputs/pallas_call | solution.py:1135

commit v7 on v6

--- a/solution.py
+++ b/solution.py
@@ -556,7 +556,7 @@
     head, hidden = wq.shape[1], w1.shape[1]
     part_rows = wq.shape[0]
     block_shape = (OUTER, p.inner, part_rows)
-    step, block, tile = 128, min(512, rows_all), min(256, rows_all)
+    step, block, tile = 128, min(512, rows_all), min(512, rows_all)
 
     (in_sems, out_sems) = take(2)
     p.greet()

time: 93.2 us -> 93 us (level)
  no operation moved by 1% of the time
where the time goes in v7:
time: 93 us; the launch traced here: 92.8 us
  Pallas kernels  92 us (99%)
    pallas_call x1, Pallas kernels, local(): pl.pallas_call(functools.partial(kernel_whole, nd, nt_), out_shape=outs,...  89.6 us
    pallas_call x1, Pallas kernels, local(): pl.pallas_call(functools.partial(kernel_outputs, len(outs)), out_shape=ou...  2.43 us

profile of v7, /device:TPU:0, one launch (start us, length us, event | category | flops | bytes accessed | tf_op | source)
XLA Modules:
  0.0 92.8 jit_solution(4268894812581095395)
XLA Ops:
  0.7 89.6 %whole_layer.1 = (bf16[512,512]{1,0:T(8,128)(2,1)}, bf16[512,512]{1,0:T(8,128)(2,1)}, f32[64,128]{1,0:T(8,128)}, f32[64,128]{1,0:T(8,128)}, f32[64,128]{1,0:T(8,...) custom-call(bf16[512,512]{1,0:T(8,128)(2,1)} %refs_0_.1, ...), custom_call_target="tpu_custom_call" | custom-call | tf_op jit(solution)/shard_map/whole_layer/pallas_call | solution.py:1124
  90.2 2.4 %outputs.1 = (bf16[512,512]{1,0:T(8,128)(2,1)}, bf16[512,512]{1,0:T(8,128)(2,1)}, f32[64,128]{1,0:T(8,128)}, f32[64,128]{1,0:T(8,128)}, f32[64,128]{1,0:T(8,128)...) custom-call(bf16[512,512]{1,0:T(8,128)(2,1)} %get-tuple-element.45.r, ...), custom_call_target="tpu_custom_call" | custom-call | tf_op jit(solution)/shard_map/outputs/pallas_call | solution.py:1135
